TPU v7x, 32 devices: a whole 2x2x4 slice. The times are simulated.
32 devices in a mesh: member: 4 (over y, x), domain: 8 (over z, core).
Axes of the slice: x: 2, y: 2, z: 4, core: 2. Of those that a mesh axis runs over, the one named last changes fastest.
Arguments:
- ensemble: float32 [80, 4, 3, 16, 2048], P('member', None, None, None, 'domain'), may hold values from -9 to 9
- velocity: float32 [2, 3, 16, 2048], P(None, None, None, 'domain'), may hold values from -0.5 to 0.5
- diffusivity: float32 [4], replicated, may hold values from 0.05 to 0.2
- land_mask: int32 [16, 2048], P(None, 'domain'), may hold values from 0 to 1
- obs_index: int32 [4, 8, 4], replicated, may hold values from 0 to 255, as said below
- obs_owner: int32 [4], replicated, may hold values from 0 to 31, as said below
- obs_value: float32 [4, 8], replicated, may hold values from -4 to 4
- obs_error: float32 [4, 8], replicated, may hold values from 0.2 to 1
Outputs:
- analysis: float32 [80, 4, 3, 16, 2048], P(None, None, None, 'member', 'domain')
Inputs may be any that keep to these rules, and one draw needn't show every extreme that they name: `obs_index`: each observed cell has land_mask 1. The first observation of batch 0 is field 0, level 0 at its block's first row and column; the last observation of batch 3 is field 3, level 2 at its block's last row and column. A device's number is its member index times the number of domain tiles plus its domain index. obs_owner[0] is the first device and obs_owner[3] the last.
All inputs are finite; a program needn't handle non-finite values.
Results may differ from a plain program's by a relative error of at most 0.0001.
Values sent between devices are 32-bit elements; how exact they have to be, the bound alone decides.
No kernel may reach another device: no remote copies, remote signals or barrier semaphores. Data moves between devices by JAX's collectives and lax.ppermute only.
A program may use at most 192 MiB of HBM per device.

v0:
```python
import jax
import jax.numpy as jnp
from jax import lax
from jax.sharding import PartitionSpec as P

LOC_RADIUS = 64


def padded_2(array, sides, width):
    for axis, dim in sides:
        size, length = (lax.axis_size(axis), array.shape[dim])
        up = [(i, (i + 1) % size) for i in range(size)]
        down = [(j, i) for i, j in up]
        last = lax.slice_in_dim(array, length - width, length, axis=dim)
        initial = lax.slice_in_dim(array, 0, width, axis=dim)
        before = lax.ppermute(last, axis, up)
        after = lax.ppermute(initial, axis, down)
        array = jnp.concatenate([before, array, after], axis=dim)
    return array


def broadcast(value, axis, source):
    kept = jnp.where(lax.axis_index(axis) == source, value, 0).astype(value.dtype)
    return lax.psum(kept, axis)


def gaspari(distance, loc_radius):
    scaled = distance / loc_radius
    scaled_safe = jnp.maximum(scaled, 1.0)
    near_part = (
        ((-0.25 * scaled + 0.5) * scaled + 0.625) * scaled - 5.0 / 3.0
    ) * scaled * scaled + 1.0
    far_part = (
        ((((scaled / 12.0 - 0.5) * scaled + 0.625) * scaled + 5.0 / 3.0) * scaled - 5.0) * scaled
        + 4.0
        - 2.0 / (3.0 * scaled_safe)
    )
    return jnp.where(scaled <= 1.0, near_part, jnp.where(scaled < 2.0, far_part, 0.0))


def separation(row_from, col_from, row_to, col_to, grid_width):
    col_gap = jnp.abs(col_from - col_to)
    col_gap = jnp.minimum(col_gap, grid_width - col_gap)
    row_gap = row_from - row_to
    return jnp.sqrt((col_gap * col_gap + row_gap * row_gap).astype(jnp.float32))


def advance(center, col_next, col_prev, row_next, row_prev, flow_u, flow_v, diffuse, wet_part):
    tendency = (
        -flow_u * (col_next - col_prev) * 0.5
        - flow_v * (row_next - row_prev) * 0.5
        + diffuse * (col_next + col_prev + row_next + row_prev - 4.0 * center)
    )
    return wet_part * (center + tendency)


def regroup(member_state):
    return lax.all_to_all(member_state, "member", split_axis=3, concat_axis=0, tiled=True)


def increment_sums(change_flat, wet_cells, levels_total, members):
    per_cell = jnp.sum(change_flat.reshape(members, levels_total, -1), axis=0)
    local_sum = jnp.sum(per_cell * wet_cells[None, :], axis=1)
    return lax.psum((local_sum, jnp.sum(wet_cells)), ("member", "domain"))


def local(ensemble, velocity, diffusivity, land_mask, obs_index, obs_owner, obs_value, obs_error):
    fields = diffusivity.shape[0]
    levels = velocity.shape[1]
    levels_total = fields * levels
    diffuse = diffusivity[None, :, None, None, None]
    domain_count = lax.axis_size("domain")
    wet_all = land_mask.astype(jnp.float32)
    padded = padded_2(ensemble, (("domain", 4),), 1)
    zero_row = jnp.zeros_like(ensemble[:, :, :, :1, :])
    row_next = jnp.concatenate([ensemble[:, :, :, 1:, :], zero_row], axis=3)
    row_prev = jnp.concatenate([zero_row, ensemble[:, :, :, :-1, :]], axis=3)
    stepped = advance(
        ensemble,
        padded[..., 2:],
        padded[..., :-2],
        row_next,
        row_prev,
        velocity[0][None, None],
        velocity[1][None, None],
        diffuse,
        wet_all,
    )
    current = regroup(stepped)
    row_count = current.shape[3]
    first_row = lax.axis_index("member") * row_count
    wet_rows = lax.dynamic_slice_in_dim(wet_all, first_row, row_count, 0)
    members = current.shape[0]
    col_count = current.shape[4]
    grid_width = col_count * domain_count
    loc_radius = float(LOC_RADIUS)
    first_col = lax.axis_index("domain") * col_count
    grid_rows = first_row + jnp.arange(row_count, dtype=jnp.int32)[:, None]
    grid_cols = first_col + jnp.arange(col_count, dtype=jnp.int32)[None, :]
    wet_cells = wet_rows.reshape(-1)
    wet_flat = jnp.broadcast_to(wet_rows[None], (levels_total, row_count, col_count)).reshape(-1)
    flat_state = current.reshape(members, -1)
    spread = jnp.float32(members - 1)
    level_ids = jnp.arange(levels_total, dtype=jnp.int32)
    pending = jnp.zeros((levels_total,), jnp.float32)
    deferred = None
    for batch_num in range(obs_owner.shape[0]):
        obs_slot = obs_index[batch_num]
        owner_dev = obs_owner[batch_num]
        level_of = obs_slot[:, 0] * levels + obs_slot[:, 1]
        position = (level_of * row_count + obs_slot[:, 2]) * col_count + obs_slot[:, 3]
        own_priors = jnp.take(flat_state, position, axis=1).T
        priors = broadcast(own_priors, ("member", "domain"), owner_dev)
        if deferred is not None:
            total_inc, wet_count = increment_sums(deferred, wet_cells, levels_total, members)
            pending = pending + total_inc / (members * wet_count)
        lowered = jnp.sum(
            jnp.where(level_of[:, None] == level_ids[None, :], pending[None, :], 0.0), axis=1
        )
        priors = priors - lowered[:, None]
        obs_rows = owner_dev // domain_count * row_count + obs_slot[:, 2]
        obs_cols = owner_dev % domain_count * col_count + obs_slot[:, 3]
        mutual = gaspari(
            separation(
                obs_rows[:, None],
                obs_cols[:, None],
                obs_rows[None, :],
                obs_cols[None, :],
                grid_width,
            ),
            loc_radius,
        )
        before = flat_state
        for obs_num in range(priors.shape[0]):
            prior_row = priors[obs_num]
            mean_prior = jnp.mean(prior_row)
            anomaly = prior_row - mean_prior
            obs_var = obs_error[batch_num, obs_num]
            denominator = jnp.sum(anomaly * anomaly) / spread + obs_var
            shrink = 1.0 / (1.0 + jnp.sqrt(obs_var / denominator))
            weight = obs_value[batch_num, obs_num] - mean_prior - shrink * anomaly
            taper = gaspari(
                separation(grid_rows, grid_cols, obs_rows[obs_num], obs_cols[obs_num], grid_width),
                loc_radius,
            )
            taper_flat = (
                jnp.broadcast_to(taper[None], (levels_total, row_count, col_count)).reshape(-1)
                * wet_flat
            )
            covariance = jnp.dot(anomaly, flat_state, precision=lax.Precision.HIGHEST)
            kalman = taper_flat * covariance / (spread * denominator)
            flat_state = flat_state + weight[:, None] * kalman[None, :]
            prior_cov = jnp.dot(priors, anomaly, precision=lax.Precision.HIGHEST)
            priors = (
                priors
                + (mutual[obs_num] * prior_cov / (spread * denominator))[:, None] * weight[None, :]
            )
        deferred = flat_state - before
    total_inc, wet_count = increment_sums(deferred, wet_cells, levels_total, members)
    pending = pending + total_inc / (members * wet_count)
    flat_state = (
        flat_state.reshape(members, levels_total, -1)
        - pending[None, :, None] * wet_cells[None, None, :]
    ).reshape(members, -1)
    return flat_state.reshape(members, fields, levels, row_count, col_count)


def solution(mesh):
    in_specs = (
        P("member", None, None, None, "domain"),
        P(None, None, None, "domain"),
        P(),
        P(None, "domain"),
        P(),
        P(),
        P(),
        P(),
    )
    out_specs = P(None, None, None, "member", "domain")
    return jax.shard_map(local, mesh=mesh, in_specs=in_specs, out_specs=out_specs, check_vma=False)
```

profile of v0, /device:TPU:0, one launch (start us, length us, event | category | flops | bytes accessed | tf_op | source)
XLA Modules:
  0.0 1168.0 jit_solution(10798302134221968660)
XLA Ops:
  19.1 6.6 copy.70
  31.2 8.1 fusion.475
  100.0 12.5 %add_multiply_fusion = f32[20,4,3,16,256]{4,0,2,1,3:T(8,128)} fusion(f32[20,4,3,16,256]{4,0,2,1,3:T(8,128)} %copy.70, f32[20,4,3,15,256]{4,0,2,1,3:T(8,128)} %get-tuple-element.94, f32[20,4,3,15,256]{4,0,2,1,3:T(8,128)} %get-tuple-element.93, f32[20,4,3,16,1]{4,0,2,1,3:T(8,128)S(1)} %copy.62, f32[20,4,3,16,1]{4,0,2,1,3:T(8,128)} %copy.64, f32[4]{0:T(128)} %param.12, ...), kind=kLoop, calls=%fused_computation.6 | loop fusion | flops 17694720 | bytes 15382544 | tf_op jit(solution)/shard_map/mul | solution.py:54
  112.7 17.4 %all-to-all-start = ((f32[20,4,3,16,256]{4,0,2,1,3:T(8,128)}), f32[20,4,3,16,256]{4,0,2,1,3:T(8,128)}, u32[]{:S(2)}, u32[]{:S(2)}) async-start(f32[20,4,3,16,256]{4,0,2,1,3:T(8,128)} %add_multiply_fusion), calls=%async_computation | async-start | bytes 9437184 | tf_op jit(solution)/shard_map/all_to_all | solution.py:58
  143.7 38.2 %all-to-all-done = f32[20,4,3,16,256]{4,0,2,1,3:T(8,128)} async-done(((f32[20,4,3,16,256]{4,0,2,1,3:T(8,128)}), f32[20,4,3,16,256]{4,0,2,1,3:T(8,128)}, u32[]{:S(2)}, u32[]{:S(2)}) %all-to-all-start) | async-done | bytes 3932192 | tf_op jit(solution)/shard_map/all_to_all | solution.py:58
  182.0 6.8 copy.119
  188.8 5.8 reshape.9563
  194.5 6.0 copy.72
  204.0 38.7 %psum.72 = f32[8,80]{1,0:T(8,128)S(1)} all-reduce(f32[8,80]{1,0:T(8,128)S(1)} %fusion.191), channel_id=1, replica_groups=mesh['member'=4,'domain'=8] {'member','domain'}, use_global_device_ids=true, to_apply=%region_0.0 | all-reduce | flops 640 | bytes 5120 | tf_op jit(solution)/shard_map/psum | solution.py:24
  284.7 7.2 multiply_add_fusion.33
  291.9 5.8 add.4235
  301.8 7.6 multiply_add_fusion.32
  309.4 5.8 add.4250
  319.3 7.4 multiply_add_fusion.31
  326.7 5.8 add.4265
  336.6 7.8 multiply_add_fusion.30
  344.4 5.9 add.4280
  354.4 7.6 multiply_add_fusion.29
  362.1 5.8 add.4295
  372.0 8.0 multiply_add_fusion.28
  379.9 6.0 add.4310
  390.0 8.1 multiply_add_fusion.27
  398.1 5.8 add.4325
  413.2 6.0 copy.73
  419.3 8.6 subtract_reduce_fusion.3
  431.5 41.0 %all-reduce.4 = (f32[12]{0:T(128)S(1)}, f32[]{:T(128)}, f32[8,80]{1,0:T(8,128)S(1)}) all-reduce(f32[12]{0:T(128)S(1)} %reduce_sum.726, f32[]{:T(128)} %get-tuple-element.126, f32[8,80]{1,0:T(8,128)S(1)} %fusion.190), channel_id=1, replica_groups=mesh['member'=4,'domain'=8] {'member','domain'}, use_global_device_ids=true, to_apply=%region_20.22 | all-reduce | flops 653 | bytes 5224 | tf_op jit(solution)/shard_map/psum | solution.py:64
  512.5 5.8 add.4356
  543.1 5.8 add.4395
  583.0 6.1 multiply_add_fusion.20
  589.1 5.9 add.4440
  599.1 6.9 multiply_add_fusion.19
  615.8 7.4 multiply_add_fusion.18
  623.2 6.1 add.4470
  633.4 8.7 multiply_add_fusion.17
  642.1 6.0 copy.74
  648.2 8.0 subtract_reduce_fusion.2
  659.9 40.0 %all-reduce.3 = (f32[12]{0:T(128)S(1)}, f32[8,80]{1,0:T(8,128)S(1)}) all-reduce(f32[12]{0:T(128)S(1)} %reduce_sum.747, f32[8,80]{1,0:T(8,128)S(1)} %fusion.189), channel_id=1, replica_groups=mesh['member'=4,'domain'=8] {'member','domain'}, use_global_device_ids=true, to_apply=%region_43.45 | all-reduce | flops 652 | bytes 5216 | tf_op jit(solution)/shard_map/psum | solution.py:64
  738.6 5.8 add.4502
  769.1 5.9 add.4541
  784.0 5.7 add.4556
  809.1 6.1 multiply_add_fusion.11
  815.2 6.1 add.4586
  825.4 6.8 multiply_add_fusion.10
  842.1 7.4 multiply_add_fusion.9
  849.5 5.8 add.4616
  859.5 10.9 multiply_add_fusion.8
  870.4 6.0 copy.75
  876.5 8.1 subtract_reduce_fusion.1
  888.3 40.6 %all-reduce.2 = (f32[12]{0:T(128)S(1)}, f32[8,80]{1,0:T(8,128)S(1)}) all-reduce(f32[12]{0:T(128)S(1)} %reduce_sum.767, f32[8,80]{1,0:T(8,128)S(1)} %fusion.188), channel_id=1, replica_groups=mesh['member'=4,'domain'=8] {'member','domain'}, use_global_device_ids=true, to_apply=%region_64.66 | all-reduce | flops 652 | bytes 5216 | tf_op jit(solution)/shard_map/psum | solution.py:64
  969.3 5.8 add.4648
  984.5 5.7 add.4672
  999.9 6.1 add.4687
  1015.1 5.7 add.4702
  1030.4 5.7 add.4717
  1040.2 6.0 multiply_add_fusion.2
  1046.3 5.9 add.4732
  1056.3 6.8 multiply_add_fusion.1
  1063.1 5.7 add.4747
  1072.9 7.3 multiply_add_fusion
  1080.2 5.7 add.4762
  1090.0 7.0 subtract_reduce_fusion
  1097.2 6.8 copy.71
  1103.9 39.9 %psum.80 = f32[12]{0:T(128)S(1)} all-reduce(f32[12]{0:T(128)S(1)} %reduce_sum.787), channel_id=1, replica_groups=mesh['member'=4,'domain'=8] {'member','domain'}, use_global_device_ids=true, to_apply=%region_84.86 | all-reduce | flops 12 | bytes 96 | tf_op jit(solution)/shard_map/psum | solution.py:64
  1144.0 23.8 %add_subtract_fusion = f32[80,4,3,4,256]{4,3,2,1,0:T(4,128)} fusion(f32[20,4,3,4,4,256]{5,4,2,1,0,3:T(4,128)} %copy.71, f32[4,3,4,256]{3,2,1,0:T(4,128)S(1)} %broadcast_multiply_fusion, f32[4,3,4,256]{3,2,1,0:T(4,128)S(1)} %mul.7381, f32[80]{0:T(128)S(1)} %get-tuple-element.210, f32[4,3,4,256]{3,2,1,0:T(4,128)S(1)} %mul.7348, f32[80]{0:T(128)S(1)} %fusion.266, ...), kind=kLoop, calls=%fused_computation.21 | loop fusion | flops 63897600 | bytes 9496576 | tf_op jit(solution)/shard_map/sub | solution.py:162
  (616 shorter events, 392.1 us)
Async XLA Ops:
  4.1 9.8 copy-start.42
  7.0 87.3 %collective-permute-start = (f32[20,4,3,16,1]{0,3,4,2,1:T(8,128)S(1)}, f32[20,4,3,16,1]{0,3,4,2,1:T(8,128)}, u32[]{:S(2)}, u32[]{:S(2)}) collective-permute-start(f32[20,4,3,16,1]{0,3,4,2,1:T(8,128)S(1)} %copy.76), channel_id=1, source_target_pairs={{1,0},{2,1},{3,2},{4,3},{5,4},{6,5},{7,6},{0,7},{9,8},{10,9},{11,1... | collective-permute-start | bytes 46088 | tf_op jit(solution)/shard_map/ppermute | solution.py:17
  13.6 82.9 %collective-permute-start.1 = (f32[20,4,3,16,1]{0,3,4,2,1:T(8,128)}, f32[20,4,3,16,1]{0,3,4,2,1:T(8,128)}, u32[]{:S(2)}, u32[]{:S(2)}) collective-permute-start(f32[20,4,3,16,1]{0,3,4,2,1:T(8,128)} %copy.77), channel_id=1, source_target_pairs={{0,1},{1,2},{2,3},{3,4},{4,5},{5,6},{6,7},{7,0},{8,9},{9,10},{10,1... | collective-permute-start | bytes 46088 | tf_op jit(solution)/shard_map/ppermute | solution.py:16
  19.1 11.9 %copy-start.41 = (s32[4,8,4]{1,2,0:T(4,128)S(1)}, s32[4,8,4]{1,2,0:T(4,128)}, u32[]{:S(2)}) copy-start(s32[4,8,4]{1,2,0:T(4,128)} %param.14) | copy-start | bytes 1540
  31.1 8.2 copy-start.30
  31.1 10.2 copy-start.32
  31.1 10.2 copy-start.39
  31.1 32.6 %copy-start.28 = (s32[8,4]{0,1:T(4,128)}, s32[8,4]{0,1:T(4,128)S(1)}, u32[]{:S(2)}) copy-start(s32[8,4]{0,1:T(4,128)S(1)} %get-tuple-element.99) | copy-start | bytes 388
  31.1 8.1 copy-start.17
  31.1 8.1 copy-start.34
  39.9 23.8 %copy-start.18 = (s32[8,1]{0,1:T(1,128)}, s32[8,1]{0,1:T(1,128)S(1)}, u32[]{:S(2)}) copy-start(s32[8,1]{0,1:T(1,128)S(1)} %get-tuple-element.201) | copy-start | bytes 100
  41.9 21.8 %copy-start.20 = (s32[8,1]{0,1:T(1,128)}, s32[8,1]{0,1:T(1,128)S(1)}, u32[]{:S(2)}) copy-start(s32[8,1]{0,1:T(1,128)S(1)} %get-tuple-element.346) | copy-start | bytes 100
  41.9 52.3 %copy-start.22 = (s32[8,1]{0,1:T(1,128)}, s32[8,1]{0,1:T(1,128)S(1)}, u32[]{:S(2)}) copy-start(s32[8,1]{0,1:T(1,128)S(1)} %get-tuple-element.347) | copy-start | bytes 100
  41.9 52.4 %copy-start.24 = (s32[8,1]{0,1:T(1,128)}, s32[8,1]{0,1:T(1,128)S(1)}, u32[]{:S(2)}) copy-start(s32[8,1]{0,1:T(1,128)S(1)} %get-tuple-element.208) | copy-start | bytes 100
  41.9 52.4 %copy-start.26 = (s32[8,1]{0,1:T(1,128)}, s32[8,1]{0,1:T(1,128)S(1)}, u32[]{:S(2)}) copy-start(s32[8,1]{0,1:T(1,128)S(1)} %get-tuple-element.209) | copy-start | bytes 100
  112.5 17.6 %copy-start.38 = (f32[4,256]{1,0:T(4,128)S(1)}, f32[4,256]{1,0:T(4,128)}, u32[]{:S(2)}) copy-start(f32[4,256]{1,0:T(4,128)} %get-tuple-element.105) | copy-start | bytes 12292
  112.5 20.8 %copy-start.1 = (f32[12,2,4,128]{3,2,1,0:T(4,128)S(1)}, f32[12,2,4,128]{3,2,1,0:T(4,128)}, u32[]{:S(2)}) copy-start(f32[12,2,4,128]{3,2,1,0:T(4,128)} %broadcast_bitcast_fusion.10) | copy-start | bytes 147460
  112.5 20.9 %copy-start.2 = (f32[12,2,4,128]{3,2,1,0:T(4,128)S(1)}, f32[12,2,4,128]{3,2,1,0:T(4,128)}, u32[]{:S(2)}) copy-start(f32[12,2,4,128]{3,2,1,0:T(4,128)} %broadcast_bitcast_fusion.9) | copy-start | bytes 147460
  112.5 20.9 %copy-start.3 = (f32[12,2,4,128]{3,2,1,0:T(4,128)S(1)}, f32[12,2,4,128]{3,2,1,0:T(4,128)}, u32[]{:S(2)}) copy-start(f32[12,2,4,128]{3,2,1,0:T(4,128)} %broadcast_bitcast_fusion.8) | copy-start | bytes 147460
  112.5 21.5 %copy-start.4 = (f32[12,2,4,128]{3,2,1,0:T(4,128)S(1)}, f32[12,2,4,128]{3,2,1,0:T(4,128)}, u32[]{:S(2)}) copy-start(f32[12,2,4,128]{3,2,1,0:T(4,128)} %broadcast_bitcast_fusion.7) | copy-start | bytes 147460
  112.5 22.2 %copy-start.5 = (f32[12,2,4,128]{3,2,1,0:T(4,128)S(1)}, f32[12,2,4,128]{3,2,1,0:T(4,128)}, u32[]{:S(2)}) copy-start(f32[12,2,4,128]{3,2,1,0:T(4,128)} %broadcast_bitcast_fusion.6) | copy-start | bytes 147460
  112.5 22.8 %copy-start.6 = (f32[12,2,4,128]{3,2,1,0:T(4,128)S(1)}, f32[12,2,4,128]{3,2,1,0:T(4,128)}, u32[]{:S(2)}) copy-start(f32[12,2,4,128]{3,2,1,0:T(4,128)} %broadcast_bitcast_fusion.5) | copy-start | bytes 147460
  112.5 23.5 %copy-start.7 = (f32[12,2,4,128]{3,2,1,0:T(4,128)S(1)}, f32[12,2,4,128]{3,2,1,0:T(4,128)}, u32[]{:S(2)}) copy-start(f32[12,2,4,128]{3,2,1,0:T(4,128)} %broadcast_bitcast_fusion.4) | copy-start | bytes 147460
  112.5 24.7 %copy-start.37 = (f32[4,256]{1,0:T(4,128)S(1)}, f32[4,256]{1,0:T(4,128)}, u32[]{:S(2)}) copy-start(f32[4,256]{1,0:T(4,128)} %get-tuple-element.104) | copy-start | bytes 12292
  112.5 25.4 %copy-start.33 = (s32[8,4]{0,1:T(4,128)S(1)}, s32[8,4]{0,1:T(4,128)}, u32[]{:S(2)}) copy-start(s32[8,4]{0,1:T(4,128)} %copy-done.32) | copy-start | bytes 388
  112.6 25.4 %copy-start.40 = (s32[8,4]{0,1:T(4,128)S(1)}, s32[8,4]{0,1:T(4,128)}, u32[]{:S(2)}) copy-start(s32[8,4]{0,1:T(4,128)} %copy-done.39) | copy-start | bytes 388
  112.6 25.4 %copy-start.29 = (s32[8,4]{0,1:T(4,128)S(1)}, s32[8,4]{0,1:T(4,128)}, u32[]{:S(2)}) copy-start(s32[8,4]{0,1:T(4,128)} %copy-done.28) | copy-start | bytes 388
  112.6 25.4 %copy-start.31 = (s32[8,4]{0,1:T(4,128)S(1)}, s32[8,4]{0,1:T(4,128)}, u32[]{:S(2)}) copy-start(s32[8,4]{0,1:T(4,128)} %copy-done.30) | copy-start | bytes 388
  112.6 26.6 %copy-start.15 = (f32[4,8]{1,0:T(4,128)S(1)}, f32[4,8]{1,0:T(4,128)}, u32[]{:S(2)}) copy-start(f32[4,8]{1,0:T(4,128)} %param.17) | copy-start | bytes 388
  112.6 27.3 %copy-start.16 = (f32[4,8]{1,0:T(4,128)S(1)}, f32[4,8]{1,0:T(4,128)}, u32[]{:S(2)}) copy-start(f32[4,8]{1,0:T(4,128)} %param.16) | copy-start | bytes 388
  112.6 29.5 %copy-start.25 = (s32[8,1]{0,1:T(1,128)S(1)}, s32[8,1]{0,1:T(1,128)}, u32[]{:S(2)}) copy-start(s32[8,1]{0,1:T(1,128)} %copy-done.24) | copy-start | bytes 100
  112.6 29.5 %copy-start.27 = (s32[8,1]{0,1:T(1,128)S(1)}, s32[8,1]{0,1:T(1,128)}, u32[]{:S(2)}) copy-start(s32[8,1]{0,1:T(1,128)} %copy-done.26) | copy-start | bytes 100
  112.6 29.6 %copy-start.21 = (s32[8,1]{0,1:T(1,128)S(1)}, s32[8,1]{0,1:T(1,128)}, u32[]{:S(2)}) copy-start(s32[8,1]{0,1:T(1,128)} %copy-done.20) | copy-start | bytes 100
  112.6 29.6 %copy-start.23 = (s32[8,1]{0,1:T(1,128)S(1)}, s32[8,1]{0,1:T(1,128)}, u32[]{:S(2)}) copy-start(s32[8,1]{0,1:T(1,128)} %copy-done.22) | copy-start | bytes 100
  112.6 29.8 %copy-start.19 = (s32[8,1]{0,1:T(1,128)S(1)}, s32[8,1]{0,1:T(1,128)}, u32[]{:S(2)}) copy-start(s32[8,1]{0,1:T(1,128)} %copy-done.18) | copy-start | bytes 100
  112.7 30.4 %copy-start.36 = (f32[4,256]{1,0:T(4,128)S(1)}, f32[4,256]{1,0:T(4,128)}, u32[]{:S(2)}) copy-start(f32[4,256]{1,0:T(4,128)} %get-tuple-element.103) | copy-start | bytes 12292
  112.7 30.5 %copy-start.35 = (f32[4,256]{1,0:T(4,128)S(1)}, f32[4,256]{1,0:T(4,128)}, u32[]{:S(2)}) copy-start(f32[4,256]{1,0:T(4,128)} %get-tuple-element.15) | copy-start | bytes 12292
  112.7 69.3 %all-to-all-start = ((f32[20,4,3,16,256]{4,0,2,1,3:T(8,128)}), f32[20,4,3,16,256]{4,0,2,1,3:T(8,128)}, u32[]{:S(2)}, u32[]{:S(2)}) async-start(f32[20,4,3,16,256]{4,0,2,1,3:T(8,128)} %add_multiply_fusion), calls=%async_computation | async-start | bytes 9437184 | tf_op jit(solution)/shard_map/all_to_all | solution.py:58
  419.3 53.8 %copy-start.47 = (s32[8]{0:T(128)S(1)}, s32[8]{0:T(128)}, u32[]{:S(2)}) copy-start(s32[8]{0:T(128)} %get-tuple-element.348) | copy-start | bytes 100
  648.2 51.7 %copy-start.46 = (s32[8]{0:T(128)S(1)}, s32[8]{0:T(128)}, u32[]{:S(2)}) copy-start(s32[8]{0:T(128)} %get-tuple-element.202) | copy-start | bytes 100
  855.3 4.1 copy-start.14
  876.5 11.7 %copy-start.44 = (pred[8]{0:T(512)(128)(4,1)S(1)}, pred[8]{0:T(512)(128)(4,1)}, u32[]{:S(2)}) copy-start(pred[8]{0:T(512)(128)(4,1)} %get-tuple-element.31) | copy-start | bytes 28
  876.5 11.8 %copy-start = (f32[12,2,4,128]{3,2,1,0:T(4,128)S(1)}, f32[12,2,4,128]{3,2,1,0:T(4,128)}, u32[]{:S(2)}) copy-start(f32[12,2,4,128]{3,2,1,0:T(4,128)} %broadcast_bitcast_fusion) | copy-start | bytes 147460
  876.5 52.5 %copy-start.45 = (s32[8]{0:T(128)S(1)}, s32[8]{0:T(128)}, u32[]{:S(2)}) copy-start(s32[8]{0:T(128)} %get-tuple-element.199) | copy-start | bytes 100
  876.5 57.4 %copy-start.43 = (f32[8,8]{1,0:T(8,128)S(1)}, f32[8,8]{1,0:T(8,128)}, u32[]{:S(2)}) copy-start(f32[8,8]{1,0:T(8,128)} %fusion.166) | copy-start | bytes 772
  975.1 4.1 copy-start.13
  990.2 4.1 copy-start.12
  1006.1 4.1 copy-start.11
  1020.8 4.1 copy-start.10
  1036.1 4.1 copy-start.9
  1052.1 4.1 copy-start.8
where the time goes:
time: 1170 us
  other arithmetic  365 us (31%)
  local copies, waits for them, and re-layouts  289 us (25%)
  blocking collectives  200 us (17%)
  matrix products  134 us (11%)
  between operations  120 us (10%)
  waiting for transfers between devices  38.2 us (3%)
  starting transfers between devices  22.3 us (2%)
    add x31, other arithmetic, local(): flat_state = flat_state + weight[:, None] * kalman[None, :]  203 us
    add x34, local copies, waits for them, and re-layouts, local(): flat_state = flat_state + weight[:, None] * kalman[None, :]  198 us
    psum x4, blocking collectives, increment_sums(): return lax.psum((local_sum, jnp.sum(wet_cells)), ('member', 'domain'))  161 us
    dot_general x32, matrix products, local(): covariance = jnp.dot(anomaly, flat_state, precision=lax.Precision.HIGHEST)  130 us
    mul x56, other arithmetic, separation(): return jnp.sqrt((col_gap * col_gap + row_gap * row_gap).astype(jnp.float32))  40.8 us
    psum x1, blocking collectives, broadcast(): return lax.psum(kept, axis)  38.7 us
    all_to_all x1, waiting for transfers between devices, regroup(): lax.all_to_all(member_state, 'member', split_axis=3, concat_axis=0, tiled...  38.2 us
    reduce_sum x4, other arithmetic, increment_sums(): per_cell = jnp.sum(change_flat.reshape(members, levels_total, -1), axis=0)  31.6 us
  transfers between devices with their start and end apart: 3, of which 1 were waited for; matrix products, arithmetic and copies ran while one was open for 7% of the time, Pallas kernels for 0%

commit v1 on v0

v1 whole, which is shorter than its diff:
```python
import functools

import jax
import jax.numpy as jnp
from jax import lax
from jax.experimental import pallas as pl
from jax.experimental.pallas import tpu as pltpu
from jax.sharding import PartitionSpec as P

LOC_RADIUS = 64
LANES = 128
SUBS = 8
F32 = jnp.float32
BF16 = jnp.bfloat16
HIGHEST = lax.Precision.HIGHEST
VMEM = pltpu.VMEM
SMEM = pltpu.SMEM


def gaspari(scaled):
    scaled_safe = jnp.maximum(scaled, 1.0)
    near_part = (
        ((-0.25 * scaled + 0.5) * scaled + 0.625) * scaled - 5.0 / 3.0
    ) * scaled * scaled + 1.0
    far_part = (
        ((((scaled / 12.0 - 0.5) * scaled + 0.625) * scaled + 5.0 / 3.0) * scaled - 5.0) * scaled
        + 4.0
        - 2.0 / (3.0 * scaled_safe)
    )
    return jnp.where(scaled <= 1.0, near_part, jnp.where(scaled < 2.0, far_part, 0.0))


def taper(row_gap, col_gap, grid_width):
    col_gap = jnp.abs(col_gap)
    col_gap = jnp.minimum(col_gap, grid_width - col_gap)
    square = (col_gap * col_gap + row_gap * row_gap).astype(F32)
    return gaspari(jnp.sqrt(square) * (1.0 / LOC_RADIUS))


def iota(shape, dim):
    return lax.broadcasted_iota(jnp.int32, shape, dim)


def split(value):
    high = value.astype(BF16)
    return high, (value - high.astype(F32)).astype(BF16)


def dot(a, b):
    return lax.dot_general(a, b, (((1,), (0,)), ((), ())), preferred_element_type=F32)


def dot_exact(a, b, dims):
    return lax.dot_general(
        a, b, ((dims[:1], dims[1:]), ((), ())), precision=HIGHEST, preferred_element_type=F32
    )


class Sizes:
    def __init__(self, ensemble, velocity, obs_index):
        self.own, self.fields, self.levels, self.rows, self.cols = ensemble.shape
        self.states = self.fields * self.levels
        self.groups_m = lax.axis_size("member")
        self.groups_d = lax.axis_size("domain")
        self.members = self.own * self.groups_m
        self.block_rows = self.rows // self.groups_m
        self.col_tiles = self.cols // LANES
        self.cells = self.block_rows * self.col_tiles
        self.per_step = SUBS // self.cells
        self.steps = self.states // self.per_step
        self.width = self.cols * self.groups_d
        self.batches, self.batch = obs_index.shape[:2]
        self.obs = self.batches * self.batch
        self.halo = -(-self.own * self.states // LANES) * LANES
        self.packs = -(-self.own // SUBS)
        self.pack_states = LANES // self.obs
        self.sum_rows = -(-self.states // self.pack_states)


def edges_kernel(z, x_ref, first_ref, last_ref):
    step = pl.program_id(0)

    @pl.when(step == 0)
    def _():
        first_ref[...] = jnp.zeros_like(first_ref)
        last_ref[...] = jnp.zeros_like(last_ref)

    lane = iota((z.rows, z.halo), 1)
    first, last = first_ref[...], last_ref[...]
    for q in range(z.per_step):
        base = (step * z.per_step + q) * z.own
        for m in range(z.own):
            hit = lane == base + m
            first = jnp.where(hit, x_ref[m, q, :, 0:1], first)
            last = jnp.where(hit, x_ref[m, q, :, z.cols - 1 : z.cols], last)
    first_ref[...] = first
    last_ref[...] = last


def forecast_kernel(
    z, place, index, owner, diff, x_ref, before_ref, after_ref, vel_ref, mask_ref, out_ref, obs_ref,
    state, picked, sems,
):
    step = pl.program_id(0)
    shape = (z.rows, z.cols)
    row, col = iota(shape, 0), iota(shape, 1)
    wet = mask_ref[...].astype(F32)
    stride = z.states * z.cells
    flat = state.reshape(z.members * stride, LANES)
    for q in range(z.per_step):
        fl = step * z.per_step + q
        level = lax.rem(fl, z.levels)
        spread = diff[fl // z.levels]
        half_u = 0.5 * vel_ref[0, level]
        half_v = 0.5 * vel_ref[1, level]
        center = wet * (1.0 - 4.0 * spread)
        east = wet * (spread - half_u)
        west = wet * (spread + half_u)
        north = jnp.where(row == z.rows - 1, 0.0, wet * (spread - half_v))
        south = jnp.where(row == 0, 0.0, wet * (spread + half_v))
        turn = lax.rem(z.halo - fl * z.own, z.halo)
        before = pltpu.roll(before_ref[...], turn, 1)
        after = pltpu.roll(after_ref[...], turn, 1)
        for m in range(z.own):
            x = x_ref[m, q]
            nxt = jnp.where(col == z.cols - 1, after[:, m : m + 1], pltpu.roll(x, z.cols - 1, 1))
            prv = jnp.where(col == 0, before[:, m : m + 1], pltpu.roll(x, 1, 1))
            y = (
                center * x
                + east * nxt
                + west * prv
                + north * pltpu.roll(x, z.rows - 1, 0)
                + south * pltpu.roll(x, 1, 0)
            )
            for p in range(z.groups_m):
                for c in range(z.col_tiles):
                    at = (p * z.own + m) * stride + q * z.cells + c * z.block_rows
                    flat[pl.ds(pl.multiple_of(step * SUBS, SUBS) + at, z.block_rows), :] = y[
                        p * z.block_rows : (p + 1) * z.block_rows, c * LANES : (c + 1) * LANES
                    ]

    def copy(at):
        lines = pl.ds(pl.multiple_of(at * SUBS, SUBS), SUBS)
        return pltpu.make_async_copy(state.at[:, lines, :], out_ref.at[:, lines, :], sems.at[at])

    copy(step).start()

    @pl.when(step == z.steps - 1)
    def _():
        picked[...] = jnp.zeros_like(picked)
        lane = iota((z.own, LANES), 1)

        def pick(k, carry):
            b, i = k // z.batch, lax.rem(k, z.batch)

            @pl.when(lax.rem(owner[b], z.groups_d) == place[1])
            def _():
                fl = index[b, i, 0] * z.levels + index[b, i, 1]
                at = index[b, i, 3]
                cell = (at // LANES) * z.block_rows + index[b, i, 2]
                base = (owner[b] // z.groups_d) * z.own * stride + fl * z.cells + cell
                got = flat[pl.ds(base, z.own, stride=stride), :]
                got = jnp.sum(
                    jnp.where(lane == lax.rem(at, LANES), got, 0.0), axis=1, keepdims=True
                )
                picked[0 : z.own, :] = jnp.where(lane == k, got, picked[0 : z.own, :])

            return carry

        lax.fori_loop(0, z.obs, pick, 0)
        total = picked[0:SUBS, :]
        for v in range(1, z.packs):
            total = total + pltpu.roll(picked[v * SUBS : (v + 1) * SUBS, :], v * z.obs, 1)
        obs_ref[...] = total

        def drain(i, carry):
            copy(i).wait()
            return carry

        lax.fori_loop(0, z.steps, drain, 0)


def filter_kernel(
    z, place, index, owner, value, error, got_ref, mask_ref,
    gain_ref, cross_ref, lift_ref, taper_ref, relay_ref, gap_ref, wet_ref,
):
    n = z.obs
    eight = z.groups_m * SUBS
    stacked = []
    for s in range(z.groups_m):
        total = got_ref[s * z.groups_d]
        for d in range(1, z.groups_d):
            total = total + got_ref[s * z.groups_d + d]
        stacked.append(total)
    stacked = jnp.concatenate(stacked, axis=0)
    square = (n, LANES)
    prior = jnp.zeros(square, F32)
    row, lane = iota(square, 0), iota(square, 1)
    for v in range(z.packs):
        pick = (lane == row + v * n).astype(F32)
        part = dot_exact(pick, stacked, (1, 1))
        src = iota((eight, LANES), 0)
        dst = iota((eight, LANES), 1)
        slot = v * SUBS + src % SUBS
        place_of = jnp.where(slot < z.own, (src // SUBS) * z.own + slot, -1)
        prior = prior + dot_exact(part, (dst == place_of).astype(F32), (1, 0))
    ones = jnp.full((SUBS, LANES), 1.0 / z.members, F32)
    mean_row = dot_exact(ones, prior, (1, 1))
    mean = jnp.sum(prior, axis=1, keepdims=True) * (1.0 / z.members)
    anomaly = jnp.where(lane < z.members, prior - mean, 0.0)
    rows_s, cols_s = jnp.zeros(square, jnp.int32), jnp.zeros(square, jnp.int32)
    rows_l, cols_l = rows_s, cols_s
    values = jnp.zeros((SUBS, n), F32)
    value_lane = iota((SUBS, n), 1)
    shape = (SUBS, LANES)
    sub = iota(shape, 0) % z.cells
    tile_col = (sub // z.block_rows) * LANES + iota(shape, 1)
    cell_row = place[0] * z.block_rows + sub % z.block_rows
    cell_col = place[1] * z.cols + tile_col
    wet = jnp.zeros(shape, F32)
    line_of = iota(shape, 0) + place[0] * SUBS
    for c in range(z.col_tiles):
        for full_row in range(z.rows):
            line = mask_ref[full_row : full_row + 1, c * LANES : (c + 1) * LANES].astype(F32)
            p, r = divmod(full_row, z.block_rows)
            for q in range(z.per_step):
                spot = p * SUBS + q * z.cells + c * z.block_rows + r
                wet = jnp.where(line_of == spot, line, wet)
    wet_ref[...] = wet
    for k in range(n):
        b, i = divmod(k, z.batch)
        at_row = owner[b] // z.groups_d * z.block_rows + index[b, i, 2]
        at_col = lax.rem(owner[b], z.groups_d) * z.cols + index[b, i, 3]
        rows_s = jnp.where(row == k, at_row, rows_s)
        cols_s = jnp.where(row == k, at_col, cols_s)
        rows_l = jnp.where(lane == k, at_row, rows_l)
        cols_l = jnp.where(lane == k, at_col, cols_l)
        values = jnp.where(value_lane == k, value[b, i], values)
        taper_ref[k] = wet * taper(cell_row - at_row, cell_col - at_col, z.width)
    gap_ref[...] = jnp.zeros_like(gap_ref)
    gap_ref[:, 0:n] = values - mean_row
    mutual = taper(rows_s - rows_l, cols_s - cols_l, z.width)
    relay = jnp.zeros(square, F32)
    inverse_l = jnp.zeros(square, F32)
    inverse_s = jnp.zeros(square, F32)
    shrink_s = jnp.zeros(square, F32)
    spread = float(z.members - 1)
    for k in range(n):
        b, i = divmod(k, z.batch)
        own = anomaly[k : k + 1, :]
        product = jnp.sum(anomaly * own, axis=1, keepdims=True)
        variance = product[k : k + 1, :] * (1.0 / spread) + error[b, i]
        inverse = 1.0 / (spread * variance)
        shrink = 1.0 / (1.0 + jnp.sqrt(error[b, i] / variance))
        ratio = jnp.where(row[:, 0:1] > k, mutual[:, k : k + 1] * product * inverse, 0.0)
        anomaly = anomaly - (shrink * ratio) * own
        relay = jnp.where(lane == k, ratio, relay)
        inverse_l = jnp.where(lane == k, inverse, inverse_l)
        inverse_s = jnp.where(row == k, inverse, inverse_s)
        shrink_s = jnp.where(row == k, shrink, shrink_s)
    gram = dot_exact(anomaly, anomaly, (1, 1))
    cross_ref[...] = -shrink_s[:, 0:n] * inverse_l[:, 0:n] * gram
    high, low = split(anomaly * inverse_s)
    gain_ref[0:n, :] = high[:, 0 : z.members]
    gain_ref[n : 2 * n, :] = low[:, 0 : z.members]
    eye = (iota((z.members, LANES), 0) == iota((z.members, LANES), 1)).astype(F32)
    lift_ref[...] = dot_exact(eye, shrink_s * anomaly, (1, 1))
    eye = (iota((n, LANES), 0) == iota((n, LANES), 1)).astype(F32)
    relay_ref[...] = dot_exact(eye, relay, (1, 1))


def gain_kernel(z, cross, x_ref, gain_ref, taper_ref, wet_ref, kalman_ref, sums_ref, work, held):
    n = z.obs
    step = pl.program_id(0)
    flat_x = x_ref.reshape(z.members * SUBS, LANES)
    flat_k = kalman_ref.reshape(SUBS * n, LANES)
    both = gain_ref[...]
    high = gain_ref[0:n, :]
    for s in range(0, SUBS, 2):
        x = jnp.concatenate(
            [flat_x[pl.ds(s + t, z.members, stride=SUBS), :] for t in range(2)], axis=1
        )
        x_high, x_low = split(x)
        first = dot(both, x_high)
        total = first[0:n] + first[n : 2 * n] + dot(high, x_low)
        work[s * n : (s + 1) * n, :] = total[:, 0:LANES]
        work[(s + 1) * n : (s + 2) * n, :] = total[:, LANES : 2 * LANES]
    part = [work[pl.ds(k, SUBS, stride=n), :] for k in range(n)]
    for k in range(n):
        kalman = taper_ref[k] * part[k]
        flat_k[pl.ds(k, SUBS, stride=n), :] = kalman
        for j in range(k + 1, n):
            part[j] = part[j] + cross[k, j] * kalman
    for q in range(z.per_step):
        total = flat_k[q * z.cells * n : (q * z.cells + 1) * n, :]
        for s in range(q * z.cells + 1, (q + 1) * z.cells):
            total = total + flat_k[s * n : (s + 1) * n, :]
        at = pl.multiple_of((step * z.per_step + q) * n, n)
        held[pl.ds(at, n), :] = total

    @pl.when(step == z.steps - 1)
    def _():
        ones = jnp.ones((SUBS, LANES), F32)
        sums_ref[...] = jnp.zeros_like(sums_ref)
        for i in range(z.sum_rows):
            line = dot_exact(ones, held[i * LANES : (i + 1) * LANES, :], (1, 1))
            sums_ref[i : i + 1, :] = line[0:1, :]
        wet = jnp.sum(wet_ref[0 : z.cells, :], axis=0, keepdims=True)
        sums_ref[z.sum_rows : z.sum_rows + 1, :] = wet


def update_kernel(
    z, index, x_ref, kalman_ref, sums_ref, lift_ref, relay_ref, gap_ref, wet_ref, out_ref,
    weight, moved,
):
    n = z.obs
    step = pl.program_id(0)

    @pl.when(step == 0)
    def _():
        sums = sums_ref[0]
        for d in range(1, z.groups_m * z.groups_d):
            sums = sums + sums_ref[d]
        count = jnp.sum(sums[z.sum_rows : z.sum_rows + 1, :], axis=1, keepdims=True)
        lines = []
        for fl in range(z.states):
            i, c = divmod(fl, z.pack_states)
            lines.append(sums[i : i + 1, c * n : (c + 1) * n])
        pad = -z.states % SUBS
        table = jnp.concatenate(lines + [jnp.zeros((pad, n), F32)], axis=0) / count
        eye = (iota((n, n), 0) == iota((n, n), 1)).astype(F32)
        turned = dot_exact(eye, table, (1, 1))
        shape = (z.states + pad, n)
        fl_row, lane = iota(shape, 0), iota(shape, 1)
        at = jnp.zeros(shape, jnp.int32)
        for k in range(n):
            b, i = divmod(k, z.batch)
            at = jnp.where(lane == k, index[b, i, 0] * z.levels + index[b, i, 1], at)
        chosen = dot_exact(turned, (fl_row == at).astype(F32), (1, 0))
        later = iota((n, n), 1) // z.batch > iota((n, n), 0) // z.batch
        relay = relay_ref[...] - jnp.where(later, chosen, 0.0)
        gap = gap_ref[0:1, 0:n]
        for k in range(n):
            gap = gap - gap[:, k : k + 1] * relay[k : k + 1, :]
        shift = jnp.sum(table * gap, axis=1, keepdims=True)
        moved[...] = jnp.broadcast_to(shift, moved.shape)
        high, low = split(gap - lift_ref[...])
        weight[0 : z.members, :] = high
        weight[z.members : 2 * z.members, :] = low

    flat_x = x_ref.reshape(z.members * SUBS, LANES)
    flat_o = out_ref.reshape(z.members * SUBS, LANES)
    both = weight[...]
    high = weight[0 : z.members, :]
    for s in range(0, SUBS, 2):
        k_high, k_low = split(jnp.concatenate([kalman_ref[0, s], kalman_ref[0, s + 1]], axis=1))
        first = dot(both, k_high)
        total = first[0 : z.members] + first[z.members : 2 * z.members] + dot(high, k_low)
        for t in range(2):
            fl = step * z.per_step + (s + t) // z.cells
            off = moved[pl.ds(fl, 1), :] * wet_ref[s + t : s + t + 1, :]
            old = flat_x[pl.ds(s + t, z.members, stride=SUBS), :]
            flat_o[pl.ds(s + t, z.members, stride=SUBS), :] = (
                old + total[:, t * LANES : (t + 1) * LANES] - off
            )


def whole(*shape):
    return pl.BlockSpec(shape, lambda *_: (0,) * len(shape))


def smem():
    return pl.BlockSpec(memory_space=SMEM)


def struct(*shape, dtype=F32):
    return jax.ShapeDtypeStruct(shape, dtype)


def spread_out(tile, axes):
    count = lax.axis_size(axes)
    copies = jnp.broadcast_to(tile[None], (count,) + tile.shape)
    return lax.all_to_all(copies, axes, 0, 0, tiled=True)


def local(ensemble, velocity, diffusivity, land_mask, obs_index, obs_owner, obs_value, obs_error):
    z = Sizes(ensemble, velocity, obs_index)
    axes = ("member", "domain")
    place = jnp.stack([lax.axis_index("member"), lax.axis_index("domain")]).astype(jnp.int32)
    state = ensemble.reshape(z.own, z.states, z.rows, z.cols)
    slab = pl.BlockSpec((z.own, z.per_step, z.rows, z.cols), lambda i: (0, i, 0, 0))
    first, last = pl.pallas_call(
        functools.partial(edges_kernel, z),
        grid=(z.steps,),
        in_specs=[slab],
        out_specs=[whole(z.rows, z.halo)] * 2,
        out_shape=[struct(z.rows, z.halo)] * 2,
        name="edges",
    )(state)
    up = [(i, (i + 1) % z.groups_d) for i in range(z.groups_d)]
    down = [(j, i) for i, j in up]
    before = lax.ppermute(last, "domain", up)
    after = lax.ppermute(first, "domain", down)
    lines = z.states * z.cells
    stepped, own_priors = pl.pallas_call(
        functools.partial(forecast_kernel, z),
        grid=(z.steps,),
        in_specs=[
            smem(),
            smem(),
            smem(),
            smem(),
            slab,
            whole(z.rows, z.halo),
            whole(z.rows, z.halo),
            whole(*velocity.shape),
            whole(*land_mask.shape),
        ],
        out_specs=[pl.BlockSpec(memory_space=pl.ANY), whole(SUBS, LANES)],
        out_shape=[struct(z.members, lines, LANES), struct(SUBS, LANES)],
        scratch_shapes=[
            VMEM((z.members, lines, LANES), F32),
            VMEM((z.packs * SUBS, LANES), F32),
            pltpu.SemaphoreType.DMA((z.steps,)),
        ],
        name="forecast",
    )(place, obs_index, obs_owner, diffusivity, state, before, after, velocity, land_mask)
    current = lax.all_to_all(stepped, "member", 0, 0, tiled=True)
    priors = spread_out(own_priors, axes)
    n = z.obs
    vmem = pl.BlockSpec(memory_space=VMEM)
    gain, cross, lift, tapers, relay, gap, wet = pl.pallas_call(
        functools.partial(filter_kernel, z),
        in_specs=[smem()] * 5 + [vmem, vmem],
        out_specs=[vmem] * 7,
        out_shape=[
            struct(2 * n, z.members, dtype=BF16),
            struct(n, n),
            struct(z.members, n),
            struct(n, SUBS, LANES),
            struct(n, n),
            struct(SUBS, LANES),
            struct(SUBS, LANES),
        ],
        name="filter",
    )(place, obs_index, obs_owner, obs_value, obs_error, priors, land_mask)
    column = pl.BlockSpec((z.members, SUBS, LANES), lambda i: (0, i, 0))
    kalman_spec = pl.BlockSpec((1, SUBS, n, LANES), lambda i: (i, 0, 0, 0))
    kalman, sums = pl.pallas_call(
        functools.partial(gain_kernel, z),
        grid=(z.steps,),
        in_specs=[
            smem(),
            column,
            whole(2 * n, z.members),
            whole(n, SUBS, LANES),
            whole(SUBS, LANES),
        ],
        out_specs=[kalman_spec, whole(z.sum_rows + 1, LANES)],
        out_shape=[struct(z.steps, SUBS, n, LANES), struct(z.sum_rows + 1, LANES)],
        scratch_shapes=[VMEM((SUBS * n, LANES), F32), VMEM((z.sum_rows * LANES, LANES), F32)],
        name="gain",
    )(cross, current, gain, tapers, wet)
    sums = spread_out(sums, axes)
    padded = z.states + -z.states % SUBS
    result = pl.pallas_call(
        functools.partial(update_kernel, z),
        grid=(z.steps,),
        in_specs=[
            smem(),
            column,
            kalman_spec,
            whole(*sums.shape),
            whole(z.members, n),
            whole(n, n),
            whole(SUBS, LANES),
            whole(SUBS, LANES),
        ],
        out_specs=column,
        out_shape=struct(z.members, lines, LANES),
        scratch_shapes=[VMEM((2 * z.members, n), BF16), VMEM((padded, LANES), F32)],
        name="update",
    )(obs_index, current, kalman, sums, lift, relay, gap, wet)
    result = result.reshape(z.members, z.fields, z.levels, z.col_tiles, z.block_rows, LANES)
    result = jnp.swapaxes(result, 3, 4)
    return result.reshape(z.members, z.fields, z.levels, z.block_rows, z.cols)


def solution(mesh):
    in_specs = (
        P("member", None, None, None, "domain"),
        P(None, None, None, "domain"),
        P(),
        P(None, "domain"),
        P(),
        P(),
        P(),
        P(),
    )
    out_specs = P(None, None, None, "member", "domain")
    return jax.shard_map(local, mesh=mesh, in_specs=in_specs, out_specs=out_specs, check_vma=False)
```

time: 1170 us -> 127 us (0.11)
  other arithmetic: 365 us -> 0.58 us
  local copies, waits for them, and re-layouts: 289 us -> 3.25 us
  blocking collectives: 200 us -> 23.6 us
  matrix products: 134 us -> 0 us
  between operations: 120 us -> 0.03 us
  Pallas kernels: 0 us -> 52.2 us
  starting transfers between devices: 22.3 us -> 9.31 us
    add x63 -> x0, other arithmetic: 206 us -> none  [the longest x31 203 us: local(): flat_state = flat_state + weight[:, None] * kalman[None, :]]
    psum x5 -> x0, blocking collectives: 200 us -> none  [the longest x4 161 us: increment_sums(): return lax.psum((local_sum, jnp.sum(wet_cells)), ('member', 'domain'))]
    add x34 -> x0, local copies, waits for them, and re-layouts: 198 us -> none  [local(): flat_state = flat_state + weight[:, None] * kalman[None, :]]
    dot_general x60 -> x0, matrix products: 134 us -> none  [the longest x32 130 us: local(): covariance = jnp.dot(anomaly, flat_state, precision=lax.Precision.HIGHEST)]
    reduce_sum x75 -> x0, other arithmetic: 74.2 us -> none  [the longest x4 31.6 us: increment_sums(): per_cell = jnp.sum(change_flat.reshape(members, levels_total, -1), axis=0)]
    mul x91 -> x0, other arithmetic: 56.4 us -> none  [the longest x56 40.8 us: separation(): return jnp.sqrt((col_gap * col_gap + row_gap * row_gap).astype(jnp.float32))]
    pallas_call x0 -> x5, Pallas kernels: none -> 52.2 us  [the longest x1 12.6 us: local(): pl.pallas_call(functools.partial(update_kernel, z), grid=(z.steps,), in_s...]
    sub x36 -> x0, other arithmetic: 24.2 us -> none  [the longest x1 23.8 us: local(): flat_state.reshape(members, levels_total, -1)]
  transfers between devices with their start and end apart: 3 -> 3, of which waited for: 1 -> 2; matrix products, arithmetic and copies ran while one was open for 7% -> 1% of each run, Pallas kernels for 0% -> 7%
where the time goes in v1:
time: 127 us; the launch traced here: 126 us
  Pallas kernels  52.2 us (41%)
  waiting for transfers between devices  37.1 us (29%)
  blocking collectives  23.6 us (19%)
  starting transfers between devices  9.31 us (7%)
  local copies, waits for them, and re-layouts  3.25 us (3%)
    all_to_all x1, waiting for transfers between devices, local(): current = lax.all_to_all(stepped, 'member', 0, 0, tiled=True)  36.8 us
    all_to_all x2, blocking collectives, spread_out(): return lax.all_to_all(copies, axes, 0, 0, tiled=True)  23.6 us
    pallas_call x1, Pallas kernels, local(): pl.pallas_call(functools.partial(update_kernel, z), grid=(z.steps,), in_s...  12.6 us
    pallas_call x1, Pallas kernels, local(): pl.pallas_call(functools.partial(forecast_kernel, z), grid=(z.steps,), in...  11.9 us
    pallas_call x1, Pallas kernels, local(): pl.pallas_call(functools.partial(gain_kernel, z), grid=(z.steps,), in_spe...  11 us
    pallas_call x1, Pallas kernels, local(): pl.pallas_call(functools.partial(filter_kernel, z), in_specs=[smem()] * 5...  8.58 us
    pallas_call x1, Pallas kernels, local(): pl.pallas_call(functools.partial(edges_kernel, z), grid=(z.steps,), in_sp...  8 us
    all_to_all x1, starting transfers between devices, local(): current = lax.all_to_all(stepped, 'member', 0, 0, tiled=True)  4.79 us
  transfers between devices with their start and end apart: 3, of which 2 were waited for; matrix products, arithmetic and copies ran while one was open for 1% of the time, Pallas kernels for 7%

profile of v1, /device:TPU:0, one launch (start us, length us, event | category | flops | bytes accessed | tf_op | source)
XLA Modules:
  0.0 126.1 jit_solution(3169376303571330905)
XLA Ops:
  0.0 0.0 copy-start.2
  0.0 8.0 %edges.1 = (f32[16,256]{1,0:T(8,128)}, f32[16,256]{1,0:T(8,128)}) custom-call(f32[20,12,16,256]{3,2,1,0:T(8,128)} %bitcast.8), custom_call_target="tpu_custom_call" | custom-call | tf_op jit(solution)/shard_map/edges/pallas_call | solution.py:392
  8.0 0.5 collective-permute-start
  8.5 4.0 %collective-permute-start.1 = (f32[16,256]{1,0:T(8,128)}, f32[16,256]{1,0:T(8,128)S(1)}, u32[]{:S(2)}, u32[]{:S(2)}) collective-permute-start(f32[16,256]{1,0:T(8,128)} %get-tuple-element.19), channel_id=1, source_target_pairs={{1,0},{2,1},{3,2},{4,3},{5,4},{6,5},{7,6},{0,7},{9,8},{10,9},{11,1... | collective-permute-start | bytes 49160 | tf_op jit(solution)/shard_map/ppermute | solution.py:403
  12.5 0.6 pad_add_fusion.place
  13.1 0.0 copy-done.2
  13.1 0.7 copy.11.index
  13.8 0.4 collective-permute-done.before_ref
  14.2 0.0 copy-start
  14.2 0.0 collective-permute-done.1.after_ref
  14.2 0.6 copy-done
  14.8 0.0 copy-start.1
  14.8 0.6 copy-done.1
  15.4 11.9 %forecast.1 = (f32[80,96,128]{2,1,0:T(8,128)}, f32[8,128]{1,0:T(8,128)}) custom-call(s32[2]{0:T(128)} %pad_add_fusion.place, s32[4,8,4]{2,1,0:T(8,128)} %copy.11.index, s32[4]{0:T(128)} %owner.3, f32[4]{0:T(128)} %diff.1, f32[20,12,16,256]{3,2,1,0:T(8,128)} %bitcast.9, f32[16,256]{1,0:T(8,128)} %copy-done, f32[16,256]{1,0:T(8,128)} %copy-done.1, ...), custom_call_target="tpu_custom_call" | custom-call | tf_op jit(solution)/shard_map/forecast/pallas_call | solution.py:405
  27.3 0.7 broadcast_in_dim.4
  28.0 13.8 %all_to_all.15.got_ref = f32[32,8,128]{2,1,0:T(8,128)} all-to-all(f32[32,8,128]{2,1,0:T(8,128)S(1)} %broadcast_in_dim.4), channel_id=1, replica_groups=mesh['member'=4,'domain'=8] {'member','domain'}, dimensions={0} | all-to-all | bytes 262144 | tf_op jit(solution)/shard_map/all_to_all | solution.py:383
  41.8 4.8 %all-to-all-start = ((f32[80,96,128]{2,1,0:T(8,128)}), f32[80,96,128]{2,1,0:T(8,128)}, u32[]{:S(2)}, u32[]{:S(2)}) async-start(f32[80,96,128]{2,1,0:T(8,128)} %get-tuple-element.20), calls=%async_computation | async-start | bytes 7864320 | tf_op jit(solution)/shard_map/all_to_all | solution.py:428
  46.6 8.6 %filter.1 = (bf16[64,80]{1,0:T(8,128)(2,1)}, f32[32,32]{1,0:T(8,128)}, f32[80,32]{1,0:T(8,128)}, f32[32,8,128]{2,1,0:T(8,128)}, f32[32,32]{1,0:T(8,128)}, /*index=5*/f32[8,128]{1,0:T(8,128)}, f32[8,128]{1,0:T(8,128)}) custom-call(s32[2]{0:T(128)} %pad_add_fusion.place, s32[4,8,4]{2,1,0:T(8,128)} %copy.11.index, s32[4]{0:T(128)} %owner.3, f32[4,8]{1,0:T(4,128)} %value.1, ...), custom_call_target="tpu_custom_call" | custom-call | tf_op jit(solution)/shard_map/filter/pallas_call | solution.py:432
  55.2 36.8 %all-to-all-done.x_ref = f32[80,96,128]{2,1,0:T(8,128)} async-done(((f32[80,96,128]{2,1,0:T(8,128)}), f32[80,96,128]{2,1,0:T(8,128)}, u32[]{:S(2)}, u32[]{:S(2)}) %all-to-all-start) | async-done | bytes 3932192 | tf_op jit(solution)/shard_map/all_to_all | solution.py:428
  92.0 11.0 %gain.1 = (f32[12,8,32,128]{3,2,1,0:T(8,128)}, f32[4,128]{1,0:T(4,128)}) custom-call(f32[32,32]{1,0:T(8,128)} %get-tuple-element.22.cross, f32[80,96,128]{2,1,0:T(8,128)} %all-to-all-done.x_ref, bf16[64,80]{1,0:T(8,128)(2,1)} %get-tuple-element.23.gain_ref, f32[32,8,128]{2,1,0:T(8,128)} %get-tuple-element.24.taper_ref, f32[8,128]{1,0:T(8,128)} %get-tuple-element.25.wet_ref), custom_call_target="tpu_custom_call" | custom-call | tf_op jit(solution)/shard_map/gain/pallas_call | solution.py:449
  103.0 0.7 broadcast_in_dim.5
  103.7 9.8 %all_to_all.16.sums_ref = f32[32,4,128]{2,1,0:T(4,128)} all-to-all(f32[32,4,128]{2,1,0:T(4,128)S(1)} %broadcast_in_dim.5), channel_id=1, replica_groups=mesh['member'=4,'domain'=8] {'member','domain'}, dimensions={0} | all-to-all | bytes 131072 | tf_op jit(solution)/shard_map/all_to_all | solution.py:383
  113.4 12.6 %update.1 = f32[80,96,128]{2,1,0:T(8,128)} custom-call(s32[4,8,4]{2,1,0:T(8,128)} %copy.11.index, f32[80,96,128]{2,1,0:T(8,128)} %all-to-all-done.x_ref, f32[12,8,32,128]{3,2,1,0:T(8,128)} %get-tuple-element.26.kalman_ref, f32[32,4,128]{2,1,0:T(4,128)} %all_to_all.16.sums_ref, f32[80,32]{1,0:T(8,128)} %get-tuple-element.28.lift_ref, ...), custom_call_target="tpu_custom_call" | custom-call | tf_op jit(solution)/shard_map/update/pallas_call | solution.py:466
Async XLA Ops:
  0.0 13.1 %copy-start.2 = (s32[4,8,4]{1,2,0:T(4,128)S(1)}, s32[4,8,4]{1,2,0:T(4,128)}, u32[]{:S(2)}) copy-start(s32[4,8,4]{1,2,0:T(4,128)} %param.12) | copy-start | bytes 1540
  8.0 6.1 %collective-permute-start = (f32[16,256]{1,0:T(8,128)}, f32[16,256]{1,0:T(8,128)S(1)}, u32[]{:S(2)}, u32[]{:S(2)}) collective-permute-start(f32[16,256]{1,0:T(8,128)} %get-tuple-element.18), channel_id=1, source_target_pairs={{0,1},{1,2},{2,3},{3,4},{4,5},{5,6},{6,7},{7,0},{8,9},{9,10},{10,1... | collective-permute-start | bytes 49160 | tf_op jit(solution)/shard_map/ppermute | solution.py:402
  8.5 5.7 %collective-permute-start.1 = (f32[16,256]{1,0:T(8,128)}, f32[16,256]{1,0:T(8,128)S(1)}, u32[]{:S(2)}, u32[]{:S(2)}) collective-permute-start(f32[16,256]{1,0:T(8,128)} %get-tuple-element.19), channel_id=1, source_target_pairs={{1,0},{2,1},{3,2},{4,3},{5,4},{6,5},{7,6},{0,7},{9,8},{10,9},{11,1... | collective-permute-start | bytes 49160 | tf_op jit(solution)/shard_map/ppermute | solution.py:403
  14.2 0.6 copy-start
  14.8 0.6 copy-start.1
  41.8 50.1 %all-to-all-start = ((f32[80,96,128]{2,1,0:T(8,128)}), f32[80,96,128]{2,1,0:T(8,128)}, u32[]{:S(2)}, u32[]{:S(2)}) async-start(f32[80,96,128]{2,1,0:T(8,128)} %get-tuple-element.20), calls=%async_computation | async-start | bytes 7864320 | tf_op jit(solution)/shard_map/all_to_all | solution.py:428

commit v2 on v1

v2 whole, which is shorter than its diff:
```python
import functools

import jax
import jax.numpy as jnp
from jax import lax
from jax.experimental import pallas as pl
from jax.experimental.pallas import tpu as pltpu
from jax.sharding import PartitionSpec as P


LOC_RADIUS = 64
LANES = 128
SUBS = 8
F32 = jnp.float32
BF16 = jnp.bfloat16
HIGHEST = lax.Precision.HIGHEST
VMEM = pltpu.VMEM
SMEM = pltpu.SMEM


def gaspari(scaled):
    scaled_safe = jnp.maximum(scaled, 1.0)
    near_part = (
        ((-0.25 * scaled + 0.5) * scaled + 0.625) * scaled - 5.0 / 3.0
    ) * scaled * scaled + 1.0
    far_part = (
        ((((scaled / 12.0 - 0.5) * scaled + 0.625) * scaled + 5.0 / 3.0) * scaled - 5.0) * scaled
        + 4.0
        - 2.0 / (3.0 * scaled_safe)
    )
    return jnp.where(scaled <= 1.0, near_part, jnp.where(scaled < 2.0, far_part, 0.0))


def taper(row_gap, col_gap, grid_width):
    col_gap = jnp.abs(col_gap)
    col_gap = jnp.minimum(col_gap, grid_width - col_gap)
    square = (col_gap * col_gap + row_gap * row_gap).astype(F32)
    return gaspari(jnp.sqrt(square) * (1.0 / LOC_RADIUS))


def iota(shape, dim):
    return lax.broadcasted_iota(jnp.int32, shape, dim)


def split(value):
    high = value.astype(BF16)
    return high, (value - high.astype(F32)).astype(BF16)


def dot(a, b):
    return lax.dot_general(a, b, (((1,), (0,)), ((), ())), preferred_element_type=F32)


def dot_exact(a, b, dims):
    return lax.dot_general(
        a, b, ((dims[:1], dims[1:]), ((), ())), precision=HIGHEST, preferred_element_type=F32
    )


class Sizes:
    def __init__(self, ensemble, obs_index):
        self.own, self.fields, self.levels, self.rows, self.cols = ensemble.shape
        self.states = self.fields * self.levels
        self.groups_m = lax.axis_size("member")
        self.groups_d = lax.axis_size("domain")
        self.members = self.own * self.groups_m
        self.block_rows = self.rows // self.groups_m
        self.col_tiles = self.cols // LANES
        self.cells = self.block_rows * self.col_tiles
        self.per_step = SUBS // self.cells
        self.steps = self.states // self.per_step
        self.width = self.cols * self.groups_d
        self.batches, self.batch = obs_index.shape[:2]
        self.obs = self.batches * self.batch
        self.pack_states = LANES // self.obs
        self.sum_rows = -(-self.states // self.pack_states)
        self.part = next(m for m in (5, 4, 3, 2, 1) if self.own % m == 0)
        self.parts = self.own // self.part
        self.lines = self.states * self.cells
        self.groups = next(g for g in (3, 2, 1) if self.steps % g == 0)
        self.window = -(-self.own // SUBS) * SUBS

    def start(self, p):
        return min(p * self.own, self.members - self.window)


def arrivals(z, step, source, held, sems):
    def copy(at):
        part = pl.ds(at * z.part, z.part)
        return pltpu.make_async_copy(source.at[part], held.at[part], sems.at[at])

    @pl.when(step == 0)
    def _():
        for at in range(z.parts):
            copy(at).start()

    copy(step).wait()


def edges_kernel(z, source, first_ref, last_ref, held, sems):
    step = pl.program_id(0)
    arrivals(z, step, source, held, sems)
    lane = iota((z.rows, LANES), 1)
    first = jnp.zeros((z.rows, LANES), F32)
    last = first
    for m in range(z.part):
        for fl in range(z.states):
            hit = lane == m * z.states + fl
            at = step * z.part + m
            first = jnp.where(hit, held[at, fl, :, 0:1], first)
            last = jnp.where(hit, held[at, fl, :, z.cols - 1 : z.cols], last)
    first_ref[...] = first
    last_ref[...] = last


def forecast_kernel(
    z, group, domain, index, owner, diff, source, before_ref, after_ref, vel_ref, mask_ref,
    out_ref, *refs,
):
    others = refs[: z.groups_m - 1]
    obs_ref, held, state, picked, in_sems, sems = refs[z.groups_m - 1 :]
    step = pl.program_id(0)
    arrivals(z, step, source, held, in_sems)
    shape = (z.rows, z.cols)
    row, col = iota(shape, 0), iota(shape, 1)
    wet = mask_ref[...].astype(F32)
    flat = state.reshape(z.members * z.lines, LANES)
    member = pl.multiple_of(step * (z.part * z.lines), SUBS)
    side = pl.ds(pl.multiple_of(step * LANES, LANES), LANES)
    before = before_ref[:, side]
    after = after_ref[:, side]
    for fl in range(z.states):
        level = fl % z.levels
        spread = diff[fl // z.levels]
        half_u = 0.5 * vel_ref[0, level]
        half_v = 0.5 * vel_ref[1, level]
        center = wet * (1.0 - 4.0 * spread)
        east = wet * (spread - half_u)
        west = wet * (spread + half_u)
        north = jnp.where(row == z.rows - 1, 0.0, wet * (spread - half_v))
        south = jnp.where(row == 0, 0.0, wet * (spread + half_v))
        for m in range(z.part):
            x = held[step * z.part + m, fl]
            at = m * z.states + fl
            nxt = jnp.where(col == z.cols - 1, after[:, at : at + 1], pltpu.roll(x, z.cols - 1, 1))
            prv = jnp.where(col == 0, before[:, at : at + 1], pltpu.roll(x, 1, 1))
            y = (
                center * x
                + east * nxt
                + west * prv
                + north * pltpu.roll(x, z.rows - 1, 0)
                + south * pltpu.roll(x, 1, 0)
            )
            for p in range(z.groups_m):
                for c in range(z.col_tiles):
                    line = (p * z.own + m) * z.lines + fl * z.cells + c * z.block_rows
                    flat[pl.ds(member + line, z.block_rows), :] = y[
                        p * z.block_rows : (p + 1) * z.block_rows, c * LANES : (c + 1) * LANES
                    ]

    def copies(at):
        part = pl.ds(at * z.part, z.part)
        yield pltpu.make_async_copy(state.at[:, part], out_ref.at[:, part], sems.at[0, at])
        for x, other in enumerate(others, 1):
            p = jnp.bitwise_xor(group[0], x)
            yield pltpu.make_async_copy(state.at[p, part], other.at[part], sems.at[x, at])

    for copy in copies(step):
        copy.start()

    @pl.when(step == z.parts - 1)
    def _():
        picked[...] = jnp.zeros_like(picked)
        lane = iota((z.own, LANES), 1)

        def pick(k, carry):
            b, i = k // z.batch, lax.rem(k, z.batch)

            @pl.when(lax.rem(owner[b], z.groups_d) == domain[0])
            def _():
                fl = index[b, 0, i] * z.levels + index[b, 1, i]
                at = index[b, 3, i]
                cell = (at // LANES) * z.block_rows + index[b, 2, i]
                base = (owner[b] // z.groups_d) * z.own * z.lines + fl * z.cells + cell
                got = flat[pl.ds(base, z.own, stride=z.lines), :]
                got = jnp.where(lane == lax.rem(at, LANES), got, 0.0)
                got = jnp.sum(got, axis=1, keepdims=True)
                picked[0 : z.own, :] = jnp.where(lane == k, got, picked[0 : z.own, :])

            return carry

        lax.fori_loop(0, z.obs, pick, 0)
        total = picked[0:SUBS, :]
        for v in range(1, z.window // SUBS):
            total = total + pltpu.roll(picked[v * SUBS : (v + 1) * SUBS, :], v * z.obs, 1)
        obs_ref[...] = total

        def drain(at, carry):
            for copy in copies(at):
                copy.wait()
            return carry

        lax.fori_loop(0, z.parts, drain, 0)


def filter_kernel(
    z, domain, index, owner, value, error, got_ref, mask_ref,
    gain_ref, part_ref, cross_ref, flag, lift_ref, taper_ref, relay_ref, gap_ref, wet_ref,
):
    n = z.obs
    eight = z.groups_m * SUBS
    stacked = []
    for x in range(z.groups_m):
        total = got_ref[0, x]
        for d in range(1, z.groups_d):
            total = total + got_ref[d, x]
        stacked.append(total)
    stacked = jnp.concatenate(stacked, axis=0)
    square = (n, LANES)
    prior = jnp.zeros(square, F32)
    row, lane = iota(square, 0), iota(square, 1)
    for v in range(z.window // SUBS):
        pick = (lane == row + v * n).astype(F32)
        part = dot_exact(pick, stacked, (1, 1))
        src = iota((eight, LANES), 0)
        dst = iota((eight, LANES), 1)
        slot = v * SUBS + src % SUBS
        place_of = jnp.where(slot < z.own, (src // SUBS) * z.own + slot, -1)
        prior = prior + dot_exact(part, (dst == place_of).astype(F32), (1, 0))
    ones = jnp.full((SUBS, LANES), 1.0 / z.members, F32)
    mean_row = dot_exact(ones, prior, (1, 1))
    mean = jnp.sum(prior, axis=1, keepdims=True) * (1.0 / z.members)
    anomaly = jnp.where(lane < z.members, prior - mean, 0.0)
    rows_s, cols_s = jnp.zeros(square, jnp.int32), jnp.zeros(square, jnp.int32)
    rows_l, cols_l = rows_s, cols_s
    values = jnp.zeros((SUBS, n), F32)
    value_lane = iota((SUBS, n), 1)
    shape = (SUBS, LANES)
    sub = iota(shape, 0) % z.cells
    cell_row = sub % z.block_rows
    first_col = domain[0] * z.cols
    cell_col = first_col + (sub // z.block_rows) * LANES + iota(shape, 1)
    wets = []
    for p in range(z.groups_m):
        wet = jnp.zeros(shape, F32)
        for c in range(z.col_tiles):
            for r in range(z.block_rows):
                full_row = p * z.block_rows + r
                line = mask_ref[full_row : full_row + 1, c * LANES : (c + 1) * LANES]
                wet = jnp.where(sub == c * z.block_rows + r, line.astype(F32), wet)
        wet_ref[p] = wet
        wets.append(wet)
    for b in range(z.batches):
        near = jnp.int32(0)
        tile = lax.rem(owner[b], z.groups_d) * z.cols
        first_row = owner[b] // z.groups_d * z.block_rows
        for i in range(z.batch):
            k = b * z.batch + i
            at_row = first_row + index[b, 2, i]
            at_col = tile + index[b, 3, i]
            rows_s = jnp.where(row == k, at_row, rows_s)
            cols_s = jnp.where(row == k, at_col, cols_s)
            rows_l = jnp.where(lane == k, at_row, rows_l)
            cols_l = jnp.where(lane == k, at_col, cols_l)
            values = jnp.where(value_lane == k, value[b, i], values)
            ahead = lax.rem(at_col - first_col + z.width, z.width)
            behind = z.width - ahead
            reach = 2 * LOC_RADIUS
            close = (ahead < z.cols + reach) | (behind < reach)
            near = jnp.where(close, 1, near)
        flag[b] = near

        @pl.when(near > 0)
        def _():
            for i in range(z.batch):
                k = b * z.batch + i
                at_row = first_row + index[b, 2, i]
                at_col = tile + index[b, 3, i]
                for p in range(z.groups_m):
                    rho = taper(cell_row + (p * z.block_rows - at_row), cell_col - at_col, z.width)
                    taper_ref[p, k] = wets[p] * rho

    gap_ref[...] = jnp.zeros_like(gap_ref)
    gap_ref[:, 0:n] = values - mean_row
    mutual = taper(rows_s - rows_l, cols_s - cols_l, z.width)
    relay = jnp.zeros(square, F32)
    inverse_l = jnp.zeros(square, F32)
    inverse_s = jnp.zeros(square, F32)
    shrink_s = jnp.zeros(square, F32)
    spread = float(z.members - 1)
    for k in range(n):
        b, i = divmod(k, z.batch)
        own = anomaly[k : k + 1, :]
        product = jnp.sum(anomaly * own, axis=1, keepdims=True)
        variance = product[k : k + 1, :] * (1.0 / spread) + error[b, i]
        inverse = 1.0 / (spread * variance)
        shrink = 1.0 / (1.0 + jnp.sqrt(error[b, i] / variance))
        ratio = jnp.where(row[:, 0:1] > k, mutual[:, k : k + 1] * product * inverse, 0.0)
        anomaly = anomaly - (shrink * ratio) * own
        relay = jnp.where(lane == k, ratio, relay)
        inverse_l = jnp.where(lane == k, inverse, inverse_l)
        inverse_s = jnp.where(row == k, inverse, inverse_s)
        shrink_s = jnp.where(row == k, shrink, shrink_s)
    gram = dot_exact(anomaly, anomaly, (1, 1))
    cross_ref[...] = -shrink_s[:, 0:n] * inverse_l[:, 0:n] * gram
    high, low = split(anomaly * inverse_s)

    def tripled(count, offset, width):
        shape = (LANES, 3 * width)
        src, dst = iota(shape, 0), iota(shape, 1)
        third, slot = dst // width, dst % width - offset
        hit = (src == slot) & (slot >= 0) & (slot < count)
        upper = (hit & (third < 2)).astype(BF16)
        lower = (hit & (third == 2)).astype(BF16)
        return (dot(high, upper) + dot(low, lower)).astype(BF16)

    gain_ref[...] = tripled(z.members, 0, z.members)
    made = {}
    for p in range(z.groups_m):
        offset = p * z.own - z.start(p)
        if offset not in made:
            made[offset] = tripled(z.own, offset, z.window)
        part_ref[p] = made[offset]
    eye = (iota((z.members, LANES), 0) == iota((z.members, LANES), 1)).astype(F32)
    lift_ref[...] = dot_exact(eye, shrink_s * anomaly, (1, 1))
    eye = (iota((n, LANES), 0) == iota((n, LANES), 1)).astype(F32)
    relay_ref[...] = dot_exact(eye, relay, (1, 1))


def stacked_rows(flat, first, count, lines):
    x = [flat[pl.ds(first + t, count, stride=lines), :] for t in range(2)]
    x = jnp.concatenate(x, axis=1)
    high = x.astype(BF16).astype(F32)
    return jnp.concatenate([high, x - high, high], axis=0).astype(BF16)


def solve_gains(z, flag, cross, taper_of, work, gains):
    n, size = z.obs, z.batch
    every = range(z.groups)

    for b in range(z.batches):

        @pl.when(flag[b] > 0)
        def _():
            part = [
                [work[pl.ds(g * SUBS * n + b * size + i, SUBS, stride=n), :] for g in every]
                for i in range(size)
            ]
            for before in range(b):

                def add(part):
                    part = [list(each) for each in part]
                    for j in range(before * size, (before + 1) * size):
                        held = [gains[g * n + j] for g in every]
                        for i in range(size):
                            factor = cross[j, b * size + i]
                            for g in every:
                                part[i][g] = part[i][g] + factor * held[g]
                    return part

                part = lax.cond(flag[before] > 0, add, lambda part: part, part)
            for i in range(size):
                k = b * size + i
                rho = taper_of(k)
                for g in every:
                    kalman = rho * part[i][g]
                    gains[g * n + k] = kalman
                    for j in range(i + 1, size):
                        part[j][g] = part[j][g] + cross[k, b * size + j] * kalman

        @pl.when(flag[b] == 0)
        def _():
            for i in range(size):
                for g in every:
                    gains[g * n + b * size + i] = jnp.zeros((SUBS, LANES), F32)


def sums_kernel(
    z, group, cross, flag, x_ref, part_ref, taper_ref, wet_ref, sums_ref, work, gains, total, held
):
    n = z.obs
    step = pl.program_id(0)
    lines = z.groups * SUBS
    flat = x_ref.reshape(z.members * lines, LANES)
    total[...] = jnp.zeros_like(total)
    every = range(z.groups)

    for p in range(z.groups_m):
        for g in every:
            for s in range(0, SUBS, 2):
                x = stacked_rows(flat, z.start(p) * lines + g * SUBS + s, z.window, lines)
                got = dot(part_ref[p], x)
                at = (g * SUBS + s) * n
                work[at : at + n, :] = got[:, 0:LANES]
                work[at + n : at + 2 * n, :] = got[:, LANES : 2 * LANES]
        solve_gains(z, flag, cross, lambda k: taper_ref[p, k], work, gains)
        for g in every:
            for k in range(n):
                total[g * n + k] = total[g * n + k] + gains[g * n + k]
    for g in every:
        for k in range(n):
            work[pl.ds(g * SUBS * n + k, SUBS, stride=n), :] = total[g * n + k]
        for q in range(z.per_step):
            first = g * SUBS + q * z.cells
            each = work[first * n : (first + 1) * n, :]
            for s in range(first + 1, first + z.cells):
                each = each + work[s * n : (s + 1) * n, :]
            fl = (step * z.groups + g) * z.per_step + q
            held[pl.ds(pl.multiple_of(fl * n, n), n), :] = each

    @pl.when(step == z.steps // z.groups - 1)
    def _():
        ones = jnp.ones((SUBS, LANES), F32)
        wet = jnp.sum(wet_ref[group[0]][0 : z.cells, :], axis=0, keepdims=True)
        rows = [
            dot_exact(ones, held[i * LANES : (i + 1) * LANES, :], (1, 1))[0:1, :]
            for i in range(z.sum_rows)
        ]
        rows.append(wet)
        for d in range(z.groups_d):
            for i, line in enumerate(rows):
                sums_ref[d, i : i + 1, :] = line


def weights_kernel(z, index, *refs):
    lift_ref, relay_ref, gap_ref, weight_ref, shift_ref = refs[z.groups_m :]
    n = z.obs
    sums = sum(ref[d] for ref in refs[: z.groups_m] for d in range(z.groups_d))
    count = jnp.sum(sums[z.sum_rows : z.sum_rows + 1, :], axis=1, keepdims=True)
    lines = []
    for fl in range(z.states):
        i, c = divmod(fl, z.pack_states)
        lines.append(sums[i : i + 1, c * n : (c + 1) * n])
    pad = -z.states % SUBS
    table = jnp.concatenate(lines + [jnp.zeros((pad, n), F32)], axis=0) / count
    eye = (iota((n, n), 0) == iota((n, n), 1)).astype(F32)
    turned = dot_exact(eye, table, (1, 1))
    shape = (z.states + pad, n)
    fl_row, lane = iota(shape, 0), iota(shape, 1)
    at = jnp.zeros(shape, jnp.int32)
    for k in range(n):
        b, i = divmod(k, z.batch)
        at = jnp.where(lane == k, index[b, 0, i] * z.levels + index[b, 1, i], at)
    chosen = dot_exact(turned, (fl_row == at).astype(F32), (1, 0))
    later = iota((n, n), 1) // z.batch > iota((n, n), 0) // z.batch
    relay = relay_ref[...] - jnp.where(later, chosen, 0.0)
    gap = gap_ref[0:1, 0:n]
    for k in range(n):
        gap = gap - gap[:, k : k + 1] * relay[k : k + 1, :]
    shift = jnp.sum(table * gap, axis=1, keepdims=True)
    shift_ref[...] = jnp.broadcast_to(shift, shift_ref.shape)
    high, low = split(gap - lift_ref[...])
    src, dst = iota((n, 3 * n), 0), iota((n, 3 * n), 1)
    hit = src == dst % n
    upper = (hit & (dst < 2 * n)).astype(BF16)
    lower = (hit & (dst >= 2 * n)).astype(BF16)
    weight_ref[...] = (dot(high, upper) + dot(low, lower)).astype(BF16)


def update_kernel(z, group, cross, flag, *refs):
    n = z.obs
    slabs = refs[: z.groups_m]
    gain_ref, taper_ref, wet_ref, weight_ref, shift_ref, out_ref = refs[z.groups_m : -6]
    got, made, work, gains, in_sems, out_sems = refs[-6:]
    chunk = z.groups * SUBS
    flat_x = got.reshape(z.members * z.lines, LANES)
    flat_o = made.reshape(z.members * z.lines, LANES)
    size = z.members * chunk
    every = range(z.groups)

    def lines(at):
        return pl.ds(pl.multiple_of(at * chunk, SUBS), chunk)

    def loads(at):
        for x, slab in enumerate(slabs):
            src = slab.at[group[0]] if x == 0 else slab
            here = got.at[at, x * z.own : (x + 1) * z.own]
            yield pltpu.make_async_copy(src.at[:, lines(at)], here, in_sems.at[x, at])

    def stores(at):
        for x in range(z.groups_m):
            first = jnp.bitwise_xor(group[0], x) * z.own
            here = made.at[at, x * z.own : (x + 1) * z.own]
            there = out_ref.at[pl.ds(first, z.own), lines(at)]
            yield pltpu.make_async_copy(here, there, out_sems.at[x, at])

    count = z.steps // z.groups
    for at in range(count):
        for copy in loads(at):
            copy.start()
    wet = wet_ref[group[0]]

    def advance(at, carry):
        for copy in loads(at):
            copy.wait()
        base = pl.multiple_of(at * size, SUBS)
        for g in every:
            for s in range(0, SUBS, 2):
                x = stacked_rows(flat_x, base + g * SUBS + s, z.members, chunk)
                new = dot(gain_ref[...], x)
                line = (g * SUBS + s) * n
                work[line : line + n, :] = new[:, 0:LANES]
                work[line + n : line + 2 * n, :] = new[:, LANES : 2 * LANES]
        solve_gains(z, flag, cross, lambda k: taper_ref[group[0], k], work, gains)
        for g in every:
            for k in range(n):
                work[pl.ds(g * SUBS * n + k, SUBS, stride=n), :] = gains[g * n + k]
            for s in range(0, SUBS, 2):
                line = (g * SUBS + s) * n
                k = [work[line : line + n, :], work[line + n : line + 2 * n, :]]
                k = jnp.concatenate(k, axis=1)
                high = k.astype(BF16)
                low = (k - high.astype(F32)).astype(BF16)
                total = dot(weight_ref[...], jnp.concatenate([high, low, high], axis=0))
                for t in range(2):
                    fl = (at * z.groups + g) * z.per_step + (s + t) // z.cells
                    off = shift_ref[pl.ds(fl, 1), :] * wet[s + t : s + t + 1, :]
                    rows = pl.ds(base + g * SUBS + s + t, z.members, stride=chunk)
                    flat_o[rows, :] = flat_x[rows, :] + (total[:, t * LANES : (t + 1) * LANES] - off)
        for copy in stores(at):
            copy.start()
        return carry

    lax.fori_loop(0, count, advance, 0)

    def drain(at, carry):
        for copy in stores(at):
            copy.wait()
        return carry

    lax.fori_loop(0, count, drain, 0)


def whole(*shape):
    return pl.BlockSpec(shape, lambda *_: (0,) * len(shape))


def smem():
    return pl.BlockSpec(memory_space=SMEM)


def struct(*shape, dtype=F32):
    return jax.ShapeDtypeStruct(shape, dtype)


def grant(mebibytes):
    return pltpu.CompilerParams(vmem_limit_bytes=mebibytes << 20)


def exchange(copies):
    return lax.all_to_all(copies, "domain", 0, 0, tiled=True)


def swap(z, array, x):
    return lax.ppermute(array, "member", [(p, p ^ x) for p in range(z.groups_m)])


def local(ensemble, velocity, diffusivity, land_mask, obs_index, obs_owner, obs_value, obs_error):
    z = Sizes(ensemble, obs_index)
    group = lax.axis_index("member").reshape(1)
    domain = lax.axis_index("domain").reshape(1)
    index = jnp.swapaxes(obs_index, 1, 2)
    state = ensemble.reshape(z.own, z.states, z.rows, z.cols)
    slab = pl.BlockSpec(memory_space=pltpu.HBM)
    held = [VMEM(state.shape, F32)]
    arrived = [pltpu.SemaphoreType.DMA((z.parts,))]
    side = pl.BlockSpec((z.rows, LANES), lambda i: (0, i))
    halo = z.parts * LANES
    first, last = pl.pallas_call(
        functools.partial(edges_kernel, z),
        grid=(z.parts,),
        in_specs=[slab],
        out_specs=[side] * 2,
        out_shape=[struct(z.rows, halo)] * 2,
        scratch_shapes=held + arrived,
        name="edges",
        compiler_params=grant(8),
    )(state)
    up = [(i, (i + 1) % z.groups_d) for i in range(z.groups_d)]
    down = [(j, i) for i, j in up]
    before = lax.ppermute(last, "domain", up)
    after = lax.ppermute(first, "domain", down)
    hbm = pl.BlockSpec(memory_space=pl.ANY)
    slots = range(1, z.groups_m)
    stepped, *moved, own_priors = pl.pallas_call(
        functools.partial(forecast_kernel, z),
        grid=(z.parts,),
        in_specs=[smem()] * 5
        + [
            slab,
            whole(z.rows, halo),
            whole(z.rows, halo),
            whole(*velocity.shape),
            whole(*land_mask.shape),
        ],
        out_specs=[hbm] * z.groups_m + [whole(SUBS, LANES)],
        out_shape=[struct(z.groups_m, z.own, z.lines, LANES)]
        + [struct(z.own, z.lines, LANES) for _ in slots]
        + [struct(SUBS, LANES)],
        scratch_shapes=held
        + [
            VMEM((z.groups_m, z.own, z.lines, LANES), F32),
            VMEM((z.window, LANES), F32),
            arrived[0],
            pltpu.SemaphoreType.DMA((z.groups_m, z.parts)),
        ],
        name="forecast",
        compiler_params=grant(16),
    )(group, domain, index, obs_owner, diffusivity, state, before, after, velocity, land_mask)
    priors = [own_priors] + [swap(z, own_priors, x) for x in slots]
    moved = [swap(z, slab, x) for x, slab in zip(slots, moved)]
    priors = jnp.broadcast_to(jnp.stack(priors)[None], (z.groups_d, z.groups_m, SUBS, LANES))
    priors = exchange(priors)
    n = z.obs
    vmem = pl.BlockSpec(memory_space=VMEM)
    gain, part, cross, flag, lift, tapers, relay, gap, wet = pl.pallas_call(
        functools.partial(filter_kernel, z),
        in_specs=[smem()] * 5 + [vmem, vmem],
        out_specs=[vmem] * 3 + [smem()] + [vmem] * 5,
        out_shape=[
            struct(n, 3 * z.members, dtype=BF16),
            struct(z.groups_m, n, 3 * z.window, dtype=BF16),
            struct(n, n),
            struct(z.batches, dtype=jnp.int32),
            struct(z.members, n),
            struct(z.groups_m, n, SUBS, LANES),
            struct(n, n),
            struct(SUBS, LANES),
            struct(z.groups_m, SUBS, LANES),
        ],
        name="filter",
        compiler_params=grant(8),
    )(domain, index, obs_owner, obs_value, obs_error, priors, land_mask)
    lines = z.groups * SUBS
    column = pl.BlockSpec((z.members, lines, LANES), lambda i: (0, i, 0))
    grid = (z.steps // z.groups,)
    work = VMEM((z.groups * SUBS * n, LANES), F32)
    gains = VMEM((z.groups * n, SUBS, LANES), F32)
    sums = pl.pallas_call(
        functools.partial(sums_kernel, z),
        grid=grid,
        in_specs=[
            smem(),
            smem(),
            smem(),
            column,
            whole(*part.shape),
            whole(*tapers.shape),
            whole(*wet.shape),
        ],
        out_specs=whole(z.groups_d, z.sum_rows + 1, LANES),
        out_shape=struct(z.groups_d, z.sum_rows + 1, LANES),
        scratch_shapes=[work, gains, gains, VMEM((z.sum_rows * LANES, LANES), F32)],
        name="sums",
        compiler_params=grant(12),
    )(group, cross, flag, stepped.reshape(z.members, z.lines, LANES), part, tapers, wet)
    sums = exchange(sums)
    sums = [sums] + [swap(z, sums, x) for x in slots]
    padded = z.states + -z.states % SUBS
    weight, shift = pl.pallas_call(
        functools.partial(weights_kernel, z),
        in_specs=[smem()] + [vmem] * (z.groups_m + 3),
        out_specs=[vmem] * 2,
        out_shape=[struct(z.members, 3 * n, dtype=BF16), struct(padded, LANES)],
        name="weights",
        compiler_params=grant(8),
    )(index, *sums, lift, relay, gap)
    sems = pltpu.SemaphoreType.DMA((z.groups_m, z.steps // z.groups))
    result = pl.pallas_call(
        functools.partial(update_kernel, z),
        in_specs=[smem()] * 3 + [hbm] * z.groups_m + [vmem] * 5,
        out_specs=hbm,
        out_shape=struct(z.members, z.lines, LANES),
        scratch_shapes=[VMEM((z.steps // z.groups, z.members, lines, LANES), F32)] * 2
        + [work, gains, sems, sems],
        name="update",
        compiler_params=grant(20),
    )(group, cross, flag, stepped, *moved, gain, tapers, wet, weight, shift)
    result = result.reshape(z.members, z.fields, z.levels, z.col_tiles, z.block_rows, LANES)
    result = jnp.swapaxes(result, 3, 4)
    return result.reshape(z.members, z.fields, z.levels, z.block_rows, z.cols)


def solution(mesh):
    in_specs = (
        P("member", None, None, None, "domain"),
        P(None, None, None, "domain"),
        P(),
        P(None, "domain"),
        P(),
        P(),
        P(),
        P(),
    )
    out_specs = P(None, None, None, "member", "domain")
    return jax.shard_map(local, mesh=mesh, in_specs=in_specs, out_specs=out_specs, check_vma=False)
```

time: 127 us -> 138 us (1.087)
  waiting for transfers between devices: 37.1 us -> 47.5 us
  starting transfers between devices: 9.31 us -> 17.2 us
  blocking collectives: 23.6 us -> 17.2 us
  Pallas kernels: 52.2 us -> 50.8 us
    ppermute x0 -> x9, waiting for transfers between devices: none -> 45.9 us  [swap(): lax.ppermute(array, 'member', [(p, p ^ x) for p in range(z.groups_m)])]
    all_to_all x1 -> x0, waiting for transfers between devices: 36.8 us -> none  [local(): current = lax.all_to_all(stepped, 'member', 0, 0, tiled=True)]
    ppermute x0 -> x9, starting transfers between devices: none -> 12.6 us  [swap(): lax.ppermute(array, 'member', [(p, p ^ x) for p in range(z.groups_m)])]
    all_to_all x2, blocking collectives: 23.6 us -> 17.2 us  [exchange(): return lax.all_to_all(copies, 'domain', 0, 0, tiled=True)]
    all_to_all x1 -> x0, starting transfers between devices: 4.79 us -> none  [local(): current = lax.all_to_all(stepped, 'member', 0, 0, tiled=True)]
    unnamed x7 -> x18, local copies, waits for them, and re-layouts: 1.88 us -> 4.27 us
    pallas_call x4 -> x5, Pallas kernels: 43.6 us -> 42.3 us  [the longest x1 14.8 us: local(): pl.pallas_call(functools.partial(sums_kernel, z), grid=grid, in_specs=[sm...]
  transfers between devices with their start and end apart: 3 -> 11, of which waited for: 2 -> 6; matrix products, arithmetic and copies ran while one was open for 1% -> 0% of each run, Pallas kernels for 7% -> 19%
where the time goes in v2:
time: 138 us; the launch traced here: 137 us
  Pallas kernels  50.8 us (37%)
  waiting for transfers between devices  47.5 us (34%)
  starting transfers between devices  17.2 us (12%)
  blocking collectives  17.2 us (12%)
  local copies, waits for them, and re-layouts  4.29 us (3%)
    ppermute x9, waiting for transfers between devices, swap(): lax.ppermute(array, 'member', [(p, p ^ x) for p in range(z.groups_m)])  45.9 us
    all_to_all x2, blocking collectives, exchange(): return lax.all_to_all(copies, 'domain', 0, 0, tiled=True)  17.2 us
    pallas_call x1, Pallas kernels, local(): pl.pallas_call(functools.partial(sums_kernel, z), grid=grid, in_specs=[sm...  14.8 us
    ppermute x9, starting transfers between devices, swap(): lax.ppermute(array, 'member', [(p, p ^ x) for p in range(z.groups_m)])  12.6 us
    pallas_call x1, Pallas kernels, local(): pl.pallas_call(functools.partial(forecast_kernel, z), grid=(z.parts,), in...  12.3 us
    pallas_call x1, Pallas kernels, local(): pl.pallas_call(functools.partial(update_kernel, z), in_specs=[smem()] * 3...  8.66 us
    pallas_call x1, Pallas kernels, local(): pl.pallas_call(functools.partial(filter_kernel, z), in_specs=[smem()] * 5...  8.5 us
    unnamed x18, local copies, waits for them, and re-layouts  4.27 us
  transfers between devices with their start and end apart: 11, of which 6 were waited for; matrix products, arithmetic and copies ran while one was open for 0% of the time, Pallas kernels for 19%

profile of v2, /device:TPU:0, one launch (start us, length us, event | category | flops | bytes accessed | tf_op | source)
XLA Modules:
  0.0 137.3 jit_solution(7598155345980717747)
XLA Ops:
  0.0 0.0 copy-start.7
  0.0 0.0 copy-start.8
  0.0 0.0 copy-start
  0.0 2.1 %copy-done = f32[20,4,3,16,256]{4,3,2,1,0:T(8,128)S(1)} copy-done((f32[20,4,3,16,256]{4,3,2,1,0:T(8,128)S(1)}, f32[20,4,3,16,256]{4,3,2,1,0:T(8,128)}, u32[]{:S(2)}) %copy-start) | copy-done | bytes 3932184
  2.1 0.0 copy-start.2
  2.1 0.0 copy-start.3
  2.1 0.0 copy-start.4
  2.2 0.0 copy-start.5
  2.2 0.0 copy-start.6
  2.2 3.1 %edges.1 = (f32[16,512]{1,0:T(8,128)S(1)}, f32[16,512]{1,0:T(8,128)S(1)}) custom-call(f32[20,12,16,256]{3,2,1,0:T(8,128)S(1)} %bitcast.14), custom_call_target="tpu_custom_call" | custom-call | tf_op jit(solution)/shard_map/edges/pallas_call | solution.py:569
  5.3 0.5 collective-permute-start
  5.8 4.1 %collective-permute-start.1 = (f32[16,512]{1,0:T(8,128)S(1)}, f32[16,512]{1,0:T(8,128)S(1)}, u32[]{:S(2)}, u32[]{:S(2)}) collective-permute-start(f32[16,512]{1,0:T(8,128)S(1)} %get-tuple-element.24), channel_id=1, source_target_pairs={{1,0},{2,1},{3,2},{4,3},{5,4},{6,5},{7,6},{0,7},{9,8},{10,9},{11,1... | collective-permute-start | bytes 98312 | tf_op jit(solution)/shard_map/ppermute | solution.py:582
  9.9 1.5 %collective-permute-done.before_ref = f32[16,512]{1,0:T(8,128)S(1)} collective-permute-done((f32[16,512]{1,0:T(8,128)S(1)}, f32[16,512]{1,0:T(8,128)S(1)}, u32[]{:S(2)}, u32[]{:S(2)}) %collective-permute-start) | collective-permute-done | bytes 32800 | tf_op jit(solution)/shard_map/ppermute | solution.py:581
  11.4 0.1 collective-permute-done.1.after_ref
  11.5 0.0 copy-done.7
  11.5 0.0 copy-done.8
  11.5 0.0 copy-done.2
  11.5 0.0 copy-done.3
  11.5 0.0 copy-done.4
  11.5 0.0 copy-start.1
  11.5 2.1 %copy-done.1 = f32[20,4,3,16,256]{4,3,2,1,0:T(8,128)S(1)} copy-done((f32[20,4,3,16,256]{4,3,2,1,0:T(8,128)S(1)}, f32[20,4,3,16,256]{4,3,2,1,0:T(8,128)}, u32[]{:S(2)}) %copy-start.1) | copy-done | bytes 3932184
  13.7 12.3 %forecast.1 = (f32[4,20,96,128]{3,2,1,0:T(8,128)S(1)}, f32[20,96,128]{2,1,0:T(8,128)S(1)}, f32[20,96,128]{2,1,0:T(8,128)S(1)}, f32[20,96,128]{2,1,0:T(8,128)S(1)}, f32[8,128]{1,0:T(8,128)S(1)}) custom-call(s32[1]{0:T(128)} %bitcast.group, s32[1]{0:T(128)} %bitcast.1.domain, s32[4,4,8]{2,1,0:T(4,128)S(1)} %bitcast.17, s32[4]{0:T(128)S(1)} %copy-done.7, ...), custom_call_target="tpu_custom_call" | custom-call | tf_op jit(solution)/shard_map/forecast/pallas_call | solution.py:585
  26.0 2.0 %collective-permute-start.5 = (f32[20,96,128]{2,1,0:T(8,128)S(1)}, f32[20,96,128]{2,1,0:T(8,128)S(1)}, u32[]{:S(2)}, u32[]{:S(2)}) collective-permute-start(f32[20,96,128]{2,1,0:T(8,128)S(1)} %get-tuple-element.29), channel_id=1, source_target_pairs={{0,8},{8,0},{16,24},{24,16},{1,9},{9,1},{17,25},{25,17},{2,10},{10... | collective-permute-start | bytes 2949128 | tf_op jit(solution)/shard_map/ppermute | solution.py:555
  28.0 1.5 %collective-permute-start.6 = (f32[20,96,128]{2,1,0:T(8,128)S(1)}, f32[20,96,128]{2,1,0:T(8,128)S(1)}, u32[]{:S(2)}, u32[]{:S(2)}) collective-permute-start(f32[20,96,128]{2,1,0:T(8,128)S(1)} %get-tuple-element.30), channel_id=1, source_target_pairs={{0,16},{8,24},{16,0},{24,8},{1,17},{9,25},{17,1},{25,9},{2,18},{10... | collective-permute-start | bytes 2949128 | tf_op jit(solution)/shard_map/ppermute | solution.py:555
  29.5 0.0 collective-permute-start.7
  29.5 2.9 %collective-permute-start.4 = (f32[8,128]{1,0:T(8,128)S(1)}, f32[8,128]{1,0:T(8,128)S(1)}, u32[]{:S(2)}, u32[]{:S(2)}) collective-permute-start(f32[8,128]{1,0:T(8,128)S(1)} %get-tuple-element.25), channel_id=1, source_target_pairs={{0,24},{8,16},{16,8},{24,0},{1,25},{9,17},{17,9},{25,1},{2,26},{10... | collective-permute-start | bytes 12296 | tf_op jit(solution)/shard_map/ppermute | solution.py:555
  32.4 0.5 collective-permute-start.3
  33.0 39.6 %collective-permute-done.4 = f32[8,128]{1,0:T(8,128)S(1)} collective-permute-done((f32[8,128]{1,0:T(8,128)S(1)}, f32[8,128]{1,0:T(8,128)S(1)}, u32[]{:S(2)}, u32[]{:S(2)}) %collective-permute-start.4) | collective-permute-done | bytes 4128 | tf_op jit(solution)/shard_map/ppermute | solution.py:555
  72.5 1.4 %collective-permute-start.2 = (f32[8,128]{1,0:T(8,128)S(1)}, f32[8,128]{1,0:T(8,128)S(1)}, u32[]{:S(2)}, u32[]{:S(2)}) collective-permute-start(f32[8,128]{1,0:T(8,128)S(1)} %get-tuple-element.25), channel_id=1, source_target_pairs={{0,8},{8,0},{16,24},{24,16},{1,9},{9,1},{17,25},{25,17},{2,10},{10... | collective-permute-start | bytes 12296 | tf_op jit(solution)/shard_map/ppermute | solution.py:555
  73.9 0.0 collective-permute-done.3
  73.9 2.2 %collective-permute-done.2 = f32[8,128]{1,0:T(8,128)S(1)} collective-permute-done((f32[8,128]{1,0:T(8,128)S(1)}, f32[8,128]{1,0:T(8,128)S(1)}, u32[]{:S(2)}, u32[]{:S(2)}) %collective-permute-start.2) | collective-permute-done | bytes 4128 | tf_op jit(solution)/shard_map/ppermute | solution.py:555
  76.1 9.1 %all_to_all.10.got_ref = f32[8,4,8,128]{3,2,1,0:T(8,128)S(1)} all-to-all(f32[8,4,8,128]{3,2,1,0:T(8,128)S(1)} %broadcast_in_dim.2), channel_id=1, replica_groups=mesh['member'=4,'domain'=8] {'domain'}, dimensions={0} | all-to-all | bytes 262144 | tf_op jit(solution)/shard_map/all_to_all | solution.py:551
  85.3 0.0 copy-done.5
  85.3 0.0 copy-done.6
  85.3 8.5 %filter.1 = (bf16[32,240]{1,0:T(8,128)(2,1)S(1)}, bf16[4,32,72]{2,1,0:T(8,128)(2,1)S(1)}, f32[32,32]{1,0:T(8,128)S(1)}, s32[4]{0:T(128)S(1)}, f32[80,32]{1,0:T(8...) custom-call(s32[1]{0:T(128)} %bitcast.1.domain, ...), custom_call_target="tpu_custom_call" | custom-call | tf_op jit(solution)/shard_map/filter/pallas_call | solution.py:616
  93.8 14.8 %sums.1 = f32[8,4,128]{2,1,0:T(4,128)S(1)} custom-call(s32[1]{0:T(128)} %bitcast.group, f32[32,32]{1,0:T(8,128)S(1)} %get-tuple-element.26.cross, s32[4]{0:T(128)S(1)} %get-tuple-element.27.flag, f32[80,96,128]{2,1,0:T(8,128)S(1)} %bitcast.16, bf16[4,32,72]{2,1,0:T(8,128)(2,1)S(1)} %get-tuple-element.35.part_ref, ...), custom_call_target="tpu_custom_call" | custom-call | tf_op jit(solution)/shard_map/sums/pallas_call | solution.py:639
  108.6 8.0 %all_to_all.11.refs_0_ = f32[8,4,128]{2,1,0:T(4,128)S(1)} all-to-all(f32[8,4,128]{2,1,0:T(4,128)S(1)} %sums.1), channel_id=1, replica_groups=mesh['member'=4,'domain'=8] {'domain'}, dimensions={0} | all-to-all | bytes 32768 | tf_op jit(solution)/shard_map/all_to_all | solution.py:551
  116.6 1.4 %collective-permute-start.10 = (f32[8,4,128]{2,1,0:T(4,128)S(1)}, f32[8,4,128]{2,1,0:T(4,128)S(1)}, u32[]{:S(2)}, u32[]{:S(2)}) collective-permute-start(f32[8,4,128]{2,1,0:T(4,128)S(1)} %all_to_all.11.refs_0_), channel_id=1, source_target_pairs={{0,24},{8,16},{16,8},{24,0},{1,25},{9,17},{17,9},{25,1},{2,26},{10... | collective-permute-start | bytes 49160 | tf_op jit(solution)/shard_map/ppermute | solution.py:555
  118.1 1.4 %collective-permute-start.9 = (f32[8,4,128]{2,1,0:T(4,128)S(1)}, f32[8,4,128]{2,1,0:T(4,128)S(1)}, u32[]{:S(2)}, u32[]{:S(2)}) collective-permute-start(f32[8,4,128]{2,1,0:T(4,128)S(1)} %all_to_all.11.refs_0_), channel_id=1, source_target_pairs={{0,16},{8,24},{16,0},{24,8},{1,17},{9,25},{17,1},{25,9},{2,18},{10... | collective-permute-start | bytes 49160 | tf_op jit(solution)/shard_map/ppermute | solution.py:555
  119.5 1.8 %collective-permute-done.10.refs_3_ = f32[8,4,128]{2,1,0:T(4,128)S(1)} collective-permute-done((f32[8,4,128]{2,1,0:T(4,128)S(1)}, f32[8,4,128]{2,1,0:T(4,128)S(1)}, u32[]{:S(2)}, u32[]{:S(2)}) %collective-permute-start.10) | collective-permute-done | bytes 16416 | tf_op jit(solution)/shard_map/ppermute | solution.py:555
  121.3 1.4 %collective-permute-start.8 = (f32[8,4,128]{2,1,0:T(4,128)S(1)}, f32[8,4,128]{2,1,0:T(4,128)S(1)}, u32[]{:S(2)}, u32[]{:S(2)}) collective-permute-start(f32[8,4,128]{2,1,0:T(4,128)S(1)} %all_to_all.11.refs_0_), channel_id=1, source_target_pairs={{0,8},{8,0},{16,24},{24,16},{1,9},{9,1},{17,25},{25,17},{2,10},{10... | collective-permute-start | bytes 49160 | tf_op jit(solution)/shard_map/ppermute | solution.py:555
  122.7 0.0 collective-permute-done.9.refs_2_
  122.7 2.3 %collective-permute-done.8.refs_1_ = f32[8,4,128]{2,1,0:T(4,128)S(1)} collective-permute-done((f32[8,4,128]{2,1,0:T(4,128)S(1)}, f32[8,4,128]{2,1,0:T(4,128)S(1)}, u32[]{:S(2)}, u32[]{:S(2)}) %collective-permute-start.8) | collective-permute-done | bytes 16416 | tf_op jit(solution)/shard_map/ppermute | solution.py:555
  125.0 3.4 %weights.1 = (bf16[80,96]{1,0:T(8,128)(2,1)S(1)}, f32[16,128]{1,0:T(8,128)S(1)}) custom-call(s32[4,4,8]{2,1,0:T(4,128)S(1)} %bitcast.19, f32[8,4,128]{2,1,0:T(4,128)S(1)} %all_to_all.11.refs_0_, f32[8,4,128]{2,1,0:T(4,128)S(1)} %collective-permute-done.8.refs_1_, f32[8,4,128]{2,1,0:T(4,128)S(1)} %collective-permute-done.9.refs_2_, ...), custom_call_target="tpu_custom_call" | custom-call | tf_op jit(solution)/shard_map/weights/pallas_call | solution.py:660
  128.4 0.0 collective-permute-done.5.refs_1_
  128.4 0.0 collective-permute-done.6.refs_2_
  128.4 0.0 collective-permute-done.7.refs_3_
  128.4 8.7 %update.1 = f32[80,96,128]{2,1,0:T(8,128)} custom-call(s32[1]{0:T(128)} %bitcast.group, f32[32,32]{1,0:T(8,128)S(1)} %get-tuple-element.26.cross, s32[4]{0:T(128)S(1)} %get-tuple-element.27.flag, f32[4,20,96,128]{3,2,1,0:T(8,128)S(1)} %get-tuple-element.28.refs_0_, f32[20,96,128]{2,1,0:T(8,128)S(1)} %collective-permute-done.5.refs_1_, ...), custom_call_target="tpu_custom_call" | custom-call | tf_op jit(solution)/shard_map/update/pallas_call | solution.py:669
  (2 shorter events, 0.0 us)
Async XLA Ops:
  0.0 11.5 %copy-start.7 = (s32[4]{0:T(128)S(1)}, s32[4]{0:T(128)}, u32[]{:S(2)}) copy-start(s32[4]{0:T(128)} %owner.3) | copy-start | bytes 52
  0.0 11.5 %copy-start.8 = (f32[4]{0:T(128)S(1)}, f32[4]{0:T(128)}, u32[]{:S(2)}) copy-start(f32[4]{0:T(128)} %diff.1) | copy-start | bytes 52
  0.0 2.1 %copy-start = (f32[20,4,3,16,256]{4,3,2,1,0:T(8,128)S(1)}, f32[20,4,3,16,256]{4,3,2,1,0:T(8,128)}, u32[]{:S(2)}) copy-start(f32[20,4,3,16,256]{4,3,2,1,0:T(8,128)} %param.8) | copy-start | bytes 11796484
  2.1 9.4 %copy-start.2 = (f32[2,3,16,256]{3,2,1,0:T(8,128)S(1)}, f32[2,3,16,256]{3,2,1,0:T(8,128)}, u32[]{:S(2)}) copy-start(f32[2,3,16,256]{3,2,1,0:T(8,128)} %vel_ref.1) | copy-start | bytes 294916
  2.1 9.4 %copy-start.3 = (s32[4,8,4]{1,2,0:T(4,128)S(1)}, s32[4,8,4]{1,2,0:T(4,128)}, u32[]{:S(2)}) copy-start(s32[4,8,4]{1,2,0:T(4,128)} %param.12) | copy-start | bytes 1540
  2.1 9.4 %copy-start.4 = (s32[16,256]{1,0:T(8,128)S(1)}, s32[16,256]{1,0:T(8,128)}, u32[]{:S(2)}) copy-start(s32[16,256]{1,0:T(8,128)} %mask_ref.3) | copy-start | bytes 49156
  2.2 83.1 %copy-start.5 = (f32[4,8]{1,0:T(4,128)S(1)}, f32[4,8]{1,0:T(4,128)}, u32[]{:S(2)}) copy-start(f32[4,8]{1,0:T(4,128)} %value.1) | copy-start | bytes 388
  2.2 83.1 %copy-start.6 = (f32[4,8]{1,0:T(4,128)S(1)}, f32[4,8]{1,0:T(4,128)}, u32[]{:S(2)}) copy-start(f32[4,8]{1,0:T(4,128)} %error.1) | copy-start | bytes 388
  5.3 6.2 %collective-permute-start = (f32[16,512]{1,0:T(8,128)S(1)}, f32[16,512]{1,0:T(8,128)S(1)}, u32[]{:S(2)}, u32[]{:S(2)}) collective-permute-start(f32[16,512]{1,0:T(8,128)S(1)} %get-tuple-element.23), channel_id=1, source_target_pairs={{0,1},{1,2},{2,3},{3,4},{4,5},{5,6},{6,7},{7,0},{8,9},{9,10},{10,1... | collective-permute-start | bytes 98312 | tf_op jit(solution)/shard_map/ppermute | solution.py:581
  5.8 5.7 %collective-permute-start.1 = (f32[16,512]{1,0:T(8,128)S(1)}, f32[16,512]{1,0:T(8,128)S(1)}, u32[]{:S(2)}, u32[]{:S(2)}) collective-permute-start(f32[16,512]{1,0:T(8,128)S(1)} %get-tuple-element.24), channel_id=1, source_target_pairs={{1,0},{2,1},{3,2},{4,3},{5,4},{6,5},{7,6},{0,7},{9,8},{10,9},{11,1... | collective-permute-start | bytes 98312 | tf_op jit(solution)/shard_map/ppermute | solution.py:582
  11.5 2.1 %copy-start.1 = (f32[20,4,3,16,256]{4,3,2,1,0:T(8,128)S(1)}, f32[20,4,3,16,256]{4,3,2,1,0:T(8,128)}, u32[]{:S(2)}) copy-start(f32[20,4,3,16,256]{4,3,2,1,0:T(8,128)} %param.8) | copy-start | bytes 11796484
  26.0 102.5 %collective-permute-start.5 = (f32[20,96,128]{2,1,0:T(8,128)S(1)}, f32[20,96,128]{2,1,0:T(8,128)S(1)}, u32[]{:S(2)}, u32[]{:S(2)}) collective-permute-start(f32[20,96,128]{2,1,0:T(8,128)S(1)} %get-tuple-element.29), channel_id=1, source_target_pairs={{0,8},{8,0},{16,24},{24,16},{1,9},{9,1},{17,25},{25,17},{2,10},{10... | collective-permute-start | bytes 2949128 | tf_op jit(solution)/shard_map/ppermute | solution.py:555
  28.0 100.4 %collective-permute-start.6 = (f32[20,96,128]{2,1,0:T(8,128)S(1)}, f32[20,96,128]{2,1,0:T(8,128)S(1)}, u32[]{:S(2)}, u32[]{:S(2)}) collective-permute-start(f32[20,96,128]{2,1,0:T(8,128)S(1)} %get-tuple-element.30), channel_id=1, source_target_pairs={{0,16},{8,24},{16,0},{24,8},{1,17},{9,25},{17,1},{25,9},{2,18},{10... | collective-permute-start | bytes 2949128 | tf_op jit(solution)/shard_map/ppermute | solution.py:555
  29.5 98.9 %collective-permute-start.7 = (f32[20,96,128]{2,1,0:T(8,128)S(1)}, f32[20,96,128]{2,1,0:T(8,128)S(1)}, u32[]{:S(2)}, u32[]{:S(2)}) collective-permute-start(f32[20,96,128]{2,1,0:T(8,128)S(1)} %get-tuple-element.31), channel_id=1, source_target_pairs={{0,24},{8,16},{16,8},{24,0},{1,25},{9,17},{17,9},{25,1},{2,26},{10... | collective-permute-start | bytes 2949128 | tf_op jit(solution)/shard_map/ppermute | solution.py:555
  29.5 43.0 %collective-permute-start.4 = (f32[8,128]{1,0:T(8,128)S(1)}, f32[8,128]{1,0:T(8,128)S(1)}, u32[]{:S(2)}, u32[]{:S(2)}) collective-permute-start(f32[8,128]{1,0:T(8,128)S(1)} %get-tuple-element.25), channel_id=1, source_target_pairs={{0,24},{8,16},{16,8},{24,0},{1,25},{9,17},{17,9},{25,1},{2,26},{10... | collective-permute-start | bytes 12296 | tf_op jit(solution)/shard_map/ppermute | solution.py:555
  32.4 41.5 %collective-permute-start.3 = (f32[8,128]{1,0:T(8,128)S(1)}, f32[8,128]{1,0:T(8,128)S(1)}, u32[]{:S(2)}, u32[]{:S(2)}) collective-permute-start(f32[8,128]{1,0:T(8,128)S(1)} %get-tuple-element.25), channel_id=1, source_target_pairs={{0,16},{8,24},{16,0},{24,8},{1,17},{9,25},{17,1},{25,9},{2,18},{10... | collective-permute-start | bytes 12296 | tf_op jit(solution)/shard_map/ppermute | solution.py:555
  72.5 3.6 %collective-permute-start.2 = (f32[8,128]{1,0:T(8,128)S(1)}, f32[8,128]{1,0:T(8,128)S(1)}, u32[]{:S(2)}, u32[]{:S(2)}) collective-permute-start(f32[8,128]{1,0:T(8,128)S(1)} %get-tuple-element.25), channel_id=1, source_target_pairs={{0,8},{8,0},{16,24},{24,16},{1,9},{9,1},{17,25},{25,17},{2,10},{10... | collective-permute-start | bytes 12296 | tf_op jit(solution)/shard_map/ppermute | solution.py:555
  116.6 4.6 %collective-permute-start.10 = (f32[8,4,128]{2,1,0:T(4,128)S(1)}, f32[8,4,128]{2,1,0:T(4,128)S(1)}, u32[]{:S(2)}, u32[]{:S(2)}) collective-permute-start(f32[8,4,128]{2,1,0:T(4,128)S(1)} %all_to_all.11.refs_0_), channel_id=1, source_target_pairs={{0,24},{8,16},{16,8},{24,0},{1,25},{9,17},{17,9},{25,1},{2,26},{10... | collective-permute-start | bytes 49160 | tf_op jit(solution)/shard_map/ppermute | solution.py:555
  118.1 4.6 %collective-permute-start.9 = (f32[8,4,128]{2,1,0:T(4,128)S(1)}, f32[8,4,128]{2,1,0:T(4,128)S(1)}, u32[]{:S(2)}, u32[]{:S(2)}) collective-permute-start(f32[8,4,128]{2,1,0:T(4,128)S(1)} %all_to_all.11.refs_0_), channel_id=1, source_target_pairs={{0,16},{8,24},{16,0},{24,8},{1,17},{9,25},{17,1},{25,9},{2,18},{10... | collective-permute-start | bytes 49160 | tf_op jit(solution)/shard_map/ppermute | solution.py:555
  121.3 3.7 %collective-permute-start.8 = (f32[8,4,128]{2,1,0:T(4,128)S(1)}, f32[8,4,128]{2,1,0:T(4,128)S(1)}, u32[]{:S(2)}, u32[]{:S(2)}) collective-permute-start(f32[8,4,128]{2,1,0:T(4,128)S(1)} %all_to_all.11.refs_0_), channel_id=1, source_target_pairs={{0,8},{8,0},{16,24},{24,16},{1,9},{9,1},{17,25},{25,17},{2,10},{10... | collective-permute-start | bytes 49160 | tf_op jit(solution)/shard_map/ppermute | solution.py:555

commit v3 on v2

--- a/solution.py
+++ b/solution.py
@@ -84,10 +84,10 @@
         return min(p * self.own, self.members - self.window)
 
 
-def arrivals(z, step, source, held, sems):
+def arrivals(z, step, given, source, sems):
     def copy(at):
         part = pl.ds(at * z.part, z.part)
-        return pltpu.make_async_copy(source.at[part], held.at[part], sems.at[at])
+        return pltpu.make_async_copy(given.at[part], source.at[part], sems.at[at])
 
     @pl.when(step == 0)
     def _():
@@ -97,9 +97,9 @@
     copy(step).wait()
 
 
-def edges_kernel(z, source, first_ref, last_ref, held, sems):
+def edges_kernel(z, given, first_ref, last_ref, source, sems):
     step = pl.program_id(0)
-    arrivals(z, step, source, held, sems)
+    arrivals(z, step, given, source, sems)
     lane = iota((z.rows, LANES), 1)
     first = jnp.zeros((z.rows, LANES), F32)
     last = first
@@ -107,20 +107,20 @@
         for fl in range(z.states):
             hit = lane == m * z.states + fl
             at = step * z.part + m
-            first = jnp.where(hit, held[at, fl, :, 0:1], first)
-            last = jnp.where(hit, held[at, fl, :, z.cols - 1 : z.cols], last)
+            first = jnp.where(hit, source[at, fl, :, 0:1], first)
+            last = jnp.where(hit, source[at, fl, :, z.cols - 1 : z.cols], last)
     first_ref[...] = first
     last_ref[...] = last
 
 
 def forecast_kernel(
-    z, group, domain, index, owner, diff, source, before_ref, after_ref, vel_ref, mask_ref,
-    out_ref, *refs,
+    z, group, domain, index, owner, diff, given, before_ref, after_ref, vel_ref, mask_ref,
+    state, *refs,
 ):
     others = refs[: z.groups_m - 1]
-    obs_ref, held, state, picked, in_sems, sems = refs[z.groups_m - 1 :]
+    obs_ref, picked, source, in_sems = refs[z.groups_m - 1 :]
     step = pl.program_id(0)
-    arrivals(z, step, source, held, in_sems)
+    arrivals(z, step, given, source, in_sems)
     shape = (z.rows, z.cols)
     row, col = iota(shape, 0), iota(shape, 1)
     wet = mask_ref[...].astype(F32)
@@ -140,7 +140,7 @@
         north = jnp.where(row == z.rows - 1, 0.0, wet * (spread - half_v))
         south = jnp.where(row == 0, 0.0, wet * (spread + half_v))
         for m in range(z.part):
-            x = held[step * z.part + m, fl]
+            x = source[step * z.part + m, fl]
             at = m * z.states + fl
             nxt = jnp.where(col == z.cols - 1, after[:, at : at + 1], pltpu.roll(x, z.cols - 1, 1))
             prv = jnp.where(col == 0, before[:, at : at + 1], pltpu.roll(x, 1, 1))
@@ -158,83 +158,43 @@
                         p * z.block_rows : (p + 1) * z.block_rows, c * LANES : (c + 1) * LANES
                     ]
 
-    def copies(at):
-        part = pl.ds(at * z.part, z.part)
-        yield pltpu.make_async_copy(state.at[:, part], out_ref.at[:, part], sems.at[0, at])
-        for x, other in enumerate(others, 1):
-            p = jnp.bitwise_xor(group[0], x)
-            yield pltpu.make_async_copy(state.at[p, part], other.at[part], sems.at[x, at])
-
-    for copy in copies(step):
-        copy.start()
+    part = pl.ds(step * z.part, z.part)
+    for x, other in enumerate(others, 1):
+        other[part] = state[jnp.bitwise_xor(group[0], x), part]
 
     @pl.when(step == z.parts - 1)
     def _():
         picked[...] = jnp.zeros_like(picked)
         lane = iota((z.own, LANES), 1)
-
-        def pick(k, carry):
-            b, i = k // z.batch, lax.rem(k, z.batch)
+        for b in range(z.batches):
 
             @pl.when(lax.rem(owner[b], z.groups_d) == domain[0])
             def _():
-                fl = index[b, 0, i] * z.levels + index[b, 1, i]
-                at = index[b, 3, i]
-                cell = (at // LANES) * z.block_rows + index[b, 2, i]
-                base = (owner[b] // z.groups_d) * z.own * z.lines + fl * z.cells + cell
-                got = flat[pl.ds(base, z.own, stride=z.lines), :]
-                got = jnp.where(lane == lax.rem(at, LANES), got, 0.0)
-                got = jnp.sum(got, axis=1, keepdims=True)
-                picked[0 : z.own, :] = jnp.where(lane == k, got, picked[0 : z.own, :])
-
-            return carry
-
-        lax.fori_loop(0, z.obs, pick, 0)
+                total = picked[0 : z.own, :]
+                first = owner[b] // z.groups_d * z.own * z.lines
+                for i in range(z.batch):
+                    fl = index[b, 0, i] * z.levels + index[b, 1, i]
+                    at = index[b, 3, i]
+                    cell = (at // LANES) * z.block_rows + index[b, 2, i]
+                    got = flat[pl.ds(first + fl * z.cells + cell, z.own, stride=z.lines), :]
+                    at = lax.rem(at, LANES)
+                    got = jnp.where(lane == at, got, 0.0)
+                    turn = lax.rem(b * z.batch + i + LANES - at, LANES)
+                    total = total + pltpu.roll(got, turn, 1)
+                picked[0 : z.own, :] = total
+
         total = picked[0:SUBS, :]
         for v in range(1, z.window // SUBS):
             total = total + pltpu.roll(picked[v * SUBS : (v + 1) * SUBS, :], v * z.obs, 1)
         obs_ref[...] = total
 
-        def drain(at, carry):
-            for copy in copies(at):
-                copy.wait()
-            return carry
-
-        lax.fori_loop(0, z.parts, drain, 0)
-
-
-def filter_kernel(
-    z, domain, index, owner, value, error, got_ref, mask_ref,
-    gain_ref, part_ref, cross_ref, flag, lift_ref, taper_ref, relay_ref, gap_ref, wet_ref,
-):
+
+def tapers_kernel(z, domain, index, owner, mask_ref, taper_ref, wet_ref, mutual_ref, flag):
     n = z.obs
-    eight = z.groups_m * SUBS
-    stacked = []
-    for x in range(z.groups_m):
-        total = got_ref[0, x]
-        for d in range(1, z.groups_d):
-            total = total + got_ref[d, x]
-        stacked.append(total)
-    stacked = jnp.concatenate(stacked, axis=0)
     square = (n, LANES)
-    prior = jnp.zeros(square, F32)
     row, lane = iota(square, 0), iota(square, 1)
-    for v in range(z.window // SUBS):
-        pick = (lane == row + v * n).astype(F32)
-        part = dot_exact(pick, stacked, (1, 1))
-        src = iota((eight, LANES), 0)
-        dst = iota((eight, LANES), 1)
-        slot = v * SUBS + src % SUBS
-        place_of = jnp.where(slot < z.own, (src // SUBS) * z.own + slot, -1)
-        prior = prior + dot_exact(part, (dst == place_of).astype(F32), (1, 0))
-    ones = jnp.full((SUBS, LANES), 1.0 / z.members, F32)
-    mean_row = dot_exact(ones, prior, (1, 1))
-    mean = jnp.sum(prior, axis=1, keepdims=True) * (1.0 / z.members)
-    anomaly = jnp.where(lane < z.members, prior - mean, 0.0)
     rows_s, cols_s = jnp.zeros(square, jnp.int32), jnp.zeros(square, jnp.int32)
     rows_l, cols_l = rows_s, cols_s
-    values = jnp.zeros((SUBS, n), F32)
-    value_lane = iota((SUBS, n), 1)
     shape = (SUBS, LANES)
     sub = iota(shape, 0) % z.cells
     cell_row = sub % z.block_rows
@@ -262,7 +222,6 @@
             cols_s = jnp.where(row == k, at_col, cols_s)
             rows_l = jnp.where(lane == k, at_row, rows_l)
             cols_l = jnp.where(lane == k, at_col, cols_l)
-            values = jnp.where(value_lane == k, value[b, i], values)
             ahead = lax.rem(at_col - first_col + z.width, z.width)
             behind = z.width - ahead
             reach = 2 * LOC_RADIUS
@@ -279,10 +238,44 @@
                 for p in range(z.groups_m):
                     rho = taper(cell_row + (p * z.block_rows - at_row), cell_col - at_col, z.width)
                     taper_ref[p, k] = wets[p] * rho
-
+    mutual_ref[...] = taper(rows_s - rows_l, cols_s - cols_l, z.width)
+
+
+def filter_kernel(
+    z, value, error, got_ref, mutual_ref,
+    gain_ref, part_ref, cross_ref, lift_ref, relay_ref, gap_ref,
+):
+    n = z.obs
+    eight = z.groups_m * SUBS
+    stacked = []
+    for x in range(z.groups_m):
+        total = got_ref[0, x]
+        for d in range(1, z.groups_d):
+            total = total + got_ref[d, x]
+        stacked.append(total)
+    stacked = jnp.concatenate(stacked, axis=0)
+    square = (n, LANES)
+    prior = jnp.zeros(square, F32)
+    row, lane = iota(square, 0), iota(square, 1)
+    for v in range(z.window // SUBS):
+        pick = (lane == row + v * n).astype(F32)
+        part = dot_exact(pick, stacked, (1, 1))
+        src = iota((eight, LANES), 0)
+        dst = iota((eight, LANES), 1)
+        slot = v * SUBS + src % SUBS
+        place_of = jnp.where(slot < z.own, (src // SUBS) * z.own + slot, -1)
+        prior = prior + dot_exact(part, (dst == place_of).astype(F32), (1, 0))
+    ones = jnp.full((SUBS, LANES), 1.0 / z.members, F32)
+    mean_row = dot_exact(ones, prior, (1, 1))
+    mean = jnp.sum(prior, axis=1, keepdims=True) * (1.0 / z.members)
+    anomaly = jnp.where(lane < z.members, prior - mean, 0.0)
+    values = jnp.zeros((SUBS, n), F32)
+    value_lane = iota((SUBS, n), 1)
+    for k in range(n):
+        values = jnp.where(value_lane == k, value[k // z.batch, k % z.batch], values)
     gap_ref[...] = jnp.zeros_like(gap_ref)
     gap_ref[:, 0:n] = values - mean_row
-    mutual = taper(rows_s - rows_l, cols_s - cols_l, z.width)
+    mutual = mutual_ref[...]
     relay = jnp.zeros(square, F32)
     inverse_l = jnp.zeros(square, F32)
     inverse_s = jnp.zeros(square, F32)
@@ -380,15 +373,17 @@
 ):
     n = z.obs
     step = pl.program_id(0)
-    lines = z.groups * SUBS
+    lines = z.lines
     flat = x_ref.reshape(z.members * lines, LANES)
+    first_line = pl.multiple_of(step * (z.groups * SUBS), SUBS)
     total[...] = jnp.zeros_like(total)
     every = range(z.groups)
 
     for p in range(z.groups_m):
         for g in every:
             for s in range(0, SUBS, 2):
-                x = stacked_rows(flat, z.start(p) * lines + g * SUBS + s, z.window, lines)
+                first = first_line + z.start(p) * lines + g * SUBS + s
+                x = stacked_rows(flat, first, z.window, lines)
                 got = dot(part_ref[p], x)
                 at = (g * SUBS + s) * n
                 work[at : at + n, :] = got[:, 0:LANES]
@@ -460,22 +455,16 @@
 def update_kernel(z, group, cross, flag, *refs):
     n = z.obs
     slabs = refs[: z.groups_m]
-    gain_ref, taper_ref, wet_ref, weight_ref, shift_ref, out_ref = refs[z.groups_m : -6]
-    got, made, work, gains, in_sems, out_sems = refs[-6:]
+    gain_ref, taper_ref, wet_ref, weight_ref, shift_ref, out_ref = refs[z.groups_m : -5]
+    got, made, work, gains, out_sems = refs[-5:]
     chunk = z.groups * SUBS
-    flat_x = got.reshape(z.members * z.lines, LANES)
+    flat_x = got.reshape(z.members * chunk, LANES)
     flat_o = made.reshape(z.members * z.lines, LANES)
     size = z.members * chunk
     every = range(z.groups)
 
     def lines(at):
         return pl.ds(pl.multiple_of(at * chunk, SUBS), chunk)
-
-    def loads(at):
-        for x, slab in enumerate(slabs):
-            src = slab.at[group[0]] if x == 0 else slab
-            here = got.at[at, x * z.own : (x + 1) * z.own]
-            yield pltpu.make_async_copy(src.at[:, lines(at)], here, in_sems.at[x, at])
 
     def stores(at):
         for x in range(z.groups_m):
@@ -485,18 +474,16 @@
             yield pltpu.make_async_copy(here, there, out_sems.at[x, at])
 
     count = z.steps // z.groups
-    for at in range(count):
-        for copy in loads(at):
-            copy.start()
     wet = wet_ref[group[0]]
 
     def advance(at, carry):
-        for copy in loads(at):
-            copy.wait()
+        for x, slab in enumerate(slabs):
+            src = slab.at[group[0]] if x == 0 else slab
+            got[x * z.own : (x + 1) * z.own] = src[:, lines(at)]
         base = pl.multiple_of(at * size, SUBS)
         for g in every:
             for s in range(0, SUBS, 2):
-                x = stacked_rows(flat_x, base + g * SUBS + s, z.members, chunk)
+                x = stacked_rows(flat_x, g * SUBS + s, z.members, chunk)
                 new = dot(gain_ref[...], x)
                 line = (g * SUBS + s) * n
                 work[line : line + n, :] = new[:, 0:LANES]
@@ -515,8 +502,10 @@
                 for t in range(2):
                     fl = (at * z.groups + g) * z.per_step + (s + t) // z.cells
                     off = shift_ref[pl.ds(fl, 1), :] * wet[s + t : s + t + 1, :]
-                    rows = pl.ds(base + g * SUBS + s + t, z.members, stride=chunk)
-                    flat_o[rows, :] = flat_x[rows, :] + (total[:, t * LANES : (t + 1) * LANES] - off)
+                    line = g * SUBS + s + t
+                    old = flat_x[pl.ds(line, z.members, stride=chunk), :]
+                    new = old + (total[:, t * LANES : (t + 1) * LANES] - off)
+                    flat_o[pl.ds(base + line, z.members, stride=chunk), :] = new
         for copy in stores(at):
             copy.start()
         return carry
@@ -561,78 +550,83 @@
     domain = lax.axis_index("domain").reshape(1)
     index = jnp.swapaxes(obs_index, 1, 2)
     state = ensemble.reshape(z.own, z.states, z.rows, z.cols)
-    slab = pl.BlockSpec(memory_space=pltpu.HBM)
-    held = [VMEM(state.shape, F32)]
-    arrived = [pltpu.SemaphoreType.DMA((z.parts,))]
+    vmem = pl.BlockSpec(memory_space=VMEM)
+    state = pltpu.with_memory_space_constraint(state, pltpu.HBM)
     side = pl.BlockSpec((z.rows, LANES), lambda i: (0, i))
     halo = z.parts * LANES
+    hbm = pl.BlockSpec(memory_space=pl.ANY)
+    arrived = [VMEM(state.shape, F32), pltpu.SemaphoreType.DMA((z.parts,))]
     first, last = pl.pallas_call(
         functools.partial(edges_kernel, z),
         grid=(z.parts,),
-        in_specs=[slab],
+        in_specs=[hbm],
         out_specs=[side] * 2,
         out_shape=[struct(z.rows, halo)] * 2,
-        scratch_shapes=held + arrived,
+        scratch_shapes=arrived,
         name="edges",
-        compiler_params=grant(8),
+        compiler_params=grant(12),
     )(state)
     up = [(i, (i + 1) % z.groups_d) for i in range(z.groups_d)]
     down = [(j, i) for i, j in up]
     before = lax.ppermute(last, "domain", up)
     after = lax.ppermute(first, "domain", down)
-    hbm = pl.BlockSpec(memory_space=pl.ANY)
+    n = z.obs
+    tapers, wet, mutual, flag = pl.pallas_call(
+        functools.partial(tapers_kernel, z),
+        in_specs=[smem()] * 3 + [vmem],
+        out_specs=[vmem] * 3 + [smem()],
+        out_shape=[
+            struct(z.groups_m, n, SUBS, LANES),
+            struct(z.groups_m, SUBS, LANES),
+            struct(n, LANES),
+            struct(z.batches, dtype=jnp.int32),
+        ],
+        name="tapers",
+        compiler_params=grant(8),
+    )(domain, index, obs_owner, land_mask)
     slots = range(1, z.groups_m)
     stepped, *moved, own_priors = pl.pallas_call(
         functools.partial(forecast_kernel, z),
         grid=(z.parts,),
         in_specs=[smem()] * 5
         + [
-            slab,
+            hbm,
             whole(z.rows, halo),
             whole(z.rows, halo),
             whole(*velocity.shape),
             whole(*land_mask.shape),
         ],
-        out_specs=[hbm] * z.groups_m + [whole(SUBS, LANES)],
+        out_specs=[vmem] * z.groups_m + [whole(SUBS, LANES)],
         out_shape=[struct(z.groups_m, z.own, z.lines, LANES)]
         + [struct(z.own, z.lines, LANES) for _ in slots]
         + [struct(SUBS, LANES)],
-        scratch_shapes=held
-        + [
-            VMEM((z.groups_m, z.own, z.lines, LANES), F32),
+        scratch_shapes=[
             VMEM((z.window, LANES), F32),
-            arrived[0],
-            pltpu.SemaphoreType.DMA((z.groups_m, z.parts)),
-        ],
+        ]
+        + arrived,
         name="forecast",
-        compiler_params=grant(16),
+        compiler_params=grant(20),
     )(group, domain, index, obs_owner, diffusivity, state, before, after, velocity, land_mask)
     priors = [own_priors] + [swap(z, own_priors, x) for x in slots]
     moved = [swap(z, slab, x) for x, slab in zip(slots, moved)]
     priors = jnp.broadcast_to(jnp.stack(priors)[None], (z.groups_d, z.groups_m, SUBS, LANES))
     priors = exchange(priors)
-    n = z.obs
-    vmem = pl.BlockSpec(memory_space=VMEM)
-    gain, part, cross, flag, lift, tapers, relay, gap, wet = pl.pallas_call(
+    gain, part, cross, lift, relay, gap = pl.pallas_call(
         functools.partial(filter_kernel, z),
-        in_specs=[smem()] * 5 + [vmem, vmem],
-        out_specs=[vmem] * 3 + [smem()] + [vmem] * 5,
+        in_specs=[smem()] * 2 + [vmem] * 2,
+        out_specs=[vmem] * 6,
         out_shape=[
             struct(n, 3 * z.members, dtype=BF16),
             struct(z.groups_m, n, 3 * z.window, dtype=BF16),
             struct(n, n),
-            struct(z.batches, dtype=jnp.int32),
             struct(z.members, n),
-            struct(z.groups_m, n, SUBS, LANES),
             struct(n, n),
             struct(SUBS, LANES),
-            struct(z.groups_m, SUBS, LANES),
         ],
         name="filter",
         compiler_params=grant(8),
-    )(domain, index, obs_owner, obs_value, obs_error, priors, land_mask)
+    )(obs_value, obs_error, priors, mutual)
     lines = z.groups * SUBS
-    column = pl.BlockSpec((z.members, lines, LANES), lambda i: (0, i, 0))
     grid = (z.steps // z.groups,)
     work = VMEM((z.groups * SUBS * n, LANES), F32)
     gains = VMEM((z.groups * n, SUBS, LANES), F32)
@@ -643,10 +637,10 @@
             smem(),
             smem(),
             smem(),
-            column,
-            whole(*part.shape),
-            whole(*tapers.shape),
-            whole(*wet.shape),
+            vmem,
+            vmem,
+            vmem,
+            vmem,
         ],
         out_specs=whole(z.groups_d, z.sum_rows + 1, LANES),
         out_shape=struct(z.groups_d, z.sum_rows + 1, LANES),
@@ -668,11 +662,16 @@
     sems = pltpu.SemaphoreType.DMA((z.groups_m, z.steps // z.groups))
     result = pl.pallas_call(
         functools.partial(update_kernel, z),
-        in_specs=[smem()] * 3 + [hbm] * z.groups_m + [vmem] * 5,
+        in_specs=[smem()] * 3 + [vmem] * (z.groups_m + 5),
         out_specs=hbm,
         out_shape=struct(z.members, z.lines, LANES),
-        scratch_shapes=[VMEM((z.steps // z.groups, z.members, lines, LANES), F32)] * 2
-        + [work, gains, sems, sems],
+        scratch_shapes=[
+            VMEM((z.members, lines, LANES), F32),
+            VMEM((z.steps // z.groups, z.members, lines, LANES), F32),
+            work,
+            gains,
+            sems,
+        ],
         name="update",
         compiler_params=grant(20),
     )(group, cross, flag, stepped, *moved, gain, tapers, wet, weight, shift)

time: 138 us -> 136 us (0.986)
  blocking collectives: 17.2 us -> 8.04 us
  waiting for transfers between devices: 47.5 us -> 52.4 us
  starting transfers between devices: 17.2 us -> 21.2 us
    all_to_all x2 -> x1, blocking collectives: 17.2 us -> 8.04 us  [exchange(): return lax.all_to_all(copies, 'domain', 0, 0, tiled=True)]
    all_to_all x0 -> x1, waiting for transfers between devices: none -> 4.71 us  [exchange(): return lax.all_to_all(copies, 'domain', 0, 0, tiled=True)]
    all_to_all x0 -> x1, starting transfers between devices: none -> 3.99 us  [exchange(): return lax.all_to_all(copies, 'domain', 0, 0, tiled=True)]
    pallas_call x1, Pallas kernels: 12.3 us -> 8.38 us  [local(): pl.pallas_call(functools.partial(forecast_kernel, z), grid=(z.parts,), in...]
    pallas_call x1, Pallas kernels: 14.8 us -> 16.4 us  [local(): pl.pallas_call(functools.partial(sums_kernel, z), grid=grid, in_specs=[sm...]
    pallas_call x1 -> x2, Pallas kernels: 8.5 us -> 9.85 us  [the longest x1 7.81 us: local(): pl.pallas_call(functools.partial(filter_kernel, z), in_specs=[smem()] * 2...]
    unnamed x18 -> x20, local copies, waits for them, and re-layouts: 4.27 us -> 4.07 us
  transfers between devices with their start and end apart: 11 -> 12, of which waited for: 6 -> 7; matrix products, arithmetic and copies ran while one was open for 0% -> 0% of each run, Pallas kernels for 19% -> 22%
where the time goes in v3:
time: 136 us
  waiting for transfers between devices  52.4 us (39%)
  Pallas kernels  49.6 us (36%)
  starting transfers between devices  21.2 us (16%)
  blocking collectives  8.04 us (6%)
  local copies, waits for them, and re-layouts  4.73 us (3%)
    ppermute x9, waiting for transfers between devices, swap(): lax.ppermute(array, 'member', [(p, p ^ x) for p in range(z.groups_m)])  46.1 us
    pallas_call x1, Pallas kernels, local(): pl.pallas_call(functools.partial(sums_kernel, z), grid=grid, in_specs=[sm...  16.4 us
    ppermute x9, starting transfers between devices, swap(): lax.ppermute(array, 'member', [(p, p ^ x) for p in range(z.groups_m)])  12.5 us
    pallas_call x1, Pallas kernels, local(): pl.pallas_call(functools.partial(forecast_kernel, z), grid=(z.parts,), in...  8.38 us
    pallas_call x1, Pallas kernels, local(): pl.pallas_call(functools.partial(update_kernel, z), in_specs=[smem()] * 3...  8.36 us
    all_to_all x1, blocking collectives, exchange(): return lax.all_to_all(copies, 'domain', 0, 0, tiled=True)  8.04 us
    pallas_call x1, Pallas kernels, local(): pl.pallas_call(functools.partial(filter_kernel, z), in_specs=[smem()] * 2...  7.81 us
    all_to_all x1, waiting for transfers between devices, exchange(): return lax.all_to_all(copies, 'domain', 0, 0, tiled=True)  4.71 us
  transfers between devices with their start and end apart: 12, of which 7 were waited for; matrix products, arithmetic and copies ran while one was open for 0% of the time, Pallas kernels for 22%

profile of v3, /device:TPU:0, one launch (start us, length us, event | category | flops | bytes accessed | tf_op | source)
XLA Modules:
  0.0 136.1 jit_solution(3422403298196071828)
XLA Ops:
  0.0 0.0 copy-start.8
  0.0 0.0 copy-start.5
  0.0 0.0 copy-start.4
  0.0 0.0 copy-start.9
  0.0 0.0 copy-start.3
  0.0 0.0 copy-start.6
  0.0 0.0 copy-start.7
  0.0 3.2 %edges.1 = (f32[16,512]{1,0:T(8,128)S(1)}, f32[16,512]{1,0:T(8,128)S(1)}) custom-call(f32[20,12,16,256]{3,2,1,0:T(8,128)} %bitcast.19), custom_call_target="tpu_custom_call" | custom-call | tf_op jit(solution)/shard_map/edges/pallas_call | solution.py:559
  3.2 0.5 collective-permute-start
  3.8 4.1 %collective-permute-start.1 = (f32[16,512]{1,0:T(8,128)S(1)}, f32[16,512]{1,0:T(8,128)S(1)}, u32[]{:S(2)}, u32[]{:S(2)}) collective-permute-start(f32[16,512]{1,0:T(8,128)S(1)} %get-tuple-element.25), channel_id=1, source_target_pairs={{1,0},{2,1},{3,2},{4,3},{5,4},{6,5},{7,6},{0,7},{9,8},{10,9},{11,1... | collective-permute-start | bytes 98312 | tf_op jit(solution)/shard_map/ppermute | solution.py:572
  7.9 1.5 %collective-permute-done.before_ref = f32[16,512]{1,0:T(8,128)S(1)} collective-permute-done((f32[16,512]{1,0:T(8,128)S(1)}, f32[16,512]{1,0:T(8,128)S(1)}, u32[]{:S(2)}, u32[]{:S(2)}) %collective-permute-start) | collective-permute-done | bytes 32800 | tf_op jit(solution)/shard_map/ppermute | solution.py:571
  9.4 0.1 collective-permute-done.1.after_ref
  9.5 0.0 copy-done.8
  9.5 0.0 copy-done.5
  9.5 0.0 copy-done.4
  9.5 0.0 copy-done.9
  9.5 0.0 copy-done.3
  9.5 8.4 %forecast.1 = (f32[4,20,96,128]{3,2,1,0:T(8,128)S(1)}, f32[20,96,128]{2,1,0:T(8,128)}, f32[20,96,128]{2,1,0:T(8,128)}, f32[20,96,128]{2,1,0:T(8,128)}, f32[8,128]{1,0:T(8,128)S(1)}) custom-call(s32[1]{0:T(128)} %bitcast.group, s32[1]{0:T(128)} %bitcast.1.domain, s32[4,4,8]{2,1,0:T(4,128)S(1)} %bitcast.15, s32[4]{0:T(128)S(1)} %copy-done.8, f32[4]{0:T(128)S(1)} %copy-done.9, ...), custom_call_target="tpu_custom_call" | custom-call | tf_op jit(solution)/shard_map/forecast/pallas_call | solution.py:588
  17.9 0.0 copy-start
  17.9 1.9 %copy-done = f32[4,20,96,128]{3,2,1,0:T(8,128)} copy-done((f32[4,20,96,128]{3,2,1,0:T(8,128)}, f32[4,20,96,128]{3,2,1,0:T(8,128)S(1)}, u32[]{:S(2)}) %copy-start) | copy-done | bytes 3932184
  19.8 2.0 %collective-permute-start.5 = (f32[20,96,128]{2,1,0:T(8,128)}, f32[20,96,128]{2,1,0:T(8,128)S(1)}, u32[]{:S(2)}, u32[]{:S(2)}) collective-permute-start(f32[20,96,128]{2,1,0:T(8,128)} %get-tuple-element.31), channel_id=1, source_target_pairs={{0,8},{8,0},{16,24},{24,16},{1,9},{9,1},{17,25},{25,17},{2,10},{10... | collective-permute-start | bytes 2949128 | tf_op jit(solution)/shard_map/ppermute | solution.py:544
  21.8 1.5 %collective-permute-start.6 = (f32[20,96,128]{2,1,0:T(8,128)}, f32[20,96,128]{2,1,0:T(8,128)S(1)}, u32[]{:S(2)}, u32[]{:S(2)}) collective-permute-start(f32[20,96,128]{2,1,0:T(8,128)} %get-tuple-element.32), channel_id=1, source_target_pairs={{0,16},{8,24},{16,0},{24,8},{1,17},{9,25},{17,1},{25,9},{2,18},{10... | collective-permute-start | bytes 2949128 | tf_op jit(solution)/shard_map/ppermute | solution.py:544
  23.3 0.0 collective-permute-start.7
  23.3 2.9 %collective-permute-start.4 = (f32[8,128]{1,0:T(8,128)S(1)}, f32[8,128]{1,0:T(8,128)S(1)}, u32[]{:S(2)}, u32[]{:S(2)}) collective-permute-start(f32[8,128]{1,0:T(8,128)S(1)} %get-tuple-element.26), channel_id=1, source_target_pairs={{0,24},{8,16},{16,8},{24,0},{1,25},{9,17},{17,9},{25,1},{2,26},{10... | collective-permute-start | bytes 12296 | tf_op jit(solution)/shard_map/ppermute | solution.py:544
  26.2 0.5 collective-permute-start.3
  26.7 39.8 %collective-permute-done.4 = f32[8,128]{1,0:T(8,128)S(1)} collective-permute-done((f32[8,128]{1,0:T(8,128)S(1)}, f32[8,128]{1,0:T(8,128)S(1)}, u32[]{:S(2)}, u32[]{:S(2)}) %collective-permute-start.4) | collective-permute-done | bytes 4128 | tf_op jit(solution)/shard_map/ppermute | solution.py:544
  66.5 1.4 %collective-permute-start.2 = (f32[8,128]{1,0:T(8,128)S(1)}, f32[8,128]{1,0:T(8,128)S(1)}, u32[]{:S(2)}, u32[]{:S(2)}) collective-permute-start(f32[8,128]{1,0:T(8,128)S(1)} %get-tuple-element.26), channel_id=1, source_target_pairs={{0,8},{8,0},{16,24},{24,16},{1,9},{9,1},{17,25},{25,17},{2,10},{10... | collective-permute-start | bytes 12296 | tf_op jit(solution)/shard_map/ppermute | solution.py:544
  67.9 0.0 collective-permute-done.3
  67.9 2.2 %collective-permute-done.2 = f32[8,128]{1,0:T(8,128)S(1)} collective-permute-done((f32[8,128]{1,0:T(8,128)S(1)}, f32[8,128]{1,0:T(8,128)S(1)}, u32[]{:S(2)}, u32[]{:S(2)}) %collective-permute-start.2) | collective-permute-done | bytes 4128 | tf_op jit(solution)/shard_map/ppermute | solution.py:544
  70.1 0.7 broadcast_in_dim.2
  70.8 4.0 %all-to-all-start = ((f32[8,4,8,128]{3,2,1,0:T(8,128)}), f32[8,4,8,128]{3,2,1,0:T(8,128)}, u32[]{:S(2)}, u32[]{:S(2)}) async-start(f32[8,4,8,128]{3,2,1,0:T(8,128)} %broadcast_in_dim.2), calls=%async_computation | async-start | bytes 262144 | tf_op jit(solution)/shard_map/all_to_all | solution.py:540
  74.8 2.0 %tapers.1 = (f32[4,32,8,128]{3,2,1,0:T(8,128)S(1)}, f32[4,8,128]{2,1,0:T(8,128)S(1)}, f32[32,128]{1,0:T(8,128)S(1)}, s32[4]{0:T(128)S(1)}) custom-call(s32[1]{0:T(128)} %bitcast.1.domain, s32[4,4,8]{2,1,0:T(4,128)S(1)} %bitcast.16, s32[4]{0:T(128)S(1)} %copy-done.8, s32[16,256]{1,0:T(8,128)S(1)} %copy-done.5), custom_call_target="tpu_custom_call" | custom-call | tf_op jit(solution)/shard_map/tapers/pallas_call | solution.py:574
  76.8 4.7 %all-to-all-done.got_ref = f32[8,4,8,128]{3,2,1,0:T(8,128)} async-done(((f32[8,4,8,128]{3,2,1,0:T(8,128)}), f32[8,4,8,128]{3,2,1,0:T(8,128)}, u32[]{:S(2)}, u32[]{:S(2)}) %all-to-all-start) | async-done | bytes 131104 | tf_op jit(solution)/shard_map/all_to_all | solution.py:540
  81.5 0.0 copy-done.6
  81.5 0.0 copy-done.7
  81.5 7.8 %filter.1 = (bf16[32,240]{1,0:T(8,128)(2,1)S(1)}, bf16[4,32,72]{2,1,0:T(8,128)(2,1)S(1)}, f32[32,32]{1,0:T(8,128)S(1)}, f32[80,32]{1,0:T(8,128)S(1)}, f32[32,32]{1,0:T(8,128)S(1)}, /*index=5*/f32[8,128]{1,0:T(8,128)S(1)}) custom-call(f32[4,8]{1,0:T(4,128)S(1)} %copy-done.6, f32[4,8]{1,0:T(4,128)S(1)} %copy-done.7, f32[8,4,8,128]{3,2,1,0:T(8,128)} %all-to-all-done.got_ref, ...), custom_call_target="tpu_custom_call" | custom-call | tf_op jit(solution)/shard_map/filter/pallas_call | solution.py:614
  89.3 0.0 copy-start.1
  89.3 2.1 %copy-done.1 = f32[4,20,96,128]{3,2,1,0:T(8,128)S(1)} copy-done((f32[4,20,96,128]{3,2,1,0:T(8,128)S(1)}, f32[4,20,96,128]{3,2,1,0:T(8,128)}, u32[]{:S(2)}) %copy-start.1) | copy-done | bytes 3932184
  91.5 0.0 copy-start.2
  91.5 16.4 %sums.1 = f32[8,4,128]{2,1,0:T(4,128)S(1)} custom-call(s32[1]{0:T(128)} %bitcast.group, f32[32,32]{1,0:T(8,128)S(1)} %get-tuple-element.28.cross, s32[4]{0:T(128)S(1)} %get-tuple-element.29.flag, f32[80,96,128]{2,1,0:T(8,128)S(1)} %bitcast.14, bf16[4,32,72]{2,1,0:T(8,128)(2,1)S(1)} %get-tuple-element.37.part_ref, ...), custom_call_target="tpu_custom_call" | custom-call | tf_op jit(solution)/shard_map/sums/pallas_call | solution.py:633
  107.8 8.0 %all_to_all.10.refs_0_ = f32[8,4,128]{2,1,0:T(4,128)S(1)} all-to-all(f32[8,4,128]{2,1,0:T(4,128)S(1)} %sums.1), channel_id=1, replica_groups=mesh['member'=4,'domain'=8] {'domain'}, dimensions={0} | all-to-all | bytes 32768 | tf_op jit(solution)/shard_map/all_to_all | solution.py:540
  115.9 1.4 %collective-permute-start.10 = (f32[8,4,128]{2,1,0:T(4,128)S(1)}, f32[8,4,128]{2,1,0:T(4,128)S(1)}, u32[]{:S(2)}, u32[]{:S(2)}) collective-permute-start(f32[8,4,128]{2,1,0:T(4,128)S(1)} %all_to_all.10.refs_0_), channel_id=1, source_target_pairs={{0,24},{8,16},{16,8},{24,0},{1,25},{9,17},{17,9},{25,1},{2,26},{10... | collective-permute-start | bytes 49160 | tf_op jit(solution)/shard_map/ppermute | solution.py:544
  117.3 1.4 %collective-permute-start.9 = (f32[8,4,128]{2,1,0:T(4,128)S(1)}, f32[8,4,128]{2,1,0:T(4,128)S(1)}, u32[]{:S(2)}, u32[]{:S(2)}) collective-permute-start(f32[8,4,128]{2,1,0:T(4,128)S(1)} %all_to_all.10.refs_0_), channel_id=1, source_target_pairs={{0,16},{8,24},{16,0},{24,8},{1,17},{9,25},{17,1},{25,9},{2,18},{10... | collective-permute-start | bytes 49160 | tf_op jit(solution)/shard_map/ppermute | solution.py:544
  118.7 1.8 %collective-permute-done.10.refs_3_ = f32[8,4,128]{2,1,0:T(4,128)S(1)} collective-permute-done((f32[8,4,128]{2,1,0:T(4,128)S(1)}, f32[8,4,128]{2,1,0:T(4,128)S(1)}, u32[]{:S(2)}, u32[]{:S(2)}) %collective-permute-start.10) | collective-permute-done | bytes 16416 | tf_op jit(solution)/shard_map/ppermute | solution.py:544
  120.5 1.4 %collective-permute-start.8 = (f32[8,4,128]{2,1,0:T(4,128)S(1)}, f32[8,4,128]{2,1,0:T(4,128)S(1)}, u32[]{:S(2)}, u32[]{:S(2)}) collective-permute-start(f32[8,4,128]{2,1,0:T(4,128)S(1)} %all_to_all.10.refs_0_), channel_id=1, source_target_pairs={{0,8},{8,0},{16,24},{24,16},{1,9},{9,1},{17,25},{25,17},{2,10},{10... | collective-permute-start | bytes 49160 | tf_op jit(solution)/shard_map/ppermute | solution.py:544
  121.9 0.0 collective-permute-done.9.refs_2_
  121.9 2.3 %collective-permute-done.8.refs_1_ = f32[8,4,128]{2,1,0:T(4,128)S(1)} collective-permute-done((f32[8,4,128]{2,1,0:T(4,128)S(1)}, f32[8,4,128]{2,1,0:T(4,128)S(1)}, u32[]{:S(2)}, u32[]{:S(2)}) %collective-permute-start.8) | collective-permute-done | bytes 16416 | tf_op jit(solution)/shard_map/ppermute | solution.py:544
  124.3 3.4 %weights.1 = (bf16[80,96]{1,0:T(8,128)(2,1)S(1)}, f32[16,128]{1,0:T(8,128)S(1)}) custom-call(s32[4,4,8]{2,1,0:T(4,128)S(1)} %bitcast.17, f32[8,4,128]{2,1,0:T(4,128)S(1)} %all_to_all.10.refs_0_, f32[8,4,128]{2,1,0:T(4,128)S(1)} %collective-permute-done.8.refs_1_, f32[8,4,128]{2,1,0:T(4,128)S(1)} %collective-permute-done.9.refs_2_, ...), custom_call_target="tpu_custom_call" | custom-call | tf_op jit(solution)/shard_map/weights/pallas_call | solution.py:654
  127.7 0.0 collective-permute-done.5.refs_1_
  127.7 0.0 collective-permute-done.6.refs_2_
  127.7 0.0 collective-permute-done.7.refs_3_
  127.7 0.0 copy-done.2
  127.7 8.4 %update.1 = f32[80,96,128]{2,1,0:T(8,128)} custom-call(s32[1]{0:T(128)} %bitcast.group, f32[32,32]{1,0:T(8,128)S(1)} %get-tuple-element.28.cross, s32[4]{0:T(128)S(1)} %get-tuple-element.29.flag, f32[4,20,96,128]{3,2,1,0:T(8,128)S(1)} %copy-done.2, f32[20,96,128]{2,1,0:T(8,128)S(1)} %collective-permute-done.5.refs_1_, ...), custom_call_target="tpu_custom_call" | custom-call | tf_op jit(solution)/shard_map/update/pallas_call | solution.py:663
  (1 shorter events, 0.0 us)
Async XLA Ops:
  0.0 9.5 %copy-start.8 = (s32[4]{0:T(128)S(1)}, s32[4]{0:T(128)}, u32[]{:S(2)}) copy-start(s32[4]{0:T(128)} %owner.3) | copy-start | bytes 52
  0.0 9.5 %copy-start.5 = (s32[16,256]{1,0:T(8,128)S(1)}, s32[16,256]{1,0:T(8,128)}, u32[]{:S(2)}) copy-start(s32[16,256]{1,0:T(8,128)} %mask_ref.3) | copy-start | bytes 49156
  0.0 9.5 %copy-start.4 = (s32[4,8,4]{1,2,0:T(4,128)S(1)}, s32[4,8,4]{1,2,0:T(4,128)}, u32[]{:S(2)}) copy-start(s32[4,8,4]{1,2,0:T(4,128)} %param.12) | copy-start | bytes 1540
  0.0 9.5 %copy-start.9 = (f32[4]{0:T(128)S(1)}, f32[4]{0:T(128)}, u32[]{:S(2)}) copy-start(f32[4]{0:T(128)} %diff.1) | copy-start | bytes 52
  0.0 9.5 %copy-start.3 = (f32[2,3,16,256]{3,2,1,0:T(8,128)S(1)}, f32[2,3,16,256]{3,2,1,0:T(8,128)}, u32[]{:S(2)}) copy-start(f32[2,3,16,256]{3,2,1,0:T(8,128)} %vel_ref.1) | copy-start | bytes 294916
  0.0 81.5 %copy-start.6 = (f32[4,8]{1,0:T(4,128)S(1)}, f32[4,8]{1,0:T(4,128)}, u32[]{:S(2)}) copy-start(f32[4,8]{1,0:T(4,128)} %value.1) | copy-start | bytes 388
  0.0 81.5 %copy-start.7 = (f32[4,8]{1,0:T(4,128)S(1)}, f32[4,8]{1,0:T(4,128)}, u32[]{:S(2)}) copy-start(f32[4,8]{1,0:T(4,128)} %error.1) | copy-start | bytes 388
  3.2 6.2 %collective-permute-start = (f32[16,512]{1,0:T(8,128)S(1)}, f32[16,512]{1,0:T(8,128)S(1)}, u32[]{:S(2)}, u32[]{:S(2)}) collective-permute-start(f32[16,512]{1,0:T(8,128)S(1)} %get-tuple-element.24), channel_id=1, source_target_pairs={{0,1},{1,2},{2,3},{3,4},{4,5},{5,6},{6,7},{7,0},{8,9},{9,10},{10,1... | collective-permute-start | bytes 98312 | tf_op jit(solution)/shard_map/ppermute | solution.py:571
  3.8 5.7 %collective-permute-start.1 = (f32[16,512]{1,0:T(8,128)S(1)}, f32[16,512]{1,0:T(8,128)S(1)}, u32[]{:S(2)}, u32[]{:S(2)}) collective-permute-start(f32[16,512]{1,0:T(8,128)S(1)} %get-tuple-element.25), channel_id=1, source_target_pairs={{1,0},{2,1},{3,2},{4,3},{5,4},{6,5},{7,6},{0,7},{9,8},{10,9},{11,1... | collective-permute-start | bytes 98312 | tf_op jit(solution)/shard_map/ppermute | solution.py:572
  17.9 1.9 %copy-start = (f32[4,20,96,128]{3,2,1,0:T(8,128)}, f32[4,20,96,128]{3,2,1,0:T(8,128)S(1)}, u32[]{:S(2)}) copy-start(f32[4,20,96,128]{3,2,1,0:T(8,128)S(1)} %get-tuple-element.30.refs_0_) | copy-start | bytes 11796484
  19.8 107.9 %collective-permute-start.5 = (f32[20,96,128]{2,1,0:T(8,128)}, f32[20,96,128]{2,1,0:T(8,128)S(1)}, u32[]{:S(2)}, u32[]{:S(2)}) collective-permute-start(f32[20,96,128]{2,1,0:T(8,128)} %get-tuple-element.31), channel_id=1, source_target_pairs={{0,8},{8,0},{16,24},{24,16},{1,9},{9,1},{17,25},{25,17},{2,10},{10... | collective-permute-start | bytes 2949128 | tf_op jit(solution)/shard_map/ppermute | solution.py:544
  21.8 105.9 %collective-permute-start.6 = (f32[20,96,128]{2,1,0:T(8,128)}, f32[20,96,128]{2,1,0:T(8,128)S(1)}, u32[]{:S(2)}, u32[]{:S(2)}) collective-permute-start(f32[20,96,128]{2,1,0:T(8,128)} %get-tuple-element.32), channel_id=1, source_target_pairs={{0,16},{8,24},{16,0},{24,8},{1,17},{9,25},{17,1},{25,9},{2,18},{10... | collective-permute-start | bytes 2949128 | tf_op jit(solution)/shard_map/ppermute | solution.py:544
  23.3 104.4 %collective-permute-start.7 = (f32[20,96,128]{2,1,0:T(8,128)}, f32[20,96,128]{2,1,0:T(8,128)S(1)}, u32[]{:S(2)}, u32[]{:S(2)}) collective-permute-start(f32[20,96,128]{2,1,0:T(8,128)} %get-tuple-element.33), channel_id=1, source_target_pairs={{0,24},{8,16},{16,8},{24,0},{1,25},{9,17},{17,9},{25,1},{2,26},{10... | collective-permute-start | bytes 2949128 | tf_op jit(solution)/shard_map/ppermute | solution.py:544
  23.3 43.2 %collective-permute-start.4 = (f32[8,128]{1,0:T(8,128)S(1)}, f32[8,128]{1,0:T(8,128)S(1)}, u32[]{:S(2)}, u32[]{:S(2)}) collective-permute-start(f32[8,128]{1,0:T(8,128)S(1)} %get-tuple-element.26), channel_id=1, source_target_pairs={{0,24},{8,16},{16,8},{24,0},{1,25},{9,17},{17,9},{25,1},{2,26},{10... | collective-permute-start | bytes 12296 | tf_op jit(solution)/shard_map/ppermute | solution.py:544
  26.2 41.7 %collective-permute-start.3 = (f32[8,128]{1,0:T(8,128)S(1)}, f32[8,128]{1,0:T(8,128)S(1)}, u32[]{:S(2)}, u32[]{:S(2)}) collective-permute-start(f32[8,128]{1,0:T(8,128)S(1)} %get-tuple-element.26), channel_id=1, source_target_pairs={{0,16},{8,24},{16,0},{24,8},{1,17},{9,25},{17,1},{25,9},{2,18},{10... | collective-permute-start | bytes 12296 | tf_op jit(solution)/shard_map/ppermute | solution.py:544
  66.5 3.6 %collective-permute-start.2 = (f32[8,128]{1,0:T(8,128)S(1)}, f32[8,128]{1,0:T(8,128)S(1)}, u32[]{:S(2)}, u32[]{:S(2)}) collective-permute-start(f32[8,128]{1,0:T(8,128)S(1)} %get-tuple-element.26), channel_id=1, source_target_pairs={{0,8},{8,0},{16,24},{24,16},{1,9},{9,1},{17,25},{25,17},{2,10},{10... | collective-permute-start | bytes 12296 | tf_op jit(solution)/shard_map/ppermute | solution.py:544
  70.8 10.8 %all-to-all-start = ((f32[8,4,8,128]{3,2,1,0:T(8,128)}), f32[8,4,8,128]{3,2,1,0:T(8,128)}, u32[]{:S(2)}, u32[]{:S(2)}) async-start(f32[8,4,8,128]{3,2,1,0:T(8,128)} %broadcast_in_dim.2), calls=%async_computation | async-start | bytes 262144 | tf_op jit(solution)/shard_map/all_to_all | solution.py:540
  89.3 2.1 %copy-start.1 = (f32[4,20,96,128]{3,2,1,0:T(8,128)S(1)}, f32[4,20,96,128]{3,2,1,0:T(8,128)}, u32[]{:S(2)}) copy-start(f32[4,20,96,128]{3,2,1,0:T(8,128)} %copy-done) | copy-start | bytes 11796484
  91.5 36.2 %copy-start.2 = (f32[4,20,96,128]{3,2,1,0:T(8,128)S(1)}, f32[4,20,96,128]{3,2,1,0:T(8,128)}, u32[]{:S(2)}) copy-start(f32[4,20,96,128]{3,2,1,0:T(8,128)} %copy-done) | copy-start | bytes 11796484
  115.9 4.6 %collective-permute-start.10 = (f32[8,4,128]{2,1,0:T(4,128)S(1)}, f32[8,4,128]{2,1,0:T(4,128)S(1)}, u32[]{:S(2)}, u32[]{:S(2)}) collective-permute-start(f32[8,4,128]{2,1,0:T(4,128)S(1)} %all_to_all.10.refs_0_), channel_id=1, source_target_pairs={{0,24},{8,16},{16,8},{24,0},{1,25},{9,17},{17,9},{25,1},{2,26},{10... | collective-permute-start | bytes 49160 | tf_op jit(solution)/shard_map/ppermute | solution.py:544
  117.3 4.6 %collective-permute-start.9 = (f32[8,4,128]{2,1,0:T(4,128)S(1)}, f32[8,4,128]{2,1,0:T(4,128)S(1)}, u32[]{:S(2)}, u32[]{:S(2)}) collective-permute-start(f32[8,4,128]{2,1,0:T(4,128)S(1)} %all_to_all.10.refs_0_), channel_id=1, source_target_pairs={{0,16},{8,24},{16,0},{24,8},{1,17},{9,25},{17,1},{25,9},{2,18},{10... | collective-permute-start | bytes 49160 | tf_op jit(solution)/shard_map/ppermute | solution.py:544
  120.5 3.7 %collective-permute-start.8 = (f32[8,4,128]{2,1,0:T(4,128)S(1)}, f32[8,4,128]{2,1,0:T(4,128)S(1)}, u32[]{:S(2)}, u32[]{:S(2)}) collective-permute-start(f32[8,4,128]{2,1,0:T(4,128)S(1)} %all_to_all.10.refs_0_), channel_id=1, source_target_pairs={{0,8},{8,0},{16,24},{24,16},{1,9},{9,1},{17,25},{25,17},{2,10},{10... | collective-permute-start | bytes 49160 | tf_op jit(solution)/shard_map/ppermute | solution.py:544

commit v4 on v3

--- a/solution.py
+++ b/solution.py
@@ -265,16 +265,12 @@
         slot = v * SUBS + src % SUBS
         place_of = jnp.where(slot < z.own, (src // SUBS) * z.own + slot, -1)
         prior = prior + dot_exact(part, (dst == place_of).astype(F32), (1, 0))
-    ones = jnp.full((SUBS, LANES), 1.0 / z.members, F32)
-    mean_row = dot_exact(ones, prior, (1, 1))
     mean = jnp.sum(prior, axis=1, keepdims=True) * (1.0 / z.members)
     anomaly = jnp.where(lane < z.members, prior - mean, 0.0)
-    values = jnp.zeros((SUBS, n), F32)
-    value_lane = iota((SUBS, n), 1)
+    values = jnp.zeros(square, F32)
     for k in range(n):
-        values = jnp.where(value_lane == k, value[k // z.batch, k % z.batch], values)
-    gap_ref[...] = jnp.zeros_like(gap_ref)
-    gap_ref[:, 0:n] = values - mean_row
+        values = jnp.where(row == k, value[k // z.batch, k % z.batch], values)
+    gap_ref[...] = values - mean
     mutual = mutual_ref[...]
     relay = jnp.zeros(square, F32)
     inverse_l = jnp.zeros(square, F32)
@@ -316,8 +312,7 @@
         part_ref[p] = made[offset]
     eye = (iota((z.members, LANES), 0) == iota((z.members, LANES), 1)).astype(F32)
     lift_ref[...] = dot_exact(eye, shrink_s * anomaly, (1, 1))
-    eye = (iota((n, LANES), 0) == iota((n, LANES), 1)).astype(F32)
-    relay_ref[...] = dot_exact(eye, relay, (1, 1))
+    relay_ref[...] = relay
 
 
 def stacked_rows(flat, first, count, lines):
@@ -428,20 +423,20 @@
         lines.append(sums[i : i + 1, c * n : (c + 1) * n])
     pad = -z.states % SUBS
     table = jnp.concatenate(lines + [jnp.zeros((pad, n), F32)], axis=0) / count
-    eye = (iota((n, n), 0) == iota((n, n), 1)).astype(F32)
-    turned = dot_exact(eye, table, (1, 1))
-    shape = (z.states + pad, n)
-    fl_row, lane = iota(shape, 0), iota(shape, 1)
+    shape = (n, z.states + pad)
+    row, fl_lane = iota(shape, 0), iota(shape, 1)
     at = jnp.zeros(shape, jnp.int32)
     for k in range(n):
         b, i = divmod(k, z.batch)
-        at = jnp.where(lane == k, index[b, 0, i] * z.levels + index[b, 1, i], at)
-    chosen = dot_exact(turned, (fl_row == at).astype(F32), (1, 0))
-    later = iota((n, n), 1) // z.batch > iota((n, n), 0) // z.batch
-    relay = relay_ref[...] - jnp.where(later, chosen, 0.0)
-    gap = gap_ref[0:1, 0:n]
+        at = jnp.where(row == k, index[b, 0, i] * z.levels + index[b, 1, i], at)
+    chosen = dot_exact((fl_lane == at).astype(F32), table, (1, 0))
+    later = iota((n, n), 0) // z.batch > iota((n, n), 1) // z.batch
+    relay = relay_ref[:, 0:n] - jnp.where(later, chosen, 0.0)
+    gap = gap_ref[...]
     for k in range(n):
-        gap = gap - gap[:, k : k + 1] * relay[k : k + 1, :]
+        gap = gap - relay[:, k : k + 1] * gap[k : k + 1, :]
+    diagonal = iota((n, n), 0) == iota((n, n), 1)
+    gap = jnp.sum(jnp.where(diagonal, gap[:, 0:n], 0.0), axis=0, keepdims=True)
     shift = jnp.sum(table * gap, axis=1, keepdims=True)
     shift_ref[...] = jnp.broadcast_to(shift, shift_ref.shape)
     high, low = split(gap - lift_ref[...])
@@ -620,8 +615,8 @@
             struct(z.groups_m, n, 3 * z.window, dtype=BF16),
             struct(n, n),
             struct(z.members, n),
-            struct(n, n),
-            struct(SUBS, LANES),
+            struct(n, LANES),
+            struct(n, LANES),
         ],
         name="filter",
         compiler_params=grant(8),

time: 136 us -> 134 us (0.985)
  Pallas kernels: 49.6 us -> 47.4 us
    pallas_call x1, Pallas kernels: 3.41 us -> 1.39 us  [local(): pl.pallas_call(functools.partial(weights_kernel, z), in_specs=[smem()] +...]
  transfers between devices with their start and end apart: 12 -> 12, of which waited for: 7 -> 7; matrix products, arithmetic and copies ran while one was open for 0% -> 0% of each run, Pallas kernels for 22% -> 20%
where the time goes in v4:
time: 134 us
  waiting for transfers between devices  52.4 us (39%)
  Pallas kernels  47.4 us (35%)
  starting transfers between devices  21.2 us (16%)
  blocking collectives  8.04 us (6%)
  local copies, waits for them, and re-layouts  4.71 us (4%)
    ppermute x9, waiting for transfers between devices, swap(): lax.ppermute(array, 'member', [(p, p ^ x) for p in range(z.groups_m)])  46.1 us
    pallas_call x1, Pallas kernels, local(): pl.pallas_call(functools.partial(sums_kernel, z), grid=grid, in_specs=[sm...  16.4 us
    ppermute x9, starting transfers between devices, swap(): lax.ppermute(array, 'member', [(p, p ^ x) for p in range(z.groups_m)])  12.5 us
    pallas_call x1, Pallas kernels, local(): pl.pallas_call(functools.partial(forecast_kernel, z), grid=(z.parts,), in...  8.38 us
    pallas_call x1, Pallas kernels, local(): pl.pallas_call(functools.partial(update_kernel, z), in_specs=[smem()] * 3...  8.36 us
    all_to_all x1, blocking collectives, exchange(): return lax.all_to_all(copies, 'domain', 0, 0, tiled=True)  8.04 us
    pallas_call x1, Pallas kernels, local(): pl.pallas_call(functools.partial(filter_kernel, z), in_specs=[smem()] * 2...  7.65 us
    all_to_all x1, waiting for transfers between devices, exchange(): return lax.all_to_all(copies, 'domain', 0, 0, tiled=True)  4.71 us
  transfers between devices with their start and end apart: 12, of which 7 were waited for; matrix products, arithmetic and copies ran while one was open for 0% of the time, Pallas kernels for 20%

profile of v4, /device:TPU:0, one launch (start us, length us, event | category | flops | bytes accessed | tf_op | source)
XLA Modules:
  0.0 134.1 jit_solution(4923890268188112510)
XLA Ops:
  0.0 0.0 copy-start.8
  0.0 0.0 copy-start.5
  0.0 0.0 copy-start.4
  0.0 0.0 copy-start.9
  0.0 0.0 copy-start.3
  0.0 0.0 copy-start.6
  0.0 0.0 copy-start.7
  0.0 3.2 %edges.1 = (f32[16,512]{1,0:T(8,128)S(1)}, f32[16,512]{1,0:T(8,128)S(1)}) custom-call(f32[20,12,16,256]{3,2,1,0:T(8,128)} %bitcast.19), custom_call_target="tpu_custom_call" | custom-call | tf_op jit(solution)/shard_map/edges/pallas_call | solution.py:554
  3.2 0.5 collective-permute-start
  3.8 4.1 %collective-permute-start.1 = (f32[16,512]{1,0:T(8,128)S(1)}, f32[16,512]{1,0:T(8,128)S(1)}, u32[]{:S(2)}, u32[]{:S(2)}) collective-permute-start(f32[16,512]{1,0:T(8,128)S(1)} %get-tuple-element.25), channel_id=1, source_target_pairs={{1,0},{2,1},{3,2},{4,3},{5,4},{6,5},{7,6},{0,7},{9,8},{10,9},{11,1... | collective-permute-start | bytes 98312 | tf_op jit(solution)/shard_map/ppermute | solution.py:567
  7.9 1.5 %collective-permute-done.before_ref = f32[16,512]{1,0:T(8,128)S(1)} collective-permute-done((f32[16,512]{1,0:T(8,128)S(1)}, f32[16,512]{1,0:T(8,128)S(1)}, u32[]{:S(2)}, u32[]{:S(2)}) %collective-permute-start) | collective-permute-done | bytes 32800 | tf_op jit(solution)/shard_map/ppermute | solution.py:566
  9.4 0.1 collective-permute-done.1.after_ref
  9.5 0.0 copy-done.8
  9.5 0.0 copy-done.5
  9.5 0.0 copy-done.4
  9.5 0.0 copy-done.9
  9.5 0.0 copy-done.3
  9.5 8.4 %forecast.1 = (f32[4,20,96,128]{3,2,1,0:T(8,128)S(1)}, f32[20,96,128]{2,1,0:T(8,128)}, f32[20,96,128]{2,1,0:T(8,128)}, f32[20,96,128]{2,1,0:T(8,128)}, f32[8,128]{1,0:T(8,128)S(1)}) custom-call(s32[1]{0:T(128)} %bitcast.group, s32[1]{0:T(128)} %bitcast.1.domain, s32[4,4,8]{2,1,0:T(4,128)S(1)} %bitcast.15, s32[4]{0:T(128)S(1)} %copy-done.8, f32[4]{0:T(128)S(1)} %copy-done.9, ...), custom_call_target="tpu_custom_call" | custom-call | tf_op jit(solution)/shard_map/forecast/pallas_call | solution.py:583
  17.9 0.0 copy-start
  17.9 1.9 %copy-done = f32[4,20,96,128]{3,2,1,0:T(8,128)} copy-done((f32[4,20,96,128]{3,2,1,0:T(8,128)}, f32[4,20,96,128]{3,2,1,0:T(8,128)S(1)}, u32[]{:S(2)}) %copy-start) | copy-done | bytes 3932184
  19.8 2.0 %collective-permute-start.5 = (f32[20,96,128]{2,1,0:T(8,128)}, f32[20,96,128]{2,1,0:T(8,128)S(1)}, u32[]{:S(2)}, u32[]{:S(2)}) collective-permute-start(f32[20,96,128]{2,1,0:T(8,128)} %get-tuple-element.31), channel_id=1, source_target_pairs={{0,8},{8,0},{16,24},{24,16},{1,9},{9,1},{17,25},{25,17},{2,10},{10... | collective-permute-start | bytes 2949128 | tf_op jit(solution)/shard_map/ppermute | solution.py:539
  21.8 1.5 %collective-permute-start.6 = (f32[20,96,128]{2,1,0:T(8,128)}, f32[20,96,128]{2,1,0:T(8,128)S(1)}, u32[]{:S(2)}, u32[]{:S(2)}) collective-permute-start(f32[20,96,128]{2,1,0:T(8,128)} %get-tuple-element.32), channel_id=1, source_target_pairs={{0,16},{8,24},{16,0},{24,8},{1,17},{9,25},{17,1},{25,9},{2,18},{10... | collective-permute-start | bytes 2949128 | tf_op jit(solution)/shard_map/ppermute | solution.py:539
  23.3 0.0 collective-permute-start.7
  23.3 2.9 %collective-permute-start.4 = (f32[8,128]{1,0:T(8,128)S(1)}, f32[8,128]{1,0:T(8,128)S(1)}, u32[]{:S(2)}, u32[]{:S(2)}) collective-permute-start(f32[8,128]{1,0:T(8,128)S(1)} %get-tuple-element.26), channel_id=1, source_target_pairs={{0,24},{8,16},{16,8},{24,0},{1,25},{9,17},{17,9},{25,1},{2,26},{10... | collective-permute-start | bytes 12296 | tf_op jit(solution)/shard_map/ppermute | solution.py:539
  26.2 0.5 collective-permute-start.3
  26.7 39.8 %collective-permute-done.4 = f32[8,128]{1,0:T(8,128)S(1)} collective-permute-done((f32[8,128]{1,0:T(8,128)S(1)}, f32[8,128]{1,0:T(8,128)S(1)}, u32[]{:S(2)}, u32[]{:S(2)}) %collective-permute-start.4) | collective-permute-done | bytes 4128 | tf_op jit(solution)/shard_map/ppermute | solution.py:539
  66.5 1.4 %collective-permute-start.2 = (f32[8,128]{1,0:T(8,128)S(1)}, f32[8,128]{1,0:T(8,128)S(1)}, u32[]{:S(2)}, u32[]{:S(2)}) collective-permute-start(f32[8,128]{1,0:T(8,128)S(1)} %get-tuple-element.26), channel_id=1, source_target_pairs={{0,8},{8,0},{16,24},{24,16},{1,9},{9,1},{17,25},{25,17},{2,10},{10... | collective-permute-start | bytes 12296 | tf_op jit(solution)/shard_map/ppermute | solution.py:539
  67.9 0.0 collective-permute-done.3
  67.9 2.2 %collective-permute-done.2 = f32[8,128]{1,0:T(8,128)S(1)} collective-permute-done((f32[8,128]{1,0:T(8,128)S(1)}, f32[8,128]{1,0:T(8,128)S(1)}, u32[]{:S(2)}, u32[]{:S(2)}) %collective-permute-start.2) | collective-permute-done | bytes 4128 | tf_op jit(solution)/shard_map/ppermute | solution.py:539
  70.1 0.7 broadcast_in_dim.2
  70.8 4.0 %all-to-all-start = ((f32[8,4,8,128]{3,2,1,0:T(8,128)}), f32[8,4,8,128]{3,2,1,0:T(8,128)}, u32[]{:S(2)}, u32[]{:S(2)}) async-start(f32[8,4,8,128]{3,2,1,0:T(8,128)} %broadcast_in_dim.2), calls=%async_computation | async-start | bytes 262144 | tf_op jit(solution)/shard_map/all_to_all | solution.py:535
  74.8 2.0 %tapers.1 = (f32[4,32,8,128]{3,2,1,0:T(8,128)S(1)}, f32[4,8,128]{2,1,0:T(8,128)S(1)}, f32[32,128]{1,0:T(8,128)S(1)}, s32[4]{0:T(128)S(1)}) custom-call(s32[1]{0:T(128)} %bitcast.1.domain, s32[4,4,8]{2,1,0:T(4,128)S(1)} %bitcast.16, s32[4]{0:T(128)S(1)} %copy-done.8, s32[16,256]{1,0:T(8,128)S(1)} %copy-done.5), custom_call_target="tpu_custom_call" | custom-call | tf_op jit(solution)/shard_map/tapers/pallas_call | solution.py:569
  76.8 4.7 %all-to-all-done.got_ref = f32[8,4,8,128]{3,2,1,0:T(8,128)} async-done(((f32[8,4,8,128]{3,2,1,0:T(8,128)}), f32[8,4,8,128]{3,2,1,0:T(8,128)}, u32[]{:S(2)}, u32[]{:S(2)}) %all-to-all-start) | async-done | bytes 131104 | tf_op jit(solution)/shard_map/all_to_all | solution.py:535
  81.5 0.0 copy-done.6
  81.5 0.0 copy-done.7
  81.5 7.6 %filter.1 = (bf16[32,240]{1,0:T(8,128)(2,1)S(1)}, bf16[4,32,72]{2,1,0:T(8,128)(2,1)S(1)}, f32[32,32]{1,0:T(8,128)S(1)}, f32[80,32]{1,0:T(8,128)S(1)}, f32[32,128]{1,0:T(8,128)S(1)}, /*index=5*/f32[32,128]{1,0:T(8,128)S(1)}) custom-call(f32[4,8]{1,0:T(4,128)S(1)} %copy-done.6, f32[4,8]{1,0:T(4,128)S(1)} %copy-done.7, f32[8,4,8,128]{3,2,1,0:T(8,128)} %all-to-all-done.got_ref, ...), custom_call_target="tpu_custom_call" | custom-call | tf_op jit(solution)/shard_map/filter/pallas_call | solution.py:609
  89.2 0.0 copy-start.1
  89.2 2.1 %copy-done.1 = f32[4,20,96,128]{3,2,1,0:T(8,128)S(1)} copy-done((f32[4,20,96,128]{3,2,1,0:T(8,128)S(1)}, f32[4,20,96,128]{3,2,1,0:T(8,128)}, u32[]{:S(2)}) %copy-start.1) | copy-done | bytes 3932184
  91.3 0.0 copy-start.2
  91.3 16.4 %sums.1 = f32[8,4,128]{2,1,0:T(4,128)S(1)} custom-call(s32[1]{0:T(128)} %bitcast.group, f32[32,32]{1,0:T(8,128)S(1)} %get-tuple-element.28.cross, s32[4]{0:T(128)S(1)} %get-tuple-element.29.flag, f32[80,96,128]{2,1,0:T(8,128)S(1)} %bitcast.14, bf16[4,32,72]{2,1,0:T(8,128)(2,1)S(1)} %get-tuple-element.37.part_ref, ...), custom_call_target="tpu_custom_call" | custom-call | tf_op jit(solution)/shard_map/sums/pallas_call | solution.py:628
  107.7 8.0 %all_to_all.10.refs_0_ = f32[8,4,128]{2,1,0:T(4,128)S(1)} all-to-all(f32[8,4,128]{2,1,0:T(4,128)S(1)} %sums.1), channel_id=1, replica_groups=mesh['member'=4,'domain'=8] {'domain'}, dimensions={0} | all-to-all | bytes 32768 | tf_op jit(solution)/shard_map/all_to_all | solution.py:535
  115.7 1.4 %collective-permute-start.10 = (f32[8,4,128]{2,1,0:T(4,128)S(1)}, f32[8,4,128]{2,1,0:T(4,128)S(1)}, u32[]{:S(2)}, u32[]{:S(2)}) collective-permute-start(f32[8,4,128]{2,1,0:T(4,128)S(1)} %all_to_all.10.refs_0_), channel_id=1, source_target_pairs={{0,24},{8,16},{16,8},{24,0},{1,25},{9,17},{17,9},{25,1},{2,26},{10... | collective-permute-start | bytes 49160 | tf_op jit(solution)/shard_map/ppermute | solution.py:539
  117.2 1.4 %collective-permute-start.9 = (f32[8,4,128]{2,1,0:T(4,128)S(1)}, f32[8,4,128]{2,1,0:T(4,128)S(1)}, u32[]{:S(2)}, u32[]{:S(2)}) collective-permute-start(f32[8,4,128]{2,1,0:T(4,128)S(1)} %all_to_all.10.refs_0_), channel_id=1, source_target_pairs={{0,16},{8,24},{16,0},{24,8},{1,17},{9,25},{17,1},{25,9},{2,18},{10... | collective-permute-start | bytes 49160 | tf_op jit(solution)/shard_map/ppermute | solution.py:539
  118.6 1.8 %collective-permute-done.10.refs_3_ = f32[8,4,128]{2,1,0:T(4,128)S(1)} collective-permute-done((f32[8,4,128]{2,1,0:T(4,128)S(1)}, f32[8,4,128]{2,1,0:T(4,128)S(1)}, u32[]{:S(2)}, u32[]{:S(2)}) %collective-permute-start.10) | collective-permute-done | bytes 16416 | tf_op jit(solution)/shard_map/ppermute | solution.py:539
  120.4 1.4 %collective-permute-start.8 = (f32[8,4,128]{2,1,0:T(4,128)S(1)}, f32[8,4,128]{2,1,0:T(4,128)S(1)}, u32[]{:S(2)}, u32[]{:S(2)}) collective-permute-start(f32[8,4,128]{2,1,0:T(4,128)S(1)} %all_to_all.10.refs_0_), channel_id=1, source_target_pairs={{0,8},{8,0},{16,24},{24,16},{1,9},{9,1},{17,25},{25,17},{2,10},{10... | collective-permute-start | bytes 49160 | tf_op jit(solution)/shard_map/ppermute | solution.py:539
  121.8 0.0 collective-permute-done.9.refs_2_
  121.8 2.3 %collective-permute-done.8.refs_1_ = f32[8,4,128]{2,1,0:T(4,128)S(1)} collective-permute-done((f32[8,4,128]{2,1,0:T(4,128)S(1)}, f32[8,4,128]{2,1,0:T(4,128)S(1)}, u32[]{:S(2)}, u32[]{:S(2)}) %collective-permute-start.8) | collective-permute-done | bytes 16416 | tf_op jit(solution)/shard_map/ppermute | solution.py:539
  124.1 1.4 %weights.1 = (bf16[80,96]{1,0:T(8,128)(2,1)S(1)}, f32[16,128]{1,0:T(8,128)S(1)}) custom-call(s32[4,4,8]{2,1,0:T(4,128)S(1)} %bitcast.17, f32[8,4,128]{2,1,0:T(4,128)S(1)} %all_to_all.10.refs_0_, f32[8,4,128]{2,1,0:T(4,128)S(1)} %collective-permute-done.8.refs_1_, f32[8,4,128]{2,1,0:T(4,128)S(1)} %collective-permute-done.9.refs_2_, ...), custom_call_target="tpu_custom_call" | custom-call | tf_op jit(solution)/shard_map/weights/pallas_call | solution.py:649
  125.5 0.0 collective-permute-done.5.refs_1_
  125.5 0.0 collective-permute-done.6.refs_2_
  125.5 0.0 collective-permute-done.7.refs_3_
  125.5 0.0 copy-done.2
  125.5 8.4 %update.1 = f32[80,96,128]{2,1,0:T(8,128)} custom-call(s32[1]{0:T(128)} %bitcast.group, f32[32,32]{1,0:T(8,128)S(1)} %get-tuple-element.28.cross, s32[4]{0:T(128)S(1)} %get-tuple-element.29.flag, f32[4,20,96,128]{3,2,1,0:T(8,128)S(1)} %copy-done.2, f32[20,96,128]{2,1,0:T(8,128)S(1)} %collective-permute-done.5.refs_1_, ...), custom_call_target="tpu_custom_call" | custom-call | tf_op jit(solution)/shard_map/update/pallas_call | solution.py:658
  (1 shorter events, 0.0 us)
Async XLA Ops:
  0.0 9.5 %copy-start.8 = (s32[4]{0:T(128)S(1)}, s32[4]{0:T(128)}, u32[]{:S(2)}) copy-start(s32[4]{0:T(128)} %owner.3) | copy-start | bytes 52
  0.0 9.5 %copy-start.5 = (s32[16,256]{1,0:T(8,128)S(1)}, s32[16,256]{1,0:T(8,128)}, u32[]{:S(2)}) copy-start(s32[16,256]{1,0:T(8,128)} %mask_ref.3) | copy-start | bytes 49156
  0.0 9.5 %copy-start.4 = (s32[4,8,4]{1,2,0:T(4,128)S(1)}, s32[4,8,4]{1,2,0:T(4,128)}, u32[]{:S(2)}) copy-start(s32[4,8,4]{1,2,0:T(4,128)} %param.12) | copy-start | bytes 1540
  0.0 9.5 %copy-start.9 = (f32[4]{0:T(128)S(1)}, f32[4]{0:T(128)}, u32[]{:S(2)}) copy-start(f32[4]{0:T(128)} %diff.1) | copy-start | bytes 52
  0.0 9.5 %copy-start.3 = (f32[2,3,16,256]{3,2,1,0:T(8,128)S(1)}, f32[2,3,16,256]{3,2,1,0:T(8,128)}, u32[]{:S(2)}) copy-start(f32[2,3,16,256]{3,2,1,0:T(8,128)} %vel_ref.1) | copy-start | bytes 294916
  0.0 81.5 %copy-start.6 = (f32[4,8]{1,0:T(4,128)S(1)}, f32[4,8]{1,0:T(4,128)}, u32[]{:S(2)}) copy-start(f32[4,8]{1,0:T(4,128)} %value.1) | copy-start | bytes 388
  0.0 81.5 %copy-start.7 = (f32[4,8]{1,0:T(4,128)S(1)}, f32[4,8]{1,0:T(4,128)}, u32[]{:S(2)}) copy-start(f32[4,8]{1,0:T(4,128)} %error.1) | copy-start | bytes 388
  3.2 6.2 %collective-permute-start = (f32[16,512]{1,0:T(8,128)S(1)}, f32[16,512]{1,0:T(8,128)S(1)}, u32[]{:S(2)}, u32[]{:S(2)}) collective-permute-start(f32[16,512]{1,0:T(8,128)S(1)} %get-tuple-element.24), channel_id=1, source_target_pairs={{0,1},{1,2},{2,3},{3,4},{4,5},{5,6},{6,7},{7,0},{8,9},{9,10},{10,1... | collective-permute-start | bytes 98312 | tf_op jit(solution)/shard_map/ppermute | solution.py:566
  3.8 5.7 %collective-permute-start.1 = (f32[16,512]{1,0:T(8,128)S(1)}, f32[16,512]{1,0:T(8,128)S(1)}, u32[]{:S(2)}, u32[]{:S(2)}) collective-permute-start(f32[16,512]{1,0:T(8,128)S(1)} %get-tuple-element.25), channel_id=1, source_target_pairs={{1,0},{2,1},{3,2},{4,3},{5,4},{6,5},{7,6},{0,7},{9,8},{10,9},{11,1... | collective-permute-start | bytes 98312 | tf_op jit(solution)/shard_map/ppermute | solution.py:567
  17.9 1.9 %copy-start = (f32[4,20,96,128]{3,2,1,0:T(8,128)}, f32[4,20,96,128]{3,2,1,0:T(8,128)S(1)}, u32[]{:S(2)}) copy-start(f32[4,20,96,128]{3,2,1,0:T(8,128)S(1)} %get-tuple-element.30.refs_0_) | copy-start | bytes 11796484
  19.8 105.7 %collective-permute-start.5 = (f32[20,96,128]{2,1,0:T(8,128)}, f32[20,96,128]{2,1,0:T(8,128)S(1)}, u32[]{:S(2)}, u32[]{:S(2)}) collective-permute-start(f32[20,96,128]{2,1,0:T(8,128)} %get-tuple-element.31), channel_id=1, source_target_pairs={{0,8},{8,0},{16,24},{24,16},{1,9},{9,1},{17,25},{25,17},{2,10},{10... | collective-permute-start | bytes 2949128 | tf_op jit(solution)/shard_map/ppermute | solution.py:539
  21.8 103.8 %collective-permute-start.6 = (f32[20,96,128]{2,1,0:T(8,128)}, f32[20,96,128]{2,1,0:T(8,128)S(1)}, u32[]{:S(2)}, u32[]{:S(2)}) collective-permute-start(f32[20,96,128]{2,1,0:T(8,128)} %get-tuple-element.32), channel_id=1, source_target_pairs={{0,16},{8,24},{16,0},{24,8},{1,17},{9,25},{17,1},{25,9},{2,18},{10... | collective-permute-start | bytes 2949128 | tf_op jit(solution)/shard_map/ppermute | solution.py:539
  23.3 102.2 %collective-permute-start.7 = (f32[20,96,128]{2,1,0:T(8,128)}, f32[20,96,128]{2,1,0:T(8,128)S(1)}, u32[]{:S(2)}, u32[]{:S(2)}) collective-permute-start(f32[20,96,128]{2,1,0:T(8,128)} %get-tuple-element.33), channel_id=1, source_target_pairs={{0,24},{8,16},{16,8},{24,0},{1,25},{9,17},{17,9},{25,1},{2,26},{10... | collective-permute-start | bytes 2949128 | tf_op jit(solution)/shard_map/ppermute | solution.py:539
  23.3 43.2 %collective-permute-start.4 = (f32[8,128]{1,0:T(8,128)S(1)}, f32[8,128]{1,0:T(8,128)S(1)}, u32[]{:S(2)}, u32[]{:S(2)}) collective-permute-start(f32[8,128]{1,0:T(8,128)S(1)} %get-tuple-element.26), channel_id=1, source_target_pairs={{0,24},{8,16},{16,8},{24,0},{1,25},{9,17},{17,9},{25,1},{2,26},{10... | collective-permute-start | bytes 12296 | tf_op jit(solution)/shard_map/ppermute | solution.py:539
  26.2 41.7 %collective-permute-start.3 = (f32[8,128]{1,0:T(8,128)S(1)}, f32[8,128]{1,0:T(8,128)S(1)}, u32[]{:S(2)}, u32[]{:S(2)}) collective-permute-start(f32[8,128]{1,0:T(8,128)S(1)} %get-tuple-element.26), channel_id=1, source_target_pairs={{0,16},{8,24},{16,0},{24,8},{1,17},{9,25},{17,1},{25,9},{2,18},{10... | collective-permute-start | bytes 12296 | tf_op jit(solution)/shard_map/ppermute | solution.py:539
  66.5 3.6 %collective-permute-start.2 = (f32[8,128]{1,0:T(8,128)S(1)}, f32[8,128]{1,0:T(8,128)S(1)}, u32[]{:S(2)}, u32[]{:S(2)}) collective-permute-start(f32[8,128]{1,0:T(8,128)S(1)} %get-tuple-element.26), channel_id=1, source_target_pairs={{0,8},{8,0},{16,24},{24,16},{1,9},{9,1},{17,25},{25,17},{2,10},{10... | collective-permute-start | bytes 12296 | tf_op jit(solution)/shard_map/ppermute | solution.py:539
  70.8 10.8 %all-to-all-start = ((f32[8,4,8,128]{3,2,1,0:T(8,128)}), f32[8,4,8,128]{3,2,1,0:T(8,128)}, u32[]{:S(2)}, u32[]{:S(2)}) async-start(f32[8,4,8,128]{3,2,1,0:T(8,128)} %broadcast_in_dim.2), calls=%async_computation | async-start | bytes 262144 | tf_op jit(solution)/shard_map/all_to_all | solution.py:535
  89.2 2.1 %copy-start.1 = (f32[4,20,96,128]{3,2,1,0:T(8,128)S(1)}, f32[4,20,96,128]{3,2,1,0:T(8,128)}, u32[]{:S(2)}) copy-start(f32[4,20,96,128]{3,2,1,0:T(8,128)} %copy-done) | copy-start | bytes 11796484
  91.3 34.2 %copy-start.2 = (f32[4,20,96,128]{3,2,1,0:T(8,128)S(1)}, f32[4,20,96,128]{3,2,1,0:T(8,128)}, u32[]{:S(2)}) copy-start(f32[4,20,96,128]{3,2,1,0:T(8,128)} %copy-done) | copy-start | bytes 11796484
  115.7 4.6 %collective-permute-start.10 = (f32[8,4,128]{2,1,0:T(4,128)S(1)}, f32[8,4,128]{2,1,0:T(4,128)S(1)}, u32[]{:S(2)}, u32[]{:S(2)}) collective-permute-start(f32[8,4,128]{2,1,0:T(4,128)S(1)} %all_to_all.10.refs_0_), channel_id=1, source_target_pairs={{0,24},{8,16},{16,8},{24,0},{1,25},{9,17},{17,9},{25,1},{2,26},{10... | collective-permute-start | bytes 49160 | tf_op jit(solution)/shard_map/ppermute | solution.py:539
  117.2 4.6 %collective-permute-start.9 = (f32[8,4,128]{2,1,0:T(4,128)S(1)}, f32[8,4,128]{2,1,0:T(4,128)S(1)}, u32[]{:S(2)}, u32[]{:S(2)}) collective-permute-start(f32[8,4,128]{2,1,0:T(4,128)S(1)} %all_to_all.10.refs_0_), channel_id=1, source_target_pairs={{0,16},{8,24},{16,0},{24,8},{1,17},{9,25},{17,1},{25,9},{2,18},{10... | collective-permute-start | bytes 49160 | tf_op jit(solution)/shard_map/ppermute | solution.py:539
  120.4 3.7 %collective-permute-start.8 = (f32[8,4,128]{2,1,0:T(4,128)S(1)}, f32[8,4,128]{2,1,0:T(4,128)S(1)}, u32[]{:S(2)}, u32[]{:S(2)}) collective-permute-start(f32[8,4,128]{2,1,0:T(4,128)S(1)} %all_to_all.10.refs_0_), channel_id=1, source_target_pairs={{0,8},{8,0},{16,24},{24,16},{1,9},{9,1},{17,25},{25,17},{2,10},{10... | collective-permute-start | bytes 49160 | tf_op jit(solution)/shard_map/ppermute | solution.py:539

commit v5 on v4

--- a/solution.py
+++ b/solution.py
@@ -67,8 +67,7 @@
         self.block_rows = self.rows // self.groups_m
         self.col_tiles = self.cols // LANES
         self.cells = self.block_rows * self.col_tiles
-        self.per_step = SUBS // self.cells
-        self.steps = self.states // self.per_step
+        self.deep = SUBS // self.block_rows
         self.width = self.cols * self.groups_d
         self.batches, self.batch = obs_index.shape[:2]
         self.obs = self.batches * self.batch
@@ -77,8 +76,18 @@
         self.part = next(m for m in (5, 4, 3, 2, 1) if self.own % m == 0)
         self.parts = self.own // self.part
         self.lines = self.states * self.cells
-        self.groups = next(g for g in (3, 2, 1) if self.steps % g == 0)
+        stacks = self.states // self.deep
+        self.groups = next(g for g in (3, 2, 1) if stacks % g == 0)
+        self.chunks = stacks // self.groups
+        self.chunk_states = self.deep * self.groups
+        self.chunk_lines = self.chunk_states * self.cells
         self.window = -(-self.own // SUBS) * SUBS
+        self.pitch = self.lines + SUBS * (1 - self.lines // SUBS % 2)
+        self.chunk_pitch = self.chunk_lines + SUBS * (1 - self.chunk_lines // SUBS % 2)
+
+    def line(self, g, s, c):
+        q, r = divmod(s, self.block_rows)
+        return (g * self.deep + q) * self.cells + c * self.block_rows + r
 
     def start(self, p):
         return min(p * self.own, self.members - self.window)
@@ -124,8 +133,8 @@
     shape = (z.rows, z.cols)
     row, col = iota(shape, 0), iota(shape, 1)
     wet = mask_ref[...].astype(F32)
-    flat = state.reshape(z.members * z.lines, LANES)
-    member = pl.multiple_of(step * (z.part * z.lines), SUBS)
+    flat = state.reshape(z.members * z.pitch, LANES)
+    member = pl.multiple_of(step * (z.part * z.pitch), SUBS)
     side = pl.ds(pl.multiple_of(step * LANES, LANES), LANES)
     before = before_ref[:, side]
     after = after_ref[:, side]
@@ -153,35 +162,38 @@
             )
             for p in range(z.groups_m):
                 for c in range(z.col_tiles):
-                    line = (p * z.own + m) * z.lines + fl * z.cells + c * z.block_rows
+                    line = (p * z.own + m) * z.pitch + fl * z.cells + c * z.block_rows
                     flat[pl.ds(member + line, z.block_rows), :] = y[
                         p * z.block_rows : (p + 1) * z.block_rows, c * LANES : (c + 1) * LANES
                     ]
 
     part = pl.ds(step * z.part, z.part)
     for x, other in enumerate(others, 1):
-        other[part] = state[jnp.bitwise_xor(group[0], x), part]
+        other[part] = state[jnp.bitwise_xor(group[0], x), part, 0 : z.lines]
 
     @pl.when(step == z.parts - 1)
     def _():
         picked[...] = jnp.zeros_like(picked)
-        lane = iota((z.own, LANES), 1)
+        lane, slot = iota((z.window, LANES), 1), iota((z.window, LANES), 0)
         for b in range(z.batches):
 
             @pl.when(lax.rem(owner[b], z.groups_d) == domain[0])
             def _():
-                total = picked[0 : z.own, :]
-                first = owner[b] // z.groups_d * z.own * z.lines
+                total = jnp.zeros((z.window, LANES), F32)
+                own = owner[b] // z.groups_d * z.own
+                first = jnp.minimum(own, z.members - z.window)
                 for i in range(z.batch):
                     fl = index[b, 0, i] * z.levels + index[b, 1, i]
                     at = index[b, 3, i]
                     cell = (at // LANES) * z.block_rows + index[b, 2, i]
-                    got = flat[pl.ds(first + fl * z.cells + cell, z.own, stride=z.lines), :]
+                    line = first * z.pitch + fl * z.cells + cell
+                    got = flat[pl.ds(line, z.window, stride=z.pitch), :]
                     at = lax.rem(at, LANES)
                     got = jnp.where(lane == at, got, 0.0)
                     turn = lax.rem(b * z.batch + i + LANES - at, LANES)
                     total = total + pltpu.roll(got, turn, 1)
-                picked[0 : z.own, :] = total
+                total = pltpu.roll(total, lax.rem(first + z.window - own, z.window), 0)
+                picked[...] = picked[...] + jnp.where(slot < z.own, total, 0.0)
 
         total = picked[0:SUBS, :]
         for v in range(1, z.window // SUBS):
@@ -196,22 +208,19 @@
     rows_s, cols_s = jnp.zeros(square, jnp.int32), jnp.zeros(square, jnp.int32)
     rows_l, cols_l = rows_s, cols_s
     shape = (SUBS, LANES)
-    sub = iota(shape, 0) % z.cells
-    cell_row = sub % z.block_rows
+    cell_row = iota(shape, 0) % z.block_rows
     first_col = domain[0] * z.cols
-    cell_col = first_col + (sub // z.block_rows) * LANES + iota(shape, 1)
-    wets = []
+    wets = {}
     for p in range(z.groups_m):
-        wet = jnp.zeros(shape, F32)
         for c in range(z.col_tiles):
+            wet = jnp.zeros(shape, F32)
             for r in range(z.block_rows):
                 full_row = p * z.block_rows + r
                 line = mask_ref[full_row : full_row + 1, c * LANES : (c + 1) * LANES]
-                wet = jnp.where(sub == c * z.block_rows + r, line.astype(F32), wet)
-        wet_ref[p] = wet
-        wets.append(wet)
+                wet = jnp.where(cell_row == r, line.astype(F32), wet)
+            wet_ref[p, c] = wet
+            wets[p, c] = wet
     for b in range(z.batches):
-        near = jnp.int32(0)
         tile = lax.rem(owner[b], z.groups_d) * z.cols
         first_row = owner[b] // z.groups_d * z.block_rows
         for i in range(z.batch):
@@ -222,22 +231,27 @@
             cols_s = jnp.where(row == k, at_col, cols_s)
             rows_l = jnp.where(lane == k, at_row, rows_l)
             cols_l = jnp.where(lane == k, at_col, cols_l)
-            ahead = lax.rem(at_col - first_col + z.width, z.width)
-            behind = z.width - ahead
+        for c in range(z.col_tiles):
+            near = jnp.int32(0)
+            start = first_col + c * LANES
             reach = 2 * LOC_RADIUS
-            close = (ahead < z.cols + reach) | (behind < reach)
-            near = jnp.where(close, 1, near)
-        flag[b] = near
-
-        @pl.when(near > 0)
-        def _():
             for i in range(z.batch):
-                k = b * z.batch + i
-                at_row = first_row + index[b, 2, i]
-                at_col = tile + index[b, 3, i]
-                for p in range(z.groups_m):
-                    rho = taper(cell_row + (p * z.block_rows - at_row), cell_col - at_col, z.width)
-                    taper_ref[p, k] = wets[p] * rho
+                ahead = lax.rem(tile + index[b, 3, i] - start + z.width, z.width)
+                close = (ahead < LANES + reach) | (z.width - ahead < reach)
+                near = jnp.where(close, 1, near)
+            flag[b, c] = near
+
+            @pl.when(near > 0)
+            def _():
+                cell_col = start + iota(shape, 1)
+                for i in range(z.batch):
+                    at_row = first_row + index[b, 2, i]
+                    at_col = tile + index[b, 3, i]
+                    for p in range(z.groups_m):
+                        row_gap = cell_row + (p * z.block_rows - at_row)
+                        rho = taper(row_gap, cell_col - at_col, z.width)
+                        taper_ref[p, c, b * z.batch + i] = wets[p, c] * rho
+
     mutual_ref[...] = taper(rows_s - rows_l, cols_s - cols_l, z.width)
 
 
@@ -322,13 +336,13 @@
     return jnp.concatenate([high, x - high, high], axis=0).astype(BF16)
 
 
-def solve_gains(z, flag, cross, taper_of, work, gains):
+def solve_gains(z, active, cross, taper_of, work, gains, total=None):
     n, size = z.obs, z.batch
     every = range(z.groups)
 
     for b in range(z.batches):
 
-        @pl.when(flag[b] > 0)
+        @pl.when(active(b))
         def _():
             part = [
                 [work[pl.ds(g * SUBS * n + b * size + i, SUBS, stride=n), :] for g in every]
@@ -346,21 +360,36 @@
                                 part[i][g] = part[i][g] + factor * held[g]
                     return part
 
-                part = lax.cond(flag[before] > 0, add, lambda part: part, part)
+                part = lax.cond(active(before), add, lambda part: part, part)
             for i in range(size):
                 k = b * size + i
                 rho = taper_of(k)
                 for g in every:
                     kalman = rho * part[i][g]
                     gains[g * n + k] = kalman
+                    if total is not None:
+                        total[g * n + k] = total[g * n + k] + kalman
                     for j in range(i + 1, size):
                         part[j][g] = part[j][g] + cross[k, b * size + j] * kalman
 
-        @pl.when(flag[b] == 0)
-        def _():
-            for i in range(size):
-                for g in every:
-                    gains[g * n + b * size + i] = jnp.zeros((SUBS, LANES), F32)
+        if total is None:
+
+            @pl.when(jnp.logical_not(active(b)))
+            def _():
+                for i in range(size):
+                    for g in every:
+                        gains[g * n + b * size + i] = jnp.zeros((SUBS, LANES), F32)
+
+
+def project(z, flat, first, count, stride, c, left, work):
+    n = z.obs
+    for g in range(z.groups):
+        for s in range(0, SUBS, 2):
+            x = stacked_rows(flat, first + z.line(g, s, c), count, stride)
+            got = dot(left, x)
+            at = (g * SUBS + s) * n
+            work[at : at + n, :] = got[:, 0:LANES]
+            work[at + n : at + 2 * n, :] = got[:, LANES : 2 * LANES]
 
 
 def sums_kernel(
@@ -368,40 +397,39 @@
 ):
     n = z.obs
     step = pl.program_id(0)
-    lines = z.lines
-    flat = x_ref.reshape(z.members * lines, LANES)
-    first_line = pl.multiple_of(step * (z.groups * SUBS), SUBS)
+    chunk, c = step // z.col_tiles, lax.rem(step, z.col_tiles)
+    flat = x_ref.reshape(z.members * z.pitch, LANES)
+    first_line = pl.multiple_of(chunk * z.chunk_lines, SUBS)
     total[...] = jnp.zeros_like(total)
     every = range(z.groups)
 
+    @pl.when(step == 0)
+    def _():
+        held[...] = jnp.zeros_like(held)
+
     for p in range(z.groups_m):
-        for g in every:
-            for s in range(0, SUBS, 2):
-                first = first_line + z.start(p) * lines + g * SUBS + s
-                x = stacked_rows(flat, first, z.window, lines)
-                got = dot(part_ref[p], x)
-                at = (g * SUBS + s) * n
-                work[at : at + n, :] = got[:, 0:LANES]
-                work[at + n : at + 2 * n, :] = got[:, LANES : 2 * LANES]
-        solve_gains(z, flag, cross, lambda k: taper_ref[p, k], work, gains)
-        for g in every:
-            for k in range(n):
-                total[g * n + k] = total[g * n + k] + gains[g * n + k]
+        first = first_line + z.start(p) * z.pitch
+        project(z, flat, first, z.window, z.pitch, c, part_ref[p], work)
+        solve_gains(
+            z, lambda b: flag[b, c] > 0, cross, lambda k: taper_ref[p, c, k], work, gains, total
+        )
     for g in every:
         for k in range(n):
             work[pl.ds(g * SUBS * n + k, SUBS, stride=n), :] = total[g * n + k]
-        for q in range(z.per_step):
-            first = g * SUBS + q * z.cells
+        for q in range(z.deep):
+            first = g * SUBS + q * z.block_rows
             each = work[first * n : (first + 1) * n, :]
-            for s in range(first + 1, first + z.cells):
+            for s in range(first + 1, first + z.block_rows):
                 each = each + work[s * n : (s + 1) * n, :]
-            fl = (step * z.groups + g) * z.per_step + q
-            held[pl.ds(pl.multiple_of(fl * n, n), n), :] = each
-
-    @pl.when(step == z.steps // z.groups - 1)
+            fl = chunk * z.chunk_states + g * z.deep + q
+            rows = pl.ds(pl.multiple_of(fl * n, n), n)
+            held[rows, :] = held[rows, :] + each
+
+    @pl.when(step == z.chunks * z.col_tiles - 1)
     def _():
         ones = jnp.ones((SUBS, LANES), F32)
-        wet = jnp.sum(wet_ref[group[0]][0 : z.cells, :], axis=0, keepdims=True)
+        wet = sum(wet_ref[group[0], c] for c in range(z.col_tiles))
+        wet = jnp.sum(wet[0 : z.block_rows, :], axis=0, keepdims=True)
         rows = [
             dot_exact(ones, held[i * LANES : (i + 1) * LANES, :], (1, 1))[0:1, :]
             for i in range(z.sum_rows)
@@ -452,67 +480,77 @@
     slabs = refs[: z.groups_m]
     gain_ref, taper_ref, wet_ref, weight_ref, shift_ref, out_ref = refs[z.groups_m : -5]
     got, made, work, gains, out_sems = refs[-5:]
-    chunk = z.groups * SUBS
-    flat_x = got.reshape(z.members * chunk, LANES)
-    flat_o = made.reshape(z.members * z.lines, LANES)
-    size = z.members * chunk
-    every = range(z.groups)
+    chunk = z.chunk_lines
+    pitch = z.chunk_pitch
+    flat_x = got.reshape(z.members * pitch, LANES)
+    flat_o = made.reshape(z.chunks * z.members * pitch, LANES)
+    size = z.members * pitch
 
     def lines(at):
         return pl.ds(pl.multiple_of(at * chunk, SUBS), chunk)
 
-    def stores(at):
+    def stores(at, g):
+        count = z.deep * z.cells
+        begin = g * count
+        rows = pl.ds(pl.multiple_of(at * chunk + begin, SUBS), count)
         for x in range(z.groups_m):
             first = jnp.bitwise_xor(group[0], x) * z.own
-            here = made.at[at, x * z.own : (x + 1) * z.own]
-            there = out_ref.at[pl.ds(first, z.own), lines(at)]
-            yield pltpu.make_async_copy(here, there, out_sems.at[x, at])
-
-    count = z.steps // z.groups
-    wet = wet_ref[group[0]]
-
-    def advance(at, carry):
-        for x, slab in enumerate(slabs):
-            src = slab.at[group[0]] if x == 0 else slab
-            got[x * z.own : (x + 1) * z.own] = src[:, lines(at)]
+            here = made.at[at, x * z.own : (x + 1) * z.own, begin : begin + count]
+            there = out_ref.at[pl.ds(first, z.own), rows]
+            yield pltpu.make_async_copy(here, there, out_sems.at[x, at, g])
+
+    def advance(at, c):
+        project(z, flat_x, 0, z.members, pitch, c, gain_ref[...], work)
+        own = group[0]
+        solve_gains(
+            z, lambda b: flag[b, c] > 0, cross, lambda k: taper_ref[own, c, k], work, gains
+        )
+        wet = wet_ref[own, c]
         base = pl.multiple_of(at * size, SUBS)
-        for g in every:
-            for s in range(0, SUBS, 2):
-                x = stacked_rows(flat_x, g * SUBS + s, z.members, chunk)
-                new = dot(gain_ref[...], x)
-                line = (g * SUBS + s) * n
-                work[line : line + n, :] = new[:, 0:LANES]
-                work[line + n : line + 2 * n, :] = new[:, LANES : 2 * LANES]
-        solve_gains(z, flag, cross, lambda k: taper_ref[group[0], k], work, gains)
-        for g in every:
+        for g in range(z.groups):
             for k in range(n):
                 work[pl.ds(g * SUBS * n + k, SUBS, stride=n), :] = gains[g * n + k]
             for s in range(0, SUBS, 2):
-                line = (g * SUBS + s) * n
-                k = [work[line : line + n, :], work[line + n : line + 2 * n, :]]
+                row = (g * SUBS + s) * n
+                k = [work[row : row + n, :], work[row + n : row + 2 * n, :]]
                 k = jnp.concatenate(k, axis=1)
                 high = k.astype(BF16)
                 low = (k - high.astype(F32)).astype(BF16)
                 total = dot(weight_ref[...], jnp.concatenate([high, low, high], axis=0))
                 for t in range(2):
-                    fl = (at * z.groups + g) * z.per_step + (s + t) // z.cells
+                    fl = at * z.chunk_states + g * z.deep + (s + t) // z.block_rows
                     off = shift_ref[pl.ds(fl, 1), :] * wet[s + t : s + t + 1, :]
-                    line = g * SUBS + s + t
-                    old = flat_x[pl.ds(line, z.members, stride=chunk), :]
+                    line = z.line(g, s + t, c)
+                    old = flat_x[pl.ds(line, z.members, stride=pitch), :]
                     new = old + (total[:, t * LANES : (t + 1) * LANES] - off)
-                    flat_o[pl.ds(base + line, z.members, stride=chunk), :] = new
-        for copy in stores(at):
-            copy.start()
+                    flat_o[pl.ds(base + line, z.members, stride=pitch), :] = new
+
+            @pl.when(c == z.col_tiles - 1)
+            def _():
+                for copy in stores(at, g):
+                    copy.start()
+
+    def advance_chunk(at, carry):
+        for x, slab in enumerate(slabs):
+            src = slab.at[group[0]] if x == 0 else slab
+            got[x * z.own : (x + 1) * z.own, 0:chunk] = src[:, lines(at)]
+
+        def tile(c, carry):
+            advance(at, c)
+            return carry
+
+        lax.fori_loop(0, z.col_tiles, tile, 0)
         return carry
 
-    lax.fori_loop(0, count, advance, 0)
+    lax.fori_loop(0, z.chunks, advance_chunk, 0)
 
     def drain(at, carry):
-        for copy in stores(at):
-            copy.wait()
+        for g in range(z.groups):
+            for copy in stores(at, g):
+                copy.wait()
         return carry
 
-    lax.fori_loop(0, count, drain, 0)
+    lax.fori_loop(0, z.chunks, drain, 0)
 
 
 def whole(*shape):
@@ -571,10 +609,10 @@
         in_specs=[smem()] * 3 + [vmem],
         out_specs=[vmem] * 3 + [smem()],
         out_shape=[
-            struct(z.groups_m, n, SUBS, LANES),
-            struct(z.groups_m, SUBS, LANES),
+            struct(z.groups_m, z.col_tiles, n, SUBS, LANES),
+            struct(z.groups_m, z.col_tiles, SUBS, LANES),
             struct(n, LANES),
-            struct(z.batches, dtype=jnp.int32),
+            struct(z.batches, z.col_tiles, dtype=jnp.int32),
         ],
         name="tapers",
         compiler_params=grant(8),
@@ -592,7 +630,7 @@
             whole(*land_mask.shape),
         ],
         out_specs=[vmem] * z.groups_m + [whole(SUBS, LANES)],
-        out_shape=[struct(z.groups_m, z.own, z.lines, LANES)]
+        out_shape=[struct(z.groups_m, z.own, z.pitch, LANES)]
         + [struct(z.own, z.lines, LANES) for _ in slots]
         + [struct(SUBS, LANES)],
         scratch_shapes=[
@@ -621,8 +659,7 @@
         name="filter",
         compiler_params=grant(8),
     )(obs_value, obs_error, priors, mutual)
-    lines = z.groups * SUBS
-    grid = (z.steps // z.groups,)
+    grid = (z.chunks * z.col_tiles,)
     work = VMEM((z.groups * SUBS * n, LANES), F32)
     gains = VMEM((z.groups * n, SUBS, LANES), F32)
     sums = pl.pallas_call(
@@ -642,7 +679,7 @@
         scratch_shapes=[work, gains, gains, VMEM((z.sum_rows * LANES, LANES), F32)],
         name="sums",
         compiler_params=grant(12),
-    )(group, cross, flag, stepped.reshape(z.members, z.lines, LANES), part, tapers, wet)
+    )(group, cross, flag, stepped.reshape(z.members, z.pitch, LANES), part, tapers, wet)
     sums = exchange(sums)
     sums = [sums] + [swap(z, sums, x) for x in slots]
     padded = z.states + -z.states % SUBS
@@ -654,15 +691,15 @@
         name="weights",
         compiler_params=grant(8),
     )(index, *sums, lift, relay, gap)
-    sems = pltpu.SemaphoreType.DMA((z.groups_m, z.steps // z.groups))
+    sems = pltpu.SemaphoreType.DMA((z.groups_m, z.chunks, z.groups))
     result = pl.pallas_call(
         functools.partial(update_kernel, z),
         in_specs=[smem()] * 3 + [vmem] * (z.groups_m + 5),
         out_specs=hbm,
         out_shape=struct(z.members, z.lines, LANES),
         scratch_shapes=[
-            VMEM((z.members, lines, LANES), F32),
-            VMEM((z.steps // z.groups, z.members, lines, LANES), F32),
+            VMEM((z.members, z.chunk_pitch, LANES), F32),
+            VMEM((z.chunks, z.members, z.chunk_pitch, LANES), F32),
             work,
             gains,
             sems,

time: 134 us -> 127 us (0.948)
  Pallas kernels: 47.4 us -> 40.6 us
    pallas_call x1, Pallas kernels: 16.4 us -> 9.99 us  [local(): pl.pallas_call(functools.partial(sums_kernel, z), grid=grid, in_specs=[sm...]
  transfers between devices with their start and end apart: 12 -> 12, of which waited for: 7 -> 7; matrix products, arithmetic and copies ran while one was open for 0% -> 1% of each run, Pallas kernels for 20% -> 17%
where the time goes in v5:
time: 127 us; the launch traced here: 126 us
  waiting for transfers between devices  52.1 us (41%)
  Pallas kernels  40.6 us (32%)
  starting transfers between devices  20.6 us (16%)
  blocking collectives  8.04 us (6%)
  local copies, waits for them, and re-layouts  4.87 us (4%)
    ppermute x9, waiting for transfers between devices, swap(): lax.ppermute(array, 'member', [(p, p ^ x) for p in range(z.groups_m)])  46.2 us
    ppermute x9, starting transfers between devices, swap(): lax.ppermute(array, 'member', [(p, p ^ x) for p in range(z.groups_m)])  12.5 us
    pallas_call x1, Pallas kernels, local(): pl.pallas_call(functools.partial(sums_kernel, z), grid=grid, in_specs=[sm...  9.99 us
    pallas_call x1, Pallas kernels, local(): pl.pallas_call(functools.partial(forecast_kernel, z), grid=(z.parts,), in...  8.37 us
    all_to_all x1, blocking collectives, exchange(): return lax.all_to_all(copies, 'domain', 0, 0, tiled=True)  8.04 us
    pallas_call x1, Pallas kernels, local(): pl.pallas_call(functools.partial(update_kernel, z), in_specs=[smem()] * 3...  7.9 us
    pallas_call x1, Pallas kernels, local(): pl.pallas_call(functools.partial(filter_kernel, z), in_specs=[smem()] * 2...  7.32 us
    all_to_all x1, waiting for transfers between devices, exchange(): return lax.all_to_all(copies, 'domain', 0, 0, tiled=True)  4.26 us
  transfers between devices with their start and end apart: 12, of which 7 were waited for; matrix products, arithmetic and copies ran while one was open for 1% of the time, Pallas kernels for 17%

profile of v5, /device:TPU:0, one launch (start us, length us, event | category | flops | bytes accessed | tf_op | source)
XLA Modules:
  0.0 126.4 jit_solution(10853177830809075606)
XLA Ops:
  0.0 0.0 copy-start.8
  0.0 0.0 copy-start.5
  0.0 0.0 copy-start.4
  0.0 0.0 copy-start.9
  0.0 0.0 copy-start.3
  0.0 0.0 copy-start.6
  0.0 0.0 copy-start.7
  0.0 3.2 %edges.1 = (f32[16,512]{1,0:T(8,128)S(1)}, f32[16,512]{1,0:T(8,128)S(1)}) custom-call(f32[20,12,16,256]{3,2,1,0:T(8,128)} %bitcast.19), custom_call_target="tpu_custom_call" | custom-call | tf_op jit(solution)/shard_map/edges/pallas_call | solution.py:592
  3.2 0.5 collective-permute-start
  3.8 4.1 %collective-permute-start.1 = (f32[16,512]{1,0:T(8,128)S(1)}, f32[16,512]{1,0:T(8,128)S(1)}, u32[]{:S(2)}, u32[]{:S(2)}) collective-permute-start(f32[16,512]{1,0:T(8,128)S(1)} %get-tuple-element.25), channel_id=1, source_target_pairs={{1,0},{2,1},{3,2},{4,3},{5,4},{6,5},{7,6},{0,7},{9,8},{10,9},{11,1... | collective-permute-start | bytes 98312 | tf_op jit(solution)/shard_map/ppermute | solution.py:605
  7.9 1.5 %collective-permute-done.before_ref = f32[16,512]{1,0:T(8,128)S(1)} collective-permute-done((f32[16,512]{1,0:T(8,128)S(1)}, f32[16,512]{1,0:T(8,128)S(1)}, u32[]{:S(2)}, u32[]{:S(2)}) %collective-permute-start) | collective-permute-done | bytes 32800 | tf_op jit(solution)/shard_map/ppermute | solution.py:604
  9.4 0.1 collective-permute-done.1.after_ref
  9.5 0.0 copy-done.8
  9.5 0.0 copy-done.5
  9.5 0.0 copy-done.4
  9.5 0.0 copy-done.9
  9.5 0.0 copy-done.3
  9.5 8.4 %forecast.1 = (f32[4,20,104,128]{3,2,1,0:T(8,128)S(1)}, f32[20,96,128]{2,1,0:T(8,128)}, f32[20,96,128]{2,1,0:T(8,128)}, f32[20,96,128]{2,1,0:T(8,128)}, f32[8,128]{1,0:T(8,128)S(1)}) custom-call(s32[1]{0:T(128)} %bitcast.group, s32[1]{0:T(128)} %bitcast.1.domain, s32[4,4,8]{2,1,0:T(4,128)S(1)} %bitcast.15, s32[4]{0:T(128)S(1)} %copy-done.8, f32[4]{0:T(128)S(1)} %copy-done.9, ...), custom_call_target="tpu_custom_call" | custom-call | tf_op jit(solution)/shard_map/forecast/pallas_call | solution.py:621
  17.9 0.0 copy-start
  17.9 2.0 %copy-done = f32[4,20,104,128]{3,2,1,0:T(8,128)} copy-done((f32[4,20,104,128]{3,2,1,0:T(8,128)}, f32[4,20,104,128]{3,2,1,0:T(8,128)S(1)}, u32[]{:S(2)}) %copy-start) | copy-done | bytes 4259864
  19.8 2.0 %collective-permute-start.5 = (f32[20,96,128]{2,1,0:T(8,128)}, f32[20,96,128]{2,1,0:T(8,128)S(1)}, u32[]{:S(2)}, u32[]{:S(2)}) collective-permute-start(f32[20,96,128]{2,1,0:T(8,128)} %get-tuple-element.31), channel_id=1, source_target_pairs={{0,8},{8,0},{16,24},{24,16},{1,9},{9,1},{17,25},{25,17},{2,10},{10... | collective-permute-start | bytes 2949128 | tf_op jit(solution)/shard_map/ppermute | solution.py:577
  21.8 1.5 %collective-permute-start.6 = (f32[20,96,128]{2,1,0:T(8,128)}, f32[20,96,128]{2,1,0:T(8,128)S(1)}, u32[]{:S(2)}, u32[]{:S(2)}) collective-permute-start(f32[20,96,128]{2,1,0:T(8,128)} %get-tuple-element.32), channel_id=1, source_target_pairs={{0,16},{8,24},{16,0},{24,8},{1,17},{9,25},{17,1},{25,9},{2,18},{10... | collective-permute-start | bytes 2949128 | tf_op jit(solution)/shard_map/ppermute | solution.py:577
  23.3 0.0 collective-permute-start.7
  23.3 2.9 %collective-permute-start.4 = (f32[8,128]{1,0:T(8,128)S(1)}, f32[8,128]{1,0:T(8,128)S(1)}, u32[]{:S(2)}, u32[]{:S(2)}) collective-permute-start(f32[8,128]{1,0:T(8,128)S(1)} %get-tuple-element.26), channel_id=1, source_target_pairs={{0,24},{8,16},{16,8},{24,0},{1,25},{9,17},{17,9},{25,1},{2,26},{10... | collective-permute-start | bytes 12296 | tf_op jit(solution)/shard_map/ppermute | solution.py:577
  26.3 0.5 collective-permute-start.3
  26.8 39.8 %collective-permute-done.4 = f32[8,128]{1,0:T(8,128)S(1)} collective-permute-done((f32[8,128]{1,0:T(8,128)S(1)}, f32[8,128]{1,0:T(8,128)S(1)}, u32[]{:S(2)}, u32[]{:S(2)}) %collective-permute-start.4) | collective-permute-done | bytes 4128 | tf_op jit(solution)/shard_map/ppermute | solution.py:577
  66.6 1.4 %collective-permute-start.2 = (f32[8,128]{1,0:T(8,128)S(1)}, f32[8,128]{1,0:T(8,128)S(1)}, u32[]{:S(2)}, u32[]{:S(2)}) collective-permute-start(f32[8,128]{1,0:T(8,128)S(1)} %get-tuple-element.26), channel_id=1, source_target_pairs={{0,8},{8,0},{16,24},{24,16},{1,9},{9,1},{17,25},{25,17},{2,10},{10... | collective-permute-start | bytes 12296 | tf_op jit(solution)/shard_map/ppermute | solution.py:577
  68.0 0.0 collective-permute-done.3
  68.0 2.2 %collective-permute-done.2 = f32[8,128]{1,0:T(8,128)S(1)} collective-permute-done((f32[8,128]{1,0:T(8,128)S(1)}, f32[8,128]{1,0:T(8,128)S(1)}, u32[]{:S(2)}, u32[]{:S(2)}) %collective-permute-start.2) | collective-permute-done | bytes 4128 | tf_op jit(solution)/shard_map/ppermute | solution.py:577
  70.2 0.7 broadcast_in_dim.2
  70.9 3.4 %all-to-all-start = ((f32[8,4,8,128]{3,2,1,0:T(8,128)}), f32[8,4,8,128]{3,2,1,0:T(8,128)S(1)}, u32[]{:S(2)}, u32[]{:S(2)}) async-start(f32[8,4,8,128]{3,2,1,0:T(8,128)} %broadcast_in_dim.2), calls=%async_computation | async-start | bytes 262144 | tf_op jit(solution)/shard_map/all_to_all | solution.py:573
  74.3 2.4 %tapers.1 = (f32[4,2,32,8,128]{4,3,2,1,0:T(8,128)S(1)}, f32[4,2,8,128]{3,2,1,0:T(8,128)S(1)}, f32[32,128]{1,0:T(8,128)S(1)}, s32[4,2]{1,0:T(4,128)S(1)}) custom-call(s32[1]{0:T(128)} %bitcast.1.domain, s32[4,4,8]{2,1,0:T(4,128)S(1)} %bitcast.16, s32[4]{0:T(128)S(1)} %copy-done.8, s32[16,256]{1,0:T(8,128)S(1)} %copy-done.5), custom_call_target="tpu_custom_call" | custom-call | tf_op jit(solution)/shard_map/tapers/pallas_call | solution.py:607
  76.7 4.3 %all-to-all-done.got_ref = f32[8,4,8,128]{3,2,1,0:T(8,128)S(1)} async-done(((f32[8,4,8,128]{3,2,1,0:T(8,128)}), f32[8,4,8,128]{3,2,1,0:T(8,128)S(1)}, u32[]{:S(2)}, u32[]{:S(2)}) %all-to-all-start) | async-done | bytes 131104 | tf_op jit(solution)/shard_map/all_to_all | solution.py:573
  80.9 0.0 copy-done.6
  80.9 0.0 copy-done.7
  80.9 7.3 %filter.1 = (bf16[32,240]{1,0:T(8,128)(2,1)S(1)}, bf16[4,32,72]{2,1,0:T(8,128)(2,1)S(1)}, f32[32,32]{1,0:T(8,128)S(1)}, f32[80,32]{1,0:T(8,128)S(1)}, f32[32,128]{1,0:T(8,128)S(1)}, /*index=5*/f32[32,128]{1,0:T(8,128)S(1)}) custom-call(f32[4,8]{1,0:T(4,128)S(1)} %copy-done.6, f32[4,8]{1,0:T(4,128)S(1)} %copy-done.7, ...), custom_call_target="tpu_custom_call" | custom-call | tf_op jit(solution)/shard_map/filter/pallas_call | solution.py:647
  88.3 0.0 copy-start.1
  88.3 2.2 %copy-done.1 = f32[4,20,104,128]{3,2,1,0:T(8,128)S(1)} copy-done((f32[4,20,104,128]{3,2,1,0:T(8,128)S(1)}, f32[4,20,104,128]{3,2,1,0:T(8,128)}, u32[]{:S(2)}) %copy-start.1) | copy-done | bytes 4259864
  90.5 0.0 copy-start.2
  90.5 10.0 %sums.1 = f32[8,4,128]{2,1,0:T(4,128)S(1)} custom-call(s32[1]{0:T(128)} %bitcast.group, f32[32,32]{1,0:T(8,128)S(1)} %get-tuple-element.28.cross, s32[4,2]{1,0:T(4,128)S(1)} %get-tuple-element.29.flag, f32[80,104,128]{2,1,0:T(8,128)S(1)} %bitcast.14, bf16[4,32,72]{2,1,0:T(8,128)(2,1)S(1)} %get-tuple-element.37.part_ref, ...), custom_call_target="tpu_custom_call" | custom-call | tf_op jit(solution)/shard_map/sums/pallas_call | solution.py:665
  100.5 8.0 %all_to_all.10.refs_0_ = f32[8,4,128]{2,1,0:T(4,128)S(1)} all-to-all(f32[8,4,128]{2,1,0:T(4,128)S(1)} %sums.1), channel_id=1, replica_groups=mesh['member'=4,'domain'=8] {'domain'}, dimensions={0} | all-to-all | bytes 32768 | tf_op jit(solution)/shard_map/all_to_all | solution.py:573
  108.5 1.4 %collective-permute-start.10 = (f32[8,4,128]{2,1,0:T(4,128)S(1)}, f32[8,4,128]{2,1,0:T(4,128)S(1)}, u32[]{:S(2)}, u32[]{:S(2)}) collective-permute-start(f32[8,4,128]{2,1,0:T(4,128)S(1)} %all_to_all.10.refs_0_), channel_id=1, source_target_pairs={{0,24},{8,16},{16,8},{24,0},{1,25},{9,17},{17,9},{25,1},{2,26},{10... | collective-permute-start | bytes 49160 | tf_op jit(solution)/shard_map/ppermute | solution.py:577
  110.0 1.4 %collective-permute-start.9 = (f32[8,4,128]{2,1,0:T(4,128)S(1)}, f32[8,4,128]{2,1,0:T(4,128)S(1)}, u32[]{:S(2)}, u32[]{:S(2)}) collective-permute-start(f32[8,4,128]{2,1,0:T(4,128)S(1)} %all_to_all.10.refs_0_), channel_id=1, source_target_pairs={{0,16},{8,24},{16,0},{24,8},{1,17},{9,25},{17,1},{25,9},{2,18},{10... | collective-permute-start | bytes 49160 | tf_op jit(solution)/shard_map/ppermute | solution.py:577
  111.4 1.8 %collective-permute-done.10.refs_3_ = f32[8,4,128]{2,1,0:T(4,128)S(1)} collective-permute-done((f32[8,4,128]{2,1,0:T(4,128)S(1)}, f32[8,4,128]{2,1,0:T(4,128)S(1)}, u32[]{:S(2)}, u32[]{:S(2)}) %collective-permute-start.10) | collective-permute-done | bytes 16416 | tf_op jit(solution)/shard_map/ppermute | solution.py:577
  113.2 1.4 %collective-permute-start.8 = (f32[8,4,128]{2,1,0:T(4,128)S(1)}, f32[8,4,128]{2,1,0:T(4,128)S(1)}, u32[]{:S(2)}, u32[]{:S(2)}) collective-permute-start(f32[8,4,128]{2,1,0:T(4,128)S(1)} %all_to_all.10.refs_0_), channel_id=1, source_target_pairs={{0,8},{8,0},{16,24},{24,16},{1,9},{9,1},{17,25},{25,17},{2,10},{10... | collective-permute-start | bytes 49160 | tf_op jit(solution)/shard_map/ppermute | solution.py:577
  114.5 0.0 collective-permute-done.9.refs_2_
  114.5 2.3 %collective-permute-done.8.refs_1_ = f32[8,4,128]{2,1,0:T(4,128)S(1)} collective-permute-done((f32[8,4,128]{2,1,0:T(4,128)S(1)}, f32[8,4,128]{2,1,0:T(4,128)S(1)}, u32[]{:S(2)}, u32[]{:S(2)}) %collective-permute-start.8) | collective-permute-done | bytes 16416 | tf_op jit(solution)/shard_map/ppermute | solution.py:577
  116.9 1.4 %weights.1 = (bf16[80,96]{1,0:T(8,128)(2,1)S(1)}, f32[16,128]{1,0:T(8,128)S(1)}) custom-call(s32[4,4,8]{2,1,0:T(4,128)S(1)} %bitcast.17, f32[8,4,128]{2,1,0:T(4,128)S(1)} %all_to_all.10.refs_0_, f32[8,4,128]{2,1,0:T(4,128)S(1)} %collective-permute-done.8.refs_1_, f32[8,4,128]{2,1,0:T(4,128)S(1)} %collective-permute-done.9.refs_2_, ...), custom_call_target="tpu_custom_call" | custom-call | tf_op jit(solution)/shard_map/weights/pallas_call | solution.py:686
  118.3 0.0 collective-permute-done.5.refs_1_
  118.3 0.0 collective-permute-done.6.refs_2_
  118.3 0.0 collective-permute-done.7.refs_3_
  118.3 0.0 copy-done.2
  118.3 7.9 %update.1 = f32[80,96,128]{2,1,0:T(8,128)} custom-call(s32[1]{0:T(128)} %bitcast.group, f32[32,32]{1,0:T(8,128)S(1)} %get-tuple-element.28.cross, s32[4,2]{1,0:T(4,128)S(1)} %get-tuple-element.29.flag, f32[4,20,104,128]{3,2,1,0:T(8,128)S(1)} %copy-done.2, f32[20,96,128]{2,1,0:T(8,128)S(1)} %collective-permute-done.5.refs_1_, ...), custom_call_target="tpu_custom_call" | custom-call | tf_op jit(solution)/shard_map/update/pallas_call | solution.py:695
  (1 shorter events, 0.0 us)
Async XLA Ops:
  0.0 9.5 %copy-start.8 = (s32[4]{0:T(128)S(1)}, s32[4]{0:T(128)}, u32[]{:S(2)}) copy-start(s32[4]{0:T(128)} %owner.3) | copy-start | bytes 52
  0.0 9.5 %copy-start.5 = (s32[16,256]{1,0:T(8,128)S(1)}, s32[16,256]{1,0:T(8,128)}, u32[]{:S(2)}) copy-start(s32[16,256]{1,0:T(8,128)} %mask_ref.3) | copy-start | bytes 49156
  0.0 9.5 %copy-start.4 = (s32[4,8,4]{1,2,0:T(4,128)S(1)}, s32[4,8,4]{1,2,0:T(4,128)}, u32[]{:S(2)}) copy-start(s32[4,8,4]{1,2,0:T(4,128)} %param.12) | copy-start | bytes 1540
  0.0 9.5 %copy-start.9 = (f32[4]{0:T(128)S(1)}, f32[4]{0:T(128)}, u32[]{:S(2)}) copy-start(f32[4]{0:T(128)} %diff.1) | copy-start | bytes 52
  0.0 9.5 %copy-start.3 = (f32[2,3,16,256]{3,2,1,0:T(8,128)S(1)}, f32[2,3,16,256]{3,2,1,0:T(8,128)}, u32[]{:S(2)}) copy-start(f32[2,3,16,256]{3,2,1,0:T(8,128)} %vel_ref.1) | copy-start | bytes 294916
  0.0 80.9 %copy-start.6 = (f32[4,8]{1,0:T(4,128)S(1)}, f32[4,8]{1,0:T(4,128)}, u32[]{:S(2)}) copy-start(f32[4,8]{1,0:T(4,128)} %value.1) | copy-start | bytes 388
  0.0 80.9 %copy-start.7 = (f32[4,8]{1,0:T(4,128)S(1)}, f32[4,8]{1,0:T(4,128)}, u32[]{:S(2)}) copy-start(f32[4,8]{1,0:T(4,128)} %error.1) | copy-start | bytes 388
  3.2 6.2 %collective-permute-start = (f32[16,512]{1,0:T(8,128)S(1)}, f32[16,512]{1,0:T(8,128)S(1)}, u32[]{:S(2)}, u32[]{:S(2)}) collective-permute-start(f32[16,512]{1,0:T(8,128)S(1)} %get-tuple-element.24), channel_id=1, source_target_pairs={{0,1},{1,2},{2,3},{3,4},{4,5},{5,6},{6,7},{7,0},{8,9},{9,10},{10,1... | collective-permute-start | bytes 98312 | tf_op jit(solution)/shard_map/ppermute | solution.py:604
  3.8 5.7 %collective-permute-start.1 = (f32[16,512]{1,0:T(8,128)S(1)}, f32[16,512]{1,0:T(8,128)S(1)}, u32[]{:S(2)}, u32[]{:S(2)}) collective-permute-start(f32[16,512]{1,0:T(8,128)S(1)} %get-tuple-element.25), channel_id=1, source_target_pairs={{1,0},{2,1},{3,2},{4,3},{5,4},{6,5},{7,6},{0,7},{9,8},{10,9},{11,1... | collective-permute-start | bytes 98312 | tf_op jit(solution)/shard_map/ppermute | solution.py:605
  17.9 2.0 %copy-start = (f32[4,20,104,128]{3,2,1,0:T(8,128)}, f32[4,20,104,128]{3,2,1,0:T(8,128)S(1)}, u32[]{:S(2)}) copy-start(f32[4,20,104,128]{3,2,1,0:T(8,128)S(1)} %get-tuple-element.30.refs_0_) | copy-start | bytes 12779524
  19.8 98.5 %collective-permute-start.5 = (f32[20,96,128]{2,1,0:T(8,128)}, f32[20,96,128]{2,1,0:T(8,128)S(1)}, u32[]{:S(2)}, u32[]{:S(2)}) collective-permute-start(f32[20,96,128]{2,1,0:T(8,128)} %get-tuple-element.31), channel_id=1, source_target_pairs={{0,8},{8,0},{16,24},{24,16},{1,9},{9,1},{17,25},{25,17},{2,10},{10... | collective-permute-start | bytes 2949128 | tf_op jit(solution)/shard_map/ppermute | solution.py:577
  21.8 96.5 %collective-permute-start.6 = (f32[20,96,128]{2,1,0:T(8,128)}, f32[20,96,128]{2,1,0:T(8,128)S(1)}, u32[]{:S(2)}, u32[]{:S(2)}) collective-permute-start(f32[20,96,128]{2,1,0:T(8,128)} %get-tuple-element.32), channel_id=1, source_target_pairs={{0,16},{8,24},{16,0},{24,8},{1,17},{9,25},{17,1},{25,9},{2,18},{10... | collective-permute-start | bytes 2949128 | tf_op jit(solution)/shard_map/ppermute | solution.py:577
  23.3 95.0 %collective-permute-start.7 = (f32[20,96,128]{2,1,0:T(8,128)}, f32[20,96,128]{2,1,0:T(8,128)}, u32[]{:S(2)}, u32[]{:S(2)}) collective-permute-start(f32[20,96,128]{2,1,0:T(8,128)} %get-tuple-element.33), channel_id=1, source_target_pairs={{0,24},{8,16},{16,8},{24,0},{1,25},{9,17},{17,9},{25,1},{2,26},{10... | collective-permute-start | bytes 2949128 | tf_op jit(solution)/shard_map/ppermute | solution.py:577
  23.3 43.3 %collective-permute-start.4 = (f32[8,128]{1,0:T(8,128)S(1)}, f32[8,128]{1,0:T(8,128)S(1)}, u32[]{:S(2)}, u32[]{:S(2)}) collective-permute-start(f32[8,128]{1,0:T(8,128)S(1)} %get-tuple-element.26), channel_id=1, source_target_pairs={{0,24},{8,16},{16,8},{24,0},{1,25},{9,17},{17,9},{25,1},{2,26},{10... | collective-permute-start | bytes 12296 | tf_op jit(solution)/shard_map/ppermute | solution.py:577
  26.3 41.7 %collective-permute-start.3 = (f32[8,128]{1,0:T(8,128)S(1)}, f32[8,128]{1,0:T(8,128)S(1)}, u32[]{:S(2)}, u32[]{:S(2)}) collective-permute-start(f32[8,128]{1,0:T(8,128)S(1)} %get-tuple-element.26), channel_id=1, source_target_pairs={{0,16},{8,24},{16,0},{24,8},{1,17},{9,25},{17,1},{25,9},{2,18},{10... | collective-permute-start | bytes 12296 | tf_op jit(solution)/shard_map/ppermute | solution.py:577
  66.6 3.6 %collective-permute-start.2 = (f32[8,128]{1,0:T(8,128)S(1)}, f32[8,128]{1,0:T(8,128)S(1)}, u32[]{:S(2)}, u32[]{:S(2)}) collective-permute-start(f32[8,128]{1,0:T(8,128)S(1)} %get-tuple-element.26), channel_id=1, source_target_pairs={{0,8},{8,0},{16,24},{24,16},{1,9},{9,1},{17,25},{25,17},{2,10},{10... | collective-permute-start | bytes 12296 | tf_op jit(solution)/shard_map/ppermute | solution.py:577
  70.9 10.1 %all-to-all-start = ((f32[8,4,8,128]{3,2,1,0:T(8,128)}), f32[8,4,8,128]{3,2,1,0:T(8,128)S(1)}, u32[]{:S(2)}, u32[]{:S(2)}) async-start(f32[8,4,8,128]{3,2,1,0:T(8,128)} %broadcast_in_dim.2), calls=%async_computation | async-start | bytes 262144 | tf_op jit(solution)/shard_map/all_to_all | solution.py:573
  88.3 2.2 %copy-start.1 = (f32[4,20,104,128]{3,2,1,0:T(8,128)S(1)}, f32[4,20,104,128]{3,2,1,0:T(8,128)}, u32[]{:S(2)}) copy-start(f32[4,20,104,128]{3,2,1,0:T(8,128)} %copy-done) | copy-start | bytes 12779524
  90.5 27.8 %copy-start.2 = (f32[4,20,104,128]{3,2,1,0:T(8,128)S(1)}, f32[4,20,104,128]{3,2,1,0:T(8,128)}, u32[]{:S(2)}) copy-start(f32[4,20,104,128]{3,2,1,0:T(8,128)} %copy-done) | copy-start | bytes 12779524
  108.5 4.6 %collective-permute-start.10 = (f32[8,4,128]{2,1,0:T(4,128)S(1)}, f32[8,4,128]{2,1,0:T(4,128)S(1)}, u32[]{:S(2)}, u32[]{:S(2)}) collective-permute-start(f32[8,4,128]{2,1,0:T(4,128)S(1)} %all_to_all.10.refs_0_), channel_id=1, source_target_pairs={{0,24},{8,16},{16,8},{24,0},{1,25},{9,17},{17,9},{25,1},{2,26},{10... | collective-permute-start | bytes 49160 | tf_op jit(solution)/shard_map/ppermute | solution.py:577
  110.0 4.6 %collective-permute-start.9 = (f32[8,4,128]{2,1,0:T(4,128)S(1)}, f32[8,4,128]{2,1,0:T(4,128)S(1)}, u32[]{:S(2)}, u32[]{:S(2)}) collective-permute-start(f32[8,4,128]{2,1,0:T(4,128)S(1)} %all_to_all.10.refs_0_), channel_id=1, source_target_pairs={{0,16},{8,24},{16,0},{24,8},{1,17},{9,25},{17,1},{25,9},{2,18},{10... | collective-permute-start | bytes 49160 | tf_op jit(solution)/shard_map/ppermute | solution.py:577
  113.2 3.7 %collective-permute-start.8 = (f32[8,4,128]{2,1,0:T(4,128)S(1)}, f32[8,4,128]{2,1,0:T(4,128)S(1)}, u32[]{:S(2)}, u32[]{:S(2)}) collective-permute-start(f32[8,4,128]{2,1,0:T(4,128)S(1)} %all_to_all.10.refs_0_), channel_id=1, source_target_pairs={{0,8},{8,0},{16,24},{24,16},{1,9},{9,1},{17,25},{25,17},{2,10},{10... | collective-permute-start | bytes 49160 | tf_op jit(solution)/shard_map/ppermute | solution.py:577
